TPU v7x, 512 devices: a whole 4x8x8 slice. The times are simulated.
512 devices in a mesh: gx: 16 (over x, y_lo, core), gy: 32 (over y_hi, z).
Axes of the slice: x: 4, y: 8 (y_hi: 4, y_lo: 2; y = y_hi * 2 + y_lo), z: 8, core: 2. Of those that a mesh axis runs over, the one named last changes fastest.
Arguments:
- state: float32 [8, 16, 384, 2048], P(None, None, 'gy', 'gx'), may hold values from -6 to 6
- register: float32 [8, 16, 384, 2048], P(None, None, 'gy', 'gx'), may hold values from -6 to 6
- checkpoint: bfloat16 [8, 16, 384, 2048], P(None, None, 'gy', 'gx'), may hold values from -6 to 6
- velocity: float32 [3, 16, 384, 2048], P(None, None, 'gy', 'gx'), may hold values from -4 to 4
- diffusivity: float32 [16, 384, 2048], P(None, 'gy', 'gx'), may hold values from 0.02 to 0.3
Outputs:
- new_state: float32 [8, 16, 384, 2048], P(None, None, 'gy', 'gx')
- new_register: float32 [8, 16, 384, 2048], P(None, None, 'gy', 'gx')
- gram: float32 [2048, 2048], P('gx', 'gy')
All inputs are finite; a program needn't handle non-finite values.
Results may differ from a plain program's by a relative error of at most 0.0003.
Values sent between devices are 32-bit elements; how exact they have to be, the bound alone decides.
No kernel may reach another device: no remote copies, remote signals or barrier semaphores. Data moves between devices by JAX's collectives and lax.ppermute only.
A program may use at most 64 MiB of HBM per device.

v0:
```python
import jax
import jax.numpy as jnp
from jax import lax
from jax.sharding import PartitionSpec as P

step_size = 0.3
carry_weight = -5.0 / 9.0
update_weight = 15.0 / 16.0


def with_halo(shard, sides, width):
    edges = {}
    for axis, dim in sides:
        size, length = (lax.axis_size(axis), shard.shape[dim])
        up = [(i, (i + 1) % size) for i in range(size)]
        last = lax.slice_in_dim(shard, length - width, length, axis=dim)
        leading = lax.slice_in_dim(shard, 0, width, axis=dim)
        edges[dim] = (
            lax.ppermute(last, axis, up),
            lax.ppermute(leading, axis, [(b, a) for a, b in up]),
        )
    done = []
    for _, dim in sides:
        low, high = edges[dim]
        around = [(width, width) if d in done else (0, 0) for d in range(shard.ndim)]
        shard = jnp.concatenate([jnp.pad(low, around), shard, jnp.pad(high, around)], axis=dim)
        done.append(dim)
    return shard


def in_blocks(shard, dim, length):
    before, after = (shard.shape[:dim], shard.shape[dim + 1 :])
    return jnp.moveaxis(shard.reshape(*before, length, -1, *after), dim, 0)


def sum_at_owner(shard, axis, dim):
    length = lax.axis_size(axis)
    pieces = lax.all_to_all(in_blocks(shard, dim, length), axis, 0, 0, tiled=True)
    return jnp.sum(pieces, axis=0)


def shifted(extended, axis, length, offset):
    return lax.slice_in_dim(extended, 2 + offset, 2 + offset + length, axis=axis)


def both_diffs(extended, axis, length):
    center = shifted(extended, axis, length, 0)
    plus_one = shifted(extended, axis, length, 1)
    minus_one = shifted(extended, axis, length, -1)
    plus_two = shifted(extended, axis, length, 2)
    minus_two = shifted(extended, axis, length, -2)
    first = (8.0 * (plus_one - minus_one) - (plus_two - minus_two)) / 12.0
    second = (16.0 * (plus_one + minus_one) - (plus_two + minus_two) - 30.0 * center) / 12.0
    return (first, second)


def tile_block(left, right):
    return lax.dot_general(
        left,
        right,
        (((0, 1, 2), (0, 1, 2)), ((), ())),
        preferred_element_type=jnp.float32,
        precision=lax.Precision.HIGHEST,
    )


def on_device(state, register, checkpoint, velocity, diffusivity):
    tile_y = state.shape[2]
    tile_x = state.shape[3]
    padded = with_halo(state, (("gy", 2), ("gx", 3)), 2)
    ext_x = padded[:, :, 2:-2, :]
    ext_y = padded[:, :, :, 2:-2]
    first_x, second_x = both_diffs(ext_x, 3, tile_x)
    first_y, second_y = both_diffs(ext_y, 2, tile_y)
    plus_one = jnp.roll(state, -1, 1)
    minus_one = jnp.roll(state, 1, 1)
    plus_two = jnp.roll(state, -2, 1)
    minus_two = jnp.roll(state, 2, 1)
    first_z = (8.0 * (plus_one - minus_one) - (plus_two - minus_two)) / 12.0
    second_z = (16.0 * (plus_one + minus_one) - (plus_two + minus_two) - 30.0 * state) / 12.0
    advect = velocity[0][None] * first_x + velocity[1][None] * first_y + velocity[2][None] * first_z
    spread = second_x + second_y + second_z
    tendency = -advect + diffusivity[None] * spread
    new_register = carry_weight * register + step_size * tendency
    new_state = state + update_weight * new_register
    change = new_state - checkpoint.astype(jnp.float32)
    rows = tile_block(change, lax.all_gather(change, "gx", axis=3, tiled=True))
    columns = state.shape[0] * state.shape[1] * tile_y * lax.axis_size("gy")
    summed = sum_at_owner(rows, "gy", 1)
    gram = summed / jnp.float32(columns)
    return (new_state, new_register, gram)


def solution(mesh):
    in_specs = (
        P(None, None, "gy", "gx"),
        P(None, None, "gy", "gx"),
        P(None, None, "gy", "gx"),
        P(None, None, "gy", "gx"),
        P(None, "gy", "gx"),
    )
    out_specs = (P(None, None, "gy", "gx"), P(None, None, "gy", "gx"), P("gx", "gy"))
    return jax.shard_map(
        on_device, mesh=mesh, in_specs=in_specs, out_specs=out_specs, check_vma=False
    )
```

profile of v0, /device:TPU:66, one launch (start us, length us, event | category | flops | bytes accessed | tf_op | source)
XLA Modules:
  0.0 206.1 jit_solution(14392529986129787925)
XLA Ops:
  7.2 0.0 all-gather.2.cloned.1.call-start
  7.2 1.7 fusion.4
  8.9 1.9 collective-permute-start.1
  10.8 4.4 %collective-permute-start = (f32[8,16,2,128]{3,1,2,0:T(8,128)}, f32[8,16,2,128]{3,1,2,0:T(8,128)}, u32[]{:S(2)}, u32[]{:S(2)}) collective-permute-start(f32[8,16,2,128]{3,1,2,0:T(8,128)} %get-tuple-element.14), channel_id=1, source_target_pairs={{0,1},{1,2},{2,3},{3,4},{4,5},{5,6},{6,7},{7,8},{8,9},{9,10},{10,1... | collective-permute-start | bytes 393224 | tf_op jit(solution)/shard_map/ppermute | solution.py:19
  15.2 1.7 fusion.3
  16.9 1.3 copy.17
  18.2 1.9 collective-permute-start.3
  20.1 1.3 copy.16
  21.4 4.5 %collective-permute-start.2 = (f32[8,16,12,2]{1,0,3,2:T(8,128)}, f32[8,16,12,2]{1,0,3,2:T(8,128)}, u32[]{:S(2)}, u32[]{:S(2)}) collective-permute-start(f32[8,16,12,2]{1,0,3,2:T(8,128)} %copy.16), channel_id=1, source_target_pairs={{32,0},{64,32},{96,64},{128,96},{160,128},{192,160},{224,192},{256... | collective-permute-start | bytes 36872 | tf_op jit(solution)/shard_map/ppermute | solution.py:20
  25.9 0.7 fusion.6
  26.6 0.7 fusion.8
  27.4 0.1 fusion.7
  27.5 0.0 copy-start.8
  27.6 1.0 fusion.5
  28.6 2.4 %copy.10 = f32[8,16,12,2]{3,1,2,0:T(8,128)} copy(f32[8,16,12,2]{1,0,3,2:T(8,128)} %collective-permute-done.2) | data formatting | bytes 24576 | tf_op jit(solution)/shard_map/ppermute | solution.py:20
  31.0 2.4 %copy.12 = f32[8,16,12,2]{3,1,2,0:T(8,128)} copy(f32[8,16,12,2]{1,0,3,2:T(8,128)} %collective-permute-done.3) | data formatting | bytes 24576 | tf_op jit(solution)/shard_map/ppermute | solution.py:19
  33.5 1.0 constant_dynamic-update-slice_fusion.2
  34.5 0.2 constant_dynamic-update-slice_fusion.1
  34.8 0.9 constant_dynamic-update-slice_fusion
  35.8 0.7 select_maximum_fusion.1
  36.6 0.3 copy-done.1
  36.9 0.2 copy-done.4
  37.1 0.1 copy-done.5
  37.2 0.0 copy-done.6
  37.2 0.0 copy-done.7
  37.3 2.9 %convert_subtract_fusion = (f32[8,16,12,128]{3,1,2,0:T(8,128)}, f32[8,16,12,128]{3,1,2,0:T(8,128)}, f32[8,16,12,128]{3,1,2,0:T(8,128)}) fusion(bf16[8,16,12,128]{3,1,2,0:T(8,128)(2,1)S(1)} %copy-done.5, f32[8,16,12,128]{3,1,2,0:T(8,128)S(1)} %copy-done, f32[16,12,128]{2,0,1:T(8,128)S(1)} %broadcast_multiply_fusion, f32[16,12,128]{2,0,1:T(8,128)S(1)} %get-tuple-element.24, ...), kind=kLoop, calls=%fused_computation.11 | loop fusion | flops 9633792 | bytes 14155776 | tf_op jit(solution)/shard_map/sub | solution.py:86
  40.1 0.0 all-gather.2.cloned.1.call-update
  40.2 90.5 %all-gather.2.cloned.1.call-done = f32[8,16,12,2048]{3,1,2,0:T(8,128)} async-done(((f32[8,16,12,128]{3,1,2,0:T(8,128)}), f32[8,16,12,2048]{3,1,2,0:T(8,128)}) %all-gather.2.cloned.1.call-update) | async-done | bytes 12582928 | tf_op jit(solution)/shard_map/all_gather | solution.py:87
  130.7 23.0 %fusion.9 = f32[128,2048,1,1]{0,1,3,2:T(8,128)S(1)} fusion(f32[8,16,12,128]{3,1,2,0:T(8,128)} %get-tuple-element.3, f32[8,16,12,2048]{3,1,2,0:T(8,128)} %all-gather.2.cloned.1.call-done), kind=kOutput, calls=%fused_computation.31 | convolution fusion | flops 4831838208 | bytes 14417920 | tf_op jit(solution)/shard_map/dot_general | solution.py:58
  153.7 44.8 %all_to_all.5 = f32[32,128,64]{1,2,0:T(8,128)S(1)} all-to-all(f32[32,128,64]{1,2,0:T(8,128)S(1)} %bitcast.13), channel_id=1, replica_groups=mesh['gx'=16,'gy'=32] {'gy'}, dimensions={0} | all-to-all | bytes 2097152 | tf_op jit(solution)/shard_map/all_to_all | solution.py:38
  198.6 0.1 reduce_sum.9
  198.6 0.6 broadcast_multiply_fusion.1
  (24 shorter events, 0.1 us)
Async XLA Ops:
  7.2 123.5 %all-gather.2.cloned.1.call-start = ((), (), s32[]{:S(2)}) async-start(), calls=%async_computation.1 | async-start | bytes 13369344 | tf_op jit(solution)/shard_map/all_gather | solution.py:87
  8.9 25.9 %collective-permute-start.1 = (f32[8,16,2,128]{3,1,2,0:T(8,128)}, f32[8,16,2,128]{3,1,2,0:T(8,128)}, u32[]{:S(2)}, u32[]{:S(2)}) collective-permute-start(f32[8,16,2,128]{3,1,2,0:T(8,128)} %get-tuple-element.13), channel_id=1, source_target_pairs={{1,0},{2,1},{3,2},{4,3},{5,4},{6,5},{7,6},{8,7},{9,8},{10,9},{11,1... | collective-permute-start | bytes 393224 | tf_op jit(solution)/shard_map/ppermute | solution.py:20
  10.8 15.1 %copy-start = (f32[8,16,12,128]{3,1,2,0:T(8,128)S(1)}, f32[8,16,12,128]{3,1,2,0:T(8,128)}, u32[]{:S(2)}) copy-start(f32[8,16,12,128]{3,1,2,0:T(8,128)} %param.5) | copy-start | bytes 2359300
  10.8 22.6 %collective-permute-start = (f32[8,16,2,128]{3,1,2,0:T(8,128)}, f32[8,16,2,128]{3,1,2,0:T(8,128)}, u32[]{:S(2)}, u32[]{:S(2)}) collective-permute-start(f32[8,16,2,128]{3,1,2,0:T(8,128)} %get-tuple-element.14), channel_id=1, source_target_pairs={{0,1},{1,2},{2,3},{3,4},{4,5},{5,6},{6,7},{7,8},{8,9},{9,10},{10,1... | collective-permute-start | bytes 393224 | tf_op jit(solution)/shard_map/ppermute | solution.py:19
  18.2 12.9 %collective-permute-start.3 = (f32[8,16,12,2]{1,0,3,2:T(8,128)}, f32[8,16,12,2]{1,0,3,2:T(8,128)}, u32[]{:S(2)}, u32[]{:S(2)}) collective-permute-start(f32[8,16,12,2]{1,0,3,2:T(8,128)} %copy.17), channel_id=1, source_target_pairs={{0,32},{32,64},{64,96},{96,128},{128,160},{160,192},{192,224},{224... | collective-permute-start | bytes 36872 | tf_op jit(solution)/shard_map/ppermute | solution.py:19
  21.4 7.3 %collective-permute-start.2 = (f32[8,16,12,2]{1,0,3,2:T(8,128)}, f32[8,16,12,2]{1,0,3,2:T(8,128)}, u32[]{:S(2)}, u32[]{:S(2)}) collective-permute-start(f32[8,16,12,2]{1,0,3,2:T(8,128)} %copy.16), channel_id=1, source_target_pairs={{32,0},{64,32},{96,64},{128,96},{160,128},{192,160},{224,192},{256... | collective-permute-start | bytes 36872 | tf_op jit(solution)/shard_map/ppermute | solution.py:20
  27.5 1.0 copy-start.8
  27.5 1.1 copy-start.11
  33.5 2.2 %copy-start.2 = (f32[8,16,12,2]{3,1,2,0:T(8,128)S(1)}, f32[8,16,12,2]{3,1,2,0:T(8,128)}, u32[]{:S(2)}) copy-start(f32[8,16,12,2]{3,1,2,0:T(8,128)} %copy.10) | copy-start | bytes 36868
  33.5 2.3 %copy-start.3 = (f32[8,16,12,2]{3,1,2,0:T(8,128)S(1)}, f32[8,16,12,2]{3,1,2,0:T(8,128)}, u32[]{:S(2)}) copy-start(f32[8,16,12,2]{3,1,2,0:T(8,128)} %copy.12) | copy-start | bytes 36868
  35.7 1.1 copy-start.1
  35.7 1.4 copy-start.4
  35.8 1.4 copy-start.5
  35.8 1.4 copy-start.6
  35.8 1.5 copy-start.7
  35.8 1.5 copy-start.9
  35.8 1.5 copy-start.10
Sparse Core Ops, SparseCore 0:
  40.3 90.3 all-gather.1
where the time goes:
time: 207 us; the launch traced here: 206 us
  waiting for transfers between devices  90.5 us (44%)
  blocking collectives  44.8 us (22%)
  matrix products  23 us (11%)
  local copies, waits for them, and re-layouts  16.3 us (8%)
  between operations  14.3 us (7%)
  starting transfers between devices  12.8 us (6%)
  other arithmetic  4.35 us (2%)
    all_gather x1, waiting for transfers between devices, on_device(): rows = tile_block(change, lax.all_gather(change, 'gx', axis=3, tiled=True))  90.5 us
    all_to_all x1, blocking collectives, sum_at_owner(): lax.all_to_all(in_blocks(shard, dim, length), axis, 0, 0, tiled=True)  44.8 us
    dot_general x1, matrix products, tile_block(): lax.dot_general(left, right, (((0, 1, 2), (0, 1, 2)), ((), ())), preferre...  23 us
    ppermute x2, starting transfers between devices, with_halo(): lax.ppermute(leading, axis, [(b, a) for a, b in up])  6.44 us
    ppermute x2, starting transfers between devices, with_halo(): lax.ppermute(last, axis, up)  6.32 us
    unnamed x28, local copies, waits for them, and re-layouts  4.59 us
  transfers between devices with their start and end apart: 5, of which 1 were waited for; matrix products, arithmetic and copies ran while one was open for 6% of the time, Pallas kernels for 0%

commit v1 on v0

v1 whole, which is shorter than its diff:
```python
import jax
import jax.numpy as jnp
from jax import lax
from jax.experimental import pallas as pl
from jax.experimental.pallas import tpu as pltpu
from jax.sharding import PartitionSpec as P

step_size = 0.3
carry_weight = -5.0 / 9.0
update_weight = 15.0 / 16.0

NX_CHIPS, NY_LO, CORES = 4, 2, 2
HIGHEST = lax.Precision.HIGHEST


def gx_of(x, y, core):
    return (x % NX_CHIPS) * NY_LO * CORES + (y % NY_LO) * CORES + core % CORES


def from_offset(dx, dy, dcore):
    return [
        (gx_of(x + dx, y + dy, core + dcore), gx_of(x, y, core))
        for x in range(NX_CHIPS)
        for y in range(NY_LO)
        for core in range(CORES)
    ]


def fetch(value, dx, dy, dcore):
    return lax.ppermute(value, "gx", from_offset(dx, dy, dcore))


def edge_lanes():
    row = lax.broadcasted_iota(jnp.int32, (8, 128), 0)
    lane = lax.broadcasted_iota(jnp.int32, (8, 128), 1)
    wanted = jnp.where(row < 2, row, row + 124)
    return jnp.where((row < 4) & (lane == wanted), 1.0, 0.0).astype(jnp.float32)


def pack_kernel(s_ref, ylo_ref, yhi_ref, xlo_ref, xhi_ref):
    ny = s_ref.shape[1]
    ylo_ref[...] = s_ref[:, 0:2]
    yhi_ref[...] = s_ref[:, ny - 2 : ny]
    flat = s_ref[...].reshape(-1, 128)
    edges = lax.dot_general(
        edge_lanes(), flat, (((1,), (1,)), ((), ())), preferred_element_type=jnp.float32, precision=HIGHEST
    )
    xlo_ref[...] = edges[0:2]
    xhi_ref[...] = edges[2:4]


def pack(s):
    nv, ny, nz, nx = s.shape
    f32 = jnp.float32
    return pl.pallas_call(
        pack_kernel,
        out_shape=(
            jax.ShapeDtypeStruct((nv, 2, nz, nx), f32),
            jax.ShapeDtypeStruct((nv, 2, nz, nx), f32),
            jax.ShapeDtypeStruct((2, nv * ny * nz), f32),
            jax.ShapeDtypeStruct((2, nv * ny * nz), f32),
        ),
        name="pack_edges",
    )(s)


def stencil_kernel(
    s_ref, r_ref, c_ref, vel_ref, dif_ref, ybelow_ref, yabove_ref, xleft_ref, xright_ref,
    ns_ref, nr_ref, chg_ref, halo_ref, edge_ref,
):
    nvb, ny, nz, nx = s_ref.shape
    halo_ref[...] = jnp.zeros_like(halo_ref)
    halo_ref[0:2, :] = xright_ref[...]
    halo_ref[2:4, :] = xleft_ref[...]
    edge_ref[...] = lax.dot_general(
        halo_ref[...], edge_lanes(), (((0,), (0,)), ((), ())), preferred_element_type=jnp.float32, precision=HIGHEST
    )
    lane = lax.broadcasted_iota(jnp.int32, (nz, nx), 1)

    def row(v, y):
        if y < 0:
            return ybelow_ref[v, y + 2]
        if y >= ny:
            return yabove_ref[v, y - ny]
        return s_ref[v, y]

    for v in range(nvb):
        for y in range(ny):
            f = row(v, y)
            e = edge_ref[pl.ds((v * ny + y) * nz, nz), :]
            xp1 = pltpu.roll(jnp.where(lane < 1, e, f), nx - 1, 1)
            xp2 = pltpu.roll(jnp.where(lane < 2, e, f), nx - 2, 1)
            xm1 = pltpu.roll(jnp.where(lane >= nx - 1, e, f), 1, 1)
            xm2 = pltpu.roll(jnp.where(lane >= nx - 2, e, f), 2, 1)
            yp1, yp2, ym1, ym2 = row(v, y + 1), row(v, y + 2), row(v, y - 1), row(v, y - 2)
            zp1 = pltpu.roll(f, nz - 1, 0)
            zp2 = pltpu.roll(f, nz - 2, 0)
            zm1 = pltpu.roll(f, 1, 0)
            zm2 = pltpu.roll(f, 2, 0)
            first_x = 8.0 * (xp1 - xm1) - (xp2 - xm2)
            first_y = 8.0 * (yp1 - ym1) - (yp2 - ym2)
            first_z = 8.0 * (zp1 - zm1) - (zp2 - zm2)
            near = (xp1 + xm1) + (yp1 + ym1) + (zp1 + zm1)
            far = (xp2 + xm2) + (yp2 + ym2) + (zp2 + zm2)
            spread = 16.0 * near - far - 90.0 * f
            advect = vel_ref[0, y] * first_x + vel_ref[1, y] * first_y + vel_ref[2, y] * first_z
            tendency = dif_ref[y] * spread - advect
            new_register = carry_weight * r_ref[v, y] + (step_size / 12.0) * tendency
            new_state = f + update_weight * new_register
            ns_ref[v, y] = new_state
            nr_ref[v, y] = new_register
            chg_ref[v, y] = new_state - c_ref[v, y].astype(jnp.float32)


def stencil(s, r, c, vel, dif, ybelow, yabove, xleft, xright, per_step=2):
    nv, ny, nz, nx = s.shape
    whole = pl.BlockSpec((per_step, ny, nz, nx), lambda i: (i, 0, 0, 0))
    side = pl.BlockSpec((per_step, 2, nz, nx), lambda i: (i, 0, 0, 0))
    cols = per_step * ny * nz
    edge = pl.BlockSpec((2, cols), lambda i: (0, i))
    out = jax.ShapeDtypeStruct(s.shape, jnp.float32)
    return pl.pallas_call(
        stencil_kernel,
        grid=(nv // per_step,),
        in_specs=[
            whole, whole, whole,
            pl.BlockSpec(vel.shape, lambda i: (0, 0, 0, 0)),
            pl.BlockSpec(dif.shape, lambda i: (0, 0, 0)),
            side, side, edge, edge,
        ],
        out_specs=[whole, whole, whole],
        out_shape=[out, out, out],
        scratch_shapes=[pltpu.VMEM((8, cols), jnp.float32), pltpu.VMEM((cols, nx), jnp.float32)],
        name="stencil",
    )(s, r, c, vel, dif, ybelow, yabove, xleft, xright)


def place_kernel(where_ref, own_ref, other_ref, out_ref):
    x, y, core = where_ref[0], where_ref[1], where_ref[2]
    for dx in range(NX_CHIPS):
        for dcore in range(CORES):
            for dy, source in ((0, own_ref), (1, other_ref)):
                at = (
                    ((x + dx) % NX_CHIPS) * NY_LO * CORES
                    + ((y + dy) % NY_LO) * CORES
                    + (core + dcore) % CORES
                )
                out_ref[at] = source[dx, dcore]


def place(where, own, other):
    n = own.shape[0] * own.shape[1] * NY_LO
    vmem = pl.BlockSpec(memory_space=pltpu.VMEM)
    return pl.pallas_call(
        place_kernel,
        in_specs=[pl.BlockSpec(memory_space=pltpu.SMEM), vmem, vmem],
        out_specs=vmem,
        out_shape=jax.ShapeDtypeStruct((n,) + own.shape[2:], jnp.float32),
        name="place",
    )(where, own, other)


def against(columns, rows):
    return lax.dot_general(
        columns, rows, (((0,), (0,)), ((), ())), preferred_element_type=jnp.float32, precision=lax.Precision.HIGH
    )


def on_device(state, register, checkpoint, velocity, diffusivity):
    nv, nz, ny, nx = state.shape
    to_yzx = lambda a: jnp.swapaxes(a, -3, -2)
    s, r, c = to_yzx(state), to_yzx(register), to_yzx(checkpoint)
    ylo, yhi, xlo, xhi = pack(s)
    up = lambda n: [(i, (i + 1) % n) for i in range(n)]
    down = lambda n: [(b, a) for a, b in up(n)]
    n_gx, n_gy = lax.axis_size("gx"), lax.axis_size("gy")
    xleft = lax.ppermute(xhi, "gx", up(n_gx))
    xright = lax.ppermute(xlo, "gx", down(n_gx))
    ybelow = lax.ppermute(yhi, "gy", up(n_gy))
    yabove = lax.ppermute(ylo, "gy", down(n_gy))
    new_state, new_register, change = stencil(
        s, r, c, to_yzx(velocity), to_yzx(diffusivity), ybelow, yabove, xleft, xright
    )
    depth = nv * ny * nz
    half = depth // 2
    mine = change.reshape(depth, nx)
    right = fetch(mine, 1, 0, 0)
    left = fetch(mine, -1, 0, 0)
    across = fetch(mine, 0, 1, 0)
    mine_too = fetch(mine, 0, 0, 1)
    far0 = fetch(right[:half], 1, 0, 0)
    far1 = fetch(left[half:], -1, 0, 0)
    right_too = fetch(right, 0, 0, 1)
    left_too = fetch(left, 0, 0, 1)
    far0_too = fetch(far0, 0, 0, 1)
    far1_too = fetch(far1, 0, 0, 1)
    rows = jnp.concatenate([mine, across], axis=1)
    near = [against(a, rows) for a in (mine, mine_too, right, right_too, left, left_too)]
    far = [
        against(a, rows[:half]) + against(b, rows[half:]) for a, b in ((far0, far1), (far0_too, far1_too))
    ]
    blocks = jnp.stack(near[:4] + far + near[4:]).reshape(NX_CHIPS, CORES, nx, 2 * nx)
    own, theirs = blocks[..., :nx], blocks[..., nx:]
    other = fetch(theirs, 0, 1, 0)
    gx = lax.axis_index("gx")
    where = jnp.stack([gx // (NY_LO * CORES), (gx // CORES) % NY_LO, gx % CORES]).astype(jnp.int32)
    partial = place(where, own, other).reshape(n_gy, -1, nx)
    pieces = lax.all_to_all(partial, "gy", 0, 0, tiled=True)
    columns = nv * nz * ny * n_gy
    gram = jnp.sum(pieces, axis=0) / jnp.float32(columns)
    return to_yzx(new_state), to_yzx(new_register), gram.T


def solution(mesh):
    in_specs = (
        P(None, None, "gy", "gx"),
        P(None, None, "gy", "gx"),
        P(None, None, "gy", "gx"),
        P(None, None, "gy", "gx"),
        P(None, "gy", "gx"),
    )
    out_specs = (P(None, None, "gy", "gx"), P(None, None, "gy", "gx"), P("gx", "gy"))
    return jax.shard_map(
        on_device, mesh=mesh, in_specs=in_specs, out_specs=out_specs, check_vma=False
    )
```

time: 207 us -> 140 us (0.68)
  the two profiles are of different devices: /device:TPU:66 before, /device:TPU:14 now
where the time goes in v1:
time: 140 us; the launch traced here: 139 us
  starting transfers between devices  52.5 us (38%)
  blocking collectives  40.9 us (29%)
  waiting for transfers between devices  23.7 us (17%)
  Pallas kernels  10.5 us (8%)
  matrix products  6.8 us (5%)
  local copies, waits for them, and re-layouts  2.45 us (2%)
    all_to_all x1, blocking collectives, on_device(): pieces = lax.all_to_all(partial, 'gy', 0, 0, tiled=True)  40.9 us
    ppermute x11, starting transfers between devices, fetch(): return lax.ppermute(value, 'gx', from_offset(dx, dy, dcore))  31.3 us
    ppermute x11, waiting for transfers between devices, fetch(): return lax.ppermute(value, 'gx', from_offset(dx, dy, dcore))  22.2 us
    ppermute x1, starting transfers between devices, on_device(): yabove = lax.ppermute(ylo, 'gy', down(n_gy))  11.4 us
    dot_general x10, matrix products, against(): lax.dot_general(columns, rows, (((0,), (0,)), ((), ())), preferred_elemen...  6.8 us
    pallas_call x1, Pallas kernels, stencil(): pl.pallas_call(stencil_kernel, grid=(nv // per_step,), in_specs=[whole, w...  5.78 us
    ppermute x1, starting transfers between devices, on_device(): ybelow = lax.ppermute(yhi, 'gy', up(n_gy))  4.27 us
    ppermute x1, starting transfers between devices, on_device(): xright = lax.ppermute(xlo, 'gx', down(n_gx))  3.64 us
  transfers between devices with their start and end apart: 15, of which 5 were waited for; matrix products, arithmetic and copies ran while one was open for 5% of the time, Pallas kernels for 0%

profile of v1, /device:TPU:14, one launch (start us, length us, event | category | flops | bytes accessed | tf_op | source)
XLA Modules:
  0.0 139.3 jit_solution(922514573904310579)
XLA Ops:
  0.6 2.5 %pack_edges.1 = (f32[8,2,16,128]{3,2,1,0:T(8,128)}, f32[8,2,16,128]{3,2,1,0:T(8,128)}, f32[2,1536]{1,0:T(2,128)}, f32[2,1536]{1,0:T(2,128)}) custom-call(f32[8,12,16,128]{3,2,1,0:T(8,128)} %bitcast.72), custom_call_target="tpu_custom_call" | custom-call | tf_op jit(solution)/shard_map/pack_edges/pallas_call | solution.py:55
  3.1 4.3 %collective-permute-start = (f32[8,2,16,128]{3,2,1,0:T(8,128)}, f32[8,2,16,128]{3,2,1,0:T(8,128)S(1)}, u32[]{:S(2)}, u32[]{:S(2)}) collective-permute-start(f32[8,2,16,128]{3,2,1,0:T(8,128)} %get-tuple-element.10), channel_id=1, source_target_pairs={{0,1},{1,2},{2,3},{3,4},{4,5},{5,6},{6,7},{7,8},{8,9},{9,10},{10,1... | collective-permute-start | bytes 393224 | tf_op jit(solution)/shard_map/ppermute | solution.py:179
  7.4 11.4 %collective-permute-start.1 = (f32[8,2,16,128]{3,2,1,0:T(8,128)}, f32[8,2,16,128]{3,2,1,0:T(8,128)S(1)}, u32[]{:S(2)}, u32[]{:S(2)}) collective-permute-start(f32[8,2,16,128]{3,2,1,0:T(8,128)} %get-tuple-element.11), channel_id=1, source_target_pairs={{1,0},{2,1},{3,2},{4,3},{5,4},{6,5},{7,6},{8,7},{9,8},{10,9},{11,1... | collective-permute-start | bytes 393224 | tf_op jit(solution)/shard_map/ppermute | solution.py:180
  18.8 1.9 %collective-permute-start.2 = (f32[2,1536]{1,0:T(2,128)}, f32[2,1536]{1,0:T(2,128)S(1)}, u32[]{:S(2)}, u32[]{:S(2)}) collective-permute-start(f32[2,1536]{1,0:T(2,128)} %get-tuple-element.12), channel_id=1, source_target_pairs={{0,32},{32,64},{64,96},{96,128},{128,160},{160,192},{192,224},{224... | collective-permute-start | bytes 36872 | tf_op jit(solution)/shard_map/ppermute | solution.py:177
  20.7 3.6 %collective-permute-start.3 = (f32[2,1536]{1,0:T(2,128)}, f32[2,1536]{1,0:T(2,128)S(1)}, u32[]{:S(2)}, u32[]{:S(2)}) collective-permute-start(f32[2,1536]{1,0:T(2,128)} %get-tuple-element.13), channel_id=1, source_target_pairs={{32,0},{64,32},{96,64},{128,96},{160,128},{192,160},{224,192},{256... | collective-permute-start | bytes 36872 | tf_op jit(solution)/shard_map/ppermute | solution.py:178
  24.4 1.6 %collective-permute-done.3.xright_ref = f32[2,1536]{1,0:T(2,128)S(1)} collective-permute-done((f32[2,1536]{1,0:T(2,128)}, f32[2,1536]{1,0:T(2,128)S(1)}, u32[]{:S(2)}, u32[]{:S(2)}) %collective-permute-start.3) | collective-permute-done | bytes 12320 | tf_op jit(solution)/shard_map/ppermute | solution.py:178
  26.6 5.8 %stencil.1 = (f32[8,12,16,128]{3,2,1,0:T(8,128)}, f32[8,12,16,128]{3,2,1,0:T(8,128)}, f32[8,12,16,128]{3,2,1,0:T(8,128)}) custom-call(f32[8,12,16,128]{3,2,1,0:T(8,128)} %bitcast.73, f32[8,12,16,128]{3,2,1,0:T(8,128)} %bitcast.75, bf16[8,12,16,128]{3,2,1,0:T(8,128)(2,1)} %bitcast.76, f32[3,12,16,128]{3,2,1,0:T(8,128)} %bitcast.77, f32[12,16,128]{2,1,0:T(8,128)} %bitcast.78, ...), custom_call_target="tpu_custom_call" | custom-call | tf_op jit(solution)/shard_map/stencil/pallas_call | solution.py:122
  32.4 2.5 %collective-permute-start.9 = (f32[1536,128]{1,0:T(8,128)}, f32[1536,128]{1,0:T(8,128)S(1)}, u32[]{:S(2)}, u32[]{:S(2)}) collective-permute-start(f32[1536,128]{1,0:T(8,128)} %bitcast.57), channel_id=1, source_target_pairs={{384,0},{416,32},{448,64},{480,96},{0,128},{32,160},{64,192},{96,2... | collective-permute-start | bytes 2359304 | tf_op jit(solution)/shard_map/ppermute | solution.py:30
  34.9 3.5 %collective-permute-start.6 = (f32[1536,128]{1,0:T(8,128)}, f32[1536,128]{1,0:T(8,128)S(1)}, u32[]{:S(2)}, u32[]{:S(2)}) collective-permute-start(f32[1536,128]{1,0:T(8,128)} %bitcast.58), channel_id=1, source_target_pairs={{128,0},{160,32},{192,64},{224,96},{256,128},{288,160},{320,192},{... | collective-permute-start | bytes 2359304 | tf_op jit(solution)/shard_map/ppermute | solution.py:30
  38.4 4.2 %collective-permute-start.4 = (f32[1536,128]{1,0:T(8,128)}, f32[1536,128]{1,0:T(8,128)S(1)}, u32[]{:S(2)}, u32[]{:S(2)}) collective-permute-start(f32[1536,128]{1,0:T(8,128)} %bitcast.59), channel_id=1, source_target_pairs={{64,0},{96,32},{0,64},{32,96},{192,128},{224,160},{128,192},{160,2... | collective-permute-start | bytes 2359304 | tf_op jit(solution)/shard_map/ppermute | solution.py:30
  42.6 2.6 %collective-permute-start.5 = (f32[1536,128]{1,0:T(8,128)}, f32[1536,128]{1,0:T(8,128)S(1)}, u32[]{:S(2)}, u32[]{:S(2)}) collective-permute-start(f32[1536,128]{1,0:T(8,128)} %bitcast.60), channel_id=1, source_target_pairs={{32,0},{0,32},{96,64},{64,96},{160,128},{128,160},{224,192},{192,2... | collective-permute-start | bytes 2359304 | tf_op jit(solution)/shard_map/ppermute | solution.py:30
  45.1 7.4 %collective-permute-done.9 = f32[1536,128]{1,0:T(8,128)S(1)} collective-permute-done((f32[1536,128]{1,0:T(8,128)}, f32[1536,128]{1,0:T(8,128)S(1)}, u32[]{:S(2)}, u32[]{:S(2)}) %collective-permute-start.9) | collective-permute-done | bytes 786464 | tf_op jit(solution)/shard_map/ppermute | solution.py:30
  52.6 3.8 %collective-permute-start.10 = (f32[768,128]{1,0:T(8,128)S(1)}, f32[768,128]{1,0:T(8,128)S(1)}, u32[]{:S(2)}, u32[]{:S(2)}) collective-permute-start(f32[768,128]{1,0:T(8,128)S(1)} %slice.29), channel_id=1, source_target_pairs={{384,0},{416,32},{448,64},{480,96},{0,128},{32,160},{64,192},{96,2... | collective-permute-start | bytes 1179656 | tf_op jit(solution)/shard_map/ppermute | solution.py:30
  56.7 2.1 %collective-permute-start.8 = (f32[768,128]{1,0:T(8,128)S(1)}, f32[768,128]{1,0:T(8,128)S(1)}, u32[]{:S(2)}, u32[]{:S(2)}) collective-permute-start(f32[768,128]{1,0:T(8,128)S(1)} %slice.26), channel_id=1, source_target_pairs={{128,0},{160,32},{192,64},{224,96},{256,128},{288,160},{320,192},{... | collective-permute-start | bytes 1179656 | tf_op jit(solution)/shard_map/ppermute | solution.py:30
  58.7 4.0 %collective-permute-start.7 = (f32[1536,128]{1,0:T(8,128)S(1)}, f32[1536,128]{1,0:T(8,128)S(1)}, u32[]{:S(2)}, u32[]{:S(2)}) collective-permute-start(f32[1536,128]{1,0:T(8,128)S(1)} %collective-permute-done.6), channel_id=1, source_target_pairs={{32,0},{0,32},{96,64},{64,96},{160,128},{128,160},{224,192},{192,2... | collective-permute-start | bytes 2359304 | tf_op jit(solution)/shard_map/ppermute | solution.py:30
  62.7 1.9 %collective-permute-start.13 = (f32[1536,128]{1,0:T(8,128)S(1)}, f32[1536,128]{1,0:T(8,128)S(1)}, u32[]{:S(2)}, u32[]{:S(2)}) collective-permute-start(f32[1536,128]{1,0:T(8,128)S(1)} %collective-permute-done.9), channel_id=1, source_target_pairs={{32,0},{0,32},{96,64},{64,96},{160,128},{128,160},{224,192},{192,2... | collective-permute-start | bytes 2359304 | tf_op jit(solution)/shard_map/ppermute | solution.py:30
  64.7 0.8 fusion.5
  65.5 0.8 fusion.4
  66.3 0.8 fusion.3
  67.1 2.4 %collective-permute-start.12 = (f32[768,128]{1,0:T(8,128)S(1)}, f32[768,128]{1,0:T(8,128)S(1)}, u32[]{:S(2)}, u32[]{:S(2)}) collective-permute-start(f32[768,128]{1,0:T(8,128)S(1)} %collective-permute-done.10), channel_id=1, source_target_pairs={{32,0},{0,32},{96,64},{64,96},{160,128},{128,160},{224,192},{192,2... | collective-permute-start | bytes 1179656 | tf_op jit(solution)/shard_map/ppermute | solution.py:30
  69.5 1.4 collective-permute-done.8
  70.9 2.6 %collective-permute-start.11 = (f32[768,128]{1,0:T(8,128)S(1)}, f32[768,128]{1,0:T(8,128)S(1)}, u32[]{:S(2)}, u32[]{:S(2)}) collective-permute-start(f32[768,128]{1,0:T(8,128)S(1)} %collective-permute-done.8), channel_id=1, source_target_pairs={{32,0},{0,32},{96,64},{64,96},{160,128},{128,160},{224,192},{192,2... | collective-permute-start | bytes 1179656 | tf_op jit(solution)/shard_map/ppermute | solution.py:30
  74.0 0.8 fusion.2
  76.3 0.8 fusion.1
  77.2 0.8 fusion
  78.0 0.9 fusion.28
  78.9 1.9 %collective-permute-start.14 = (f32[4,2,128,128]{3,2,1,0:T(8,128)S(1)}, f32[4,2,128,128]{3,2,1,0:T(8,128)S(1)}, u32[]{:S(2)}, u32[]{:S(2)}) collective-permute-start(f32[4,2,128,128]{3,2,1,0:T(8,128)S(1)} %get-tuple-element.17), channel_id=1, source_target_pairs={{64,0},{96,32},{0,64},{32,96},{192,128},{224,160},{128,192},{160,2... | collective-permute-start | bytes 1572872 | tf_op jit(solution)/shard_map/ppermute | solution.py:30
  80.8 0.7 pad_add_fusion.where_ref
  81.5 13.1 %collective-permute-done.14.other_ref = f32[4,2,128,128]{3,2,1,0:T(8,128)S(1)} collective-permute-done((f32[4,2,128,128]{3,2,1,0:T(8,128)S(1)}, f32[4,2,128,128]{3,2,1,0:T(8,128)S(1)}, u32[]{:S(2)}, u32[]{:S(2)}) %collective-permute-start.14) | collective-permute-done | bytes 524320 | tf_op jit(solution)/shard_map/ppermute | solution.py:30
  94.6 0.8 copy-done.1
  95.4 2.3 %place.1 = f32[16,128,128]{2,1,0:T(8,128)} custom-call(s32[3]{0:T(128)} %pad_add_fusion.where_ref, f32[4,2,128,128]{3,2,1,0:T(8,128)} %get-tuple-element.18.own_ref, f32[4,2,128,128]{3,2,1,0:T(8,128)} %copy-done.1), custom_call_target="tpu_custom_call" | custom-call | tf_op jit(solution)/shard_map/place/pallas_call | solution.py:154
  97.7 40.9 %all_to_all.5 = f32[32,64,128]{2,1,0:T(8,128)S(1)} all-to-all(f32[32,64,128]{2,1,0:T(8,128)} %bitcast.71), channel_id=1, replica_groups=mesh['gx'=16,'gy'=32] {'gy'}, dimensions={0} | all-to-all | bytes 2097152 | tf_op jit(solution)/shard_map/all_to_all | solution.py:208
  (30 shorter events, 3.7 us)
Async XLA Ops:
  3.1 22.8 %collective-permute-start = (f32[8,2,16,128]{3,2,1,0:T(8,128)}, f32[8,2,16,128]{3,2,1,0:T(8,128)S(1)}, u32[]{:S(2)}, u32[]{:S(2)}) collective-permute-start(f32[8,2,16,128]{3,2,1,0:T(8,128)} %get-tuple-element.10), channel_id=1, source_target_pairs={{0,1},{1,2},{2,3},{3,4},{4,5},{5,6},{6,7},{7,8},{8,9},{9,10},{10,1... | collective-permute-start | bytes 393224 | tf_op jit(solution)/shard_map/ppermute | solution.py:179
  7.4 18.6 %collective-permute-start.1 = (f32[8,2,16,128]{3,2,1,0:T(8,128)}, f32[8,2,16,128]{3,2,1,0:T(8,128)S(1)}, u32[]{:S(2)}, u32[]{:S(2)}) collective-permute-start(f32[8,2,16,128]{3,2,1,0:T(8,128)} %get-tuple-element.11), channel_id=1, source_target_pairs={{1,0},{2,1},{3,2},{4,3},{5,4},{6,5},{7,6},{8,7},{9,8},{10,9},{11,1... | collective-permute-start | bytes 393224 | tf_op jit(solution)/shard_map/ppermute | solution.py:180
  18.8 5.6 %collective-permute-start.2 = (f32[2,1536]{1,0:T(2,128)}, f32[2,1536]{1,0:T(2,128)S(1)}, u32[]{:S(2)}, u32[]{:S(2)}) collective-permute-start(f32[2,1536]{1,0:T(2,128)} %get-tuple-element.12), channel_id=1, source_target_pairs={{0,32},{32,64},{64,96},{96,128},{128,160},{160,192},{192,224},{224... | collective-permute-start | bytes 36872 | tf_op jit(solution)/shard_map/ppermute | solution.py:177
  20.7 5.2 %collective-permute-start.3 = (f32[2,1536]{1,0:T(2,128)}, f32[2,1536]{1,0:T(2,128)S(1)}, u32[]{:S(2)}, u32[]{:S(2)}) collective-permute-start(f32[2,1536]{1,0:T(2,128)} %get-tuple-element.13), channel_id=1, source_target_pairs={{32,0},{64,32},{96,64},{128,96},{160,128},{192,160},{224,192},{256... | collective-permute-start | bytes 36872 | tf_op jit(solution)/shard_map/ppermute | solution.py:178
  24.4 1.6 %copy-start.4 = (f32[2,1536]{1,0:T(2,128)}, f32[2,1536]{1,0:T(2,128)S(1)}, u32[]{:S(2)}) copy-start(f32[2,1536]{1,0:T(2,128)S(1)} %collective-permute-done.2.xleft_ref) | copy-start | bytes 36868
  25.9 0.6 copy-start.5
  25.9 0.6 copy-start.2
  26.0 0.7 copy-start.3
  32.4 32.2 %copy-start = (f32[8,12,16,128]{3,2,1,0:T(8,128)S(1)}, f32[8,12,16,128]{3,2,1,0:T(8,128)}, u32[]{:S(2)}) copy-start(f32[8,12,16,128]{3,2,1,0:T(8,128)} %get-tuple-element.16) | copy-start | bytes 2359300
  32.4 20.2 %collective-permute-start.9 = (f32[1536,128]{1,0:T(8,128)}, f32[1536,128]{1,0:T(8,128)S(1)}, u32[]{:S(2)}, u32[]{:S(2)}) collective-permute-start(f32[1536,128]{1,0:T(8,128)} %bitcast.57), channel_id=1, source_target_pairs={{384,0},{416,32},{448,64},{480,96},{0,128},{32,160},{64,192},{96,2... | collective-permute-start | bytes 2359304 | tf_op jit(solution)/shard_map/ppermute | solution.py:30
  34.9 21.7 %collective-permute-start.6 = (f32[1536,128]{1,0:T(8,128)}, f32[1536,128]{1,0:T(8,128)S(1)}, u32[]{:S(2)}, u32[]{:S(2)}) collective-permute-start(f32[1536,128]{1,0:T(8,128)} %bitcast.58), channel_id=1, source_target_pairs={{128,0},{160,32},{192,64},{224,96},{256,128},{288,160},{320,192},{... | collective-permute-start | bytes 2359304 | tf_op jit(solution)/shard_map/ppermute | solution.py:30
  38.4 24.3 %collective-permute-start.4 = (f32[1536,128]{1,0:T(8,128)}, f32[1536,128]{1,0:T(8,128)S(1)}, u32[]{:S(2)}, u32[]{:S(2)}) collective-permute-start(f32[1536,128]{1,0:T(8,128)} %bitcast.59), channel_id=1, source_target_pairs={{64,0},{96,32},{0,64},{32,96},{192,128},{224,160},{128,192},{160,2... | collective-permute-start | bytes 2359304 | tf_op jit(solution)/shard_map/ppermute | solution.py:30
  42.6 22.9 %collective-permute-start.5 = (f32[1536,128]{1,0:T(8,128)}, f32[1536,128]{1,0:T(8,128)S(1)}, u32[]{:S(2)}, u32[]{:S(2)}) collective-permute-start(f32[1536,128]{1,0:T(8,128)} %bitcast.60), channel_id=1, source_target_pairs={{32,0},{0,32},{96,64},{64,96},{160,128},{128,160},{224,192},{192,2... | collective-permute-start | bytes 2359304 | tf_op jit(solution)/shard_map/ppermute | solution.py:30
  52.6 14.5 %collective-permute-start.10 = (f32[768,128]{1,0:T(8,128)S(1)}, f32[768,128]{1,0:T(8,128)S(1)}, u32[]{:S(2)}, u32[]{:S(2)}) collective-permute-start(f32[768,128]{1,0:T(8,128)S(1)} %slice.29), channel_id=1, source_target_pairs={{384,0},{416,32},{448,64},{480,96},{0,128},{32,160},{64,192},{96,2... | collective-permute-start | bytes 1179656 | tf_op jit(solution)/shard_map/ppermute | solution.py:30
  56.7 14.2 %collective-permute-start.8 = (f32[768,128]{1,0:T(8,128)S(1)}, f32[768,128]{1,0:T(8,128)S(1)}, u32[]{:S(2)}, u32[]{:S(2)}) collective-permute-start(f32[768,128]{1,0:T(8,128)S(1)} %slice.26), channel_id=1, source_target_pairs={{128,0},{160,32},{192,64},{224,96},{256,128},{288,160},{320,192},{... | collective-permute-start | bytes 1179656 | tf_op jit(solution)/shard_map/ppermute | solution.py:30
  58.7 15.2 %collective-permute-start.7 = (f32[1536,128]{1,0:T(8,128)S(1)}, f32[1536,128]{1,0:T(8,128)S(1)}, u32[]{:S(2)}, u32[]{:S(2)}) collective-permute-start(f32[1536,128]{1,0:T(8,128)S(1)} %collective-permute-done.6), channel_id=1, source_target_pairs={{32,0},{0,32},{96,64},{64,96},{160,128},{128,160},{224,192},{192,2... | collective-permute-start | bytes 2359304 | tf_op jit(solution)/shard_map/ppermute | solution.py:30
  62.7 14.4 %collective-permute-start.13 = (f32[1536,128]{1,0:T(8,128)S(1)}, f32[1536,128]{1,0:T(8,128)S(1)}, u32[]{:S(2)}, u32[]{:S(2)}) collective-permute-start(f32[1536,128]{1,0:T(8,128)S(1)} %collective-permute-done.9), channel_id=1, source_target_pairs={{32,0},{0,32},{96,64},{64,96},{160,128},{128,160},{224,192},{192,2... | collective-permute-start | bytes 2359304 | tf_op jit(solution)/shard_map/ppermute | solution.py:30
  67.1 7.7 %collective-permute-start.12 = (f32[768,128]{1,0:T(8,128)S(1)}, f32[768,128]{1,0:T(8,128)S(1)}, u32[]{:S(2)}, u32[]{:S(2)}) collective-permute-start(f32[768,128]{1,0:T(8,128)S(1)} %collective-permute-done.10), channel_id=1, source_target_pairs={{32,0},{0,32},{96,64},{64,96},{160,128},{128,160},{224,192},{192,2... | collective-permute-start | bytes 1179656 | tf_op jit(solution)/shard_map/ppermute | solution.py:30
  70.9 4.9 %collective-permute-start.11 = (f32[768,128]{1,0:T(8,128)S(1)}, f32[768,128]{1,0:T(8,128)S(1)}, u32[]{:S(2)}, u32[]{:S(2)}) collective-permute-start(f32[768,128]{1,0:T(8,128)S(1)} %collective-permute-done.8), channel_id=1, source_target_pairs={{32,0},{0,32},{96,64},{64,96},{160,128},{128,160},{224,192},{192,2... | collective-permute-start | bytes 1179656 | tf_op jit(solution)/shard_map/ppermute | solution.py:30
  78.9 15.7 %collective-permute-start.14 = (f32[4,2,128,128]{3,2,1,0:T(8,128)S(1)}, f32[4,2,128,128]{3,2,1,0:T(8,128)S(1)}, u32[]{:S(2)}, u32[]{:S(2)}) collective-permute-start(f32[4,2,128,128]{3,2,1,0:T(8,128)S(1)} %get-tuple-element.17), channel_id=1, source_target_pairs={{64,0},{96,32},{0,64},{32,96},{192,128},{224,160},{128,192},{160,2... | collective-permute-start | bytes 1572872 | tf_op jit(solution)/shard_map/ppermute | solution.py:30
  94.6 0.8 copy-start.1

commit v2 on v1

--- a/solution.py
+++ b/solution.py
@@ -135,29 +135,42 @@
     )(s, r, c, vel, dif, ybelow, yabove, xleft, xright)
 
 
-def place_kernel(where_ref, own_ref, other_ref, out_ref):
-    x, y, core = where_ref[0], where_ref[1], where_ref[2]
-    for dx in range(NX_CHIPS):
-        for dcore in range(CORES):
-            for dy, source in ((0, own_ref), (1, other_ref)):
-                at = (
-                    ((x + dx) % NX_CHIPS) * NY_LO * CORES
-                    + ((y + dy) % NY_LO) * CORES
-                    + (core + dcore) % CORES
-                )
-                out_ref[at] = source[dx, dcore]
-
-
-def place(where, own, other):
-    n = own.shape[0] * own.shape[1] * NY_LO
+def place_kernel(near_ref, far_ref, near_y_ref, far_y_ref, near_c_ref, far_c_ref, near_yc_ref, far_yc_ref, out_ref):
+    gx = lax.axis_index("gx")
+    core = lax.rem(gx, CORES)
+    y = lax.rem(lax.div(gx, CORES), NY_LO)
+    x = lax.div(gx, CORES * NY_LO)
+    nx = out_ref.shape[-1]
+    sources = (
+        (0, 0, near_ref, far_ref),
+        (1, 0, near_y_ref, far_y_ref),
+        (0, 1, near_c_ref, far_c_ref),
+        (1, 1, near_yc_ref, far_yc_ref),
+    )
+    for dy, dcore, near, far in sources:
+        lanes = slice(dcore * nx, dcore * nx + nx)
+        for dx in range(NX_CHIPS):
+            at = (
+                lax.rem(x + dx, NX_CHIPS) * (NY_LO * CORES)
+                + lax.rem(y + dy, NY_LO) * CORES
+                + lax.rem(core + dcore, CORES)
+            )
+            out_ref[at] = far[:, lanes] if dx == 2 else near[NEAR.index(dx), :, lanes]
+
+
+NEAR = (0, 1, 3)
+
+
+def place(*parts):
+    nx = parts[0].shape[-2]
     vmem = pl.BlockSpec(memory_space=pltpu.VMEM)
     return pl.pallas_call(
         place_kernel,
-        in_specs=[pl.BlockSpec(memory_space=pltpu.SMEM), vmem, vmem],
+        in_specs=[vmem] * len(parts),
         out_specs=vmem,
-        out_shape=jax.ShapeDtypeStruct((n,) + own.shape[2:], jnp.float32),
+        out_shape=jax.ShapeDtypeStruct((NX_CHIPS * NY_LO * CORES, nx, nx), jnp.float32),
         name="place",
-    )(where, own, other)
+    )(*parts)
 
 
 def against(columns, rows):
@@ -184,27 +197,30 @@
     depth = nv * ny * nz
     half = depth // 2
     mine = change.reshape(depth, nx)
-    right = fetch(mine, 1, 0, 0)
-    left = fetch(mine, -1, 0, 0)
+    front, back = mine[:half], mine[half:]
+    right0 = fetch(front, 1, 0, 0)
+    left1 = fetch(back, -1, 0, 0)
     across = fetch(mine, 0, 1, 0)
-    mine_too = fetch(mine, 0, 0, 1)
-    far0 = fetch(right[:half], 1, 0, 0)
-    far1 = fetch(left[half:], -1, 0, 0)
-    right_too = fetch(right, 0, 0, 1)
-    left_too = fetch(left, 0, 0, 1)
-    far0_too = fetch(far0, 0, 0, 1)
-    far1_too = fetch(far1, 0, 0, 1)
-    rows = jnp.concatenate([mine, across], axis=1)
-    near = [against(a, rows) for a in (mine, mine_too, right, right_too, left, left_too)]
-    far = [
-        against(a, rows[:half]) + against(b, rows[half:]) for a, b in ((far0, far1), (far0_too, far1_too))
-    ]
-    blocks = jnp.stack(near[:4] + far + near[4:]).reshape(NX_CHIPS, CORES, nx, 2 * nx)
-    own, theirs = blocks[..., :nx], blocks[..., nx:]
-    other = fetch(theirs, 0, 1, 0)
-    gx = lax.axis_index("gx")
-    where = jnp.stack([gx // (NY_LO * CORES), (gx // CORES) % NY_LO, gx % CORES]).astype(jnp.int32)
-    partial = place(where, own, other).reshape(n_gy, -1, nx)
+    mine_c = fetch(mine, 0, 0, 1)
+    right1 = fetch(back, 1, 0, 0)
+    left0 = fetch(front, -1, 0, 0)
+    far0 = fetch(right0, 1, 0, 0)
+    far1 = fetch(left1, -1, 0, 0)
+    across_c = fetch(across, 0, 0, 1)
+
+    def by_halves(a, b, rows):
+        return against(a, rows[:half]) + against(b, rows[half:])
+
+    def products(rows):
+        near = jnp.stack([against(mine, rows), by_halves(right0, right1, rows), by_halves(left0, left1, rows)])
+        return near, by_halves(far0, far1, rows)
+
+    near, far = products(jnp.concatenate([mine, mine_c], axis=1))
+    near_y, far_y = products(jnp.concatenate([across, across_c], axis=1))
+    near_c, far_c = fetch(near, 0, 0, 1), fetch(far, 0, 0, 1)
+    near_y, far_y = fetch(near_y, 0, 1, 0), fetch(far_y, 0, 1, 0)
+    near_yc, far_yc = fetch(near_y, 0, 0, 1), fetch(far_y, 0, 0, 1)
+    partial = place(near, far, near_y, far_y, near_c, far_c, near_yc, far_yc).reshape(n_gy, -1, nx)
     pieces = lax.all_to_all(partial, "gy", 0, 0, tiled=True)
     columns = nv * nz * ny * n_gy
     gram = jnp.sum(pieces, axis=0) / jnp.float32(columns)

time: 140 us -> 147 us (1.050)
  the two profiles are of different devices: /device:TPU:14 before, /device:TPU:64 now
where the time goes in v2:
time: 147 us; the launch traced here: 146 us
  starting transfers between devices  57.6 us (39%)
  blocking collectives  44.5 us (30%)
  waiting for transfers between devices  20.3 us (14%)
  Pallas kernels  10.9 us (7%)
  matrix products  7.48 us (5%)
  local copies, waits for them, and re-layouts  3.4 us (2%)
    all_to_all x1, blocking collectives, on_device(): pieces = lax.all_to_all(partial, 'gy', 0, 0, tiled=True)  44.5 us
    ppermute x15, starting transfers between devices, fetch(): return lax.ppermute(value, 'gx', from_offset(dx, dy, dcore))  41.1 us
    ppermute x15, waiting for transfers between devices, fetch(): return lax.ppermute(value, 'gx', from_offset(dx, dy, dcore))  18.7 us
    dot_general x14, matrix products, against(): lax.dot_general(columns, rows, (((0,), (0,)), ((), ())), preferred_elemen...  7.48 us
    pallas_call x1, Pallas kernels, stencil(): pl.pallas_call(stencil_kernel, grid=(nv // per_step,), in_specs=[whole, w...  5.78 us
    ppermute x1, starting transfers between devices, on_device(): xright = lax.ppermute(xlo, 'gx', down(n_gx))  5.75 us
    ppermute x1, starting transfers between devices, on_device(): yabove = lax.ppermute(ylo, 'gy', down(n_gy))  4.55 us
    ppermute x1, starting transfers between devices, on_device(): ybelow = lax.ppermute(yhi, 'gy', up(n_gy))  4.27 us
  transfers between devices with their start and end apart: 19, of which 7 were waited for; matrix products, arithmetic and copies ran while one was open for 6% of the time, Pallas kernels for 0%

profile of v2, /device:TPU:64, one launch (start us, length us, event | category | flops | bytes accessed | tf_op | source)
XLA Modules:
  0.0 146.1 jit_solution(10843586146840474029)
XLA Ops:
  0.6 2.5 %pack_edges.1 = (f32[8,2,16,128]{3,2,1,0:T(8,128)}, f32[8,2,16,128]{3,2,1,0:T(8,128)}, f32[2,1536]{1,0:T(2,128)}, f32[2,1536]{1,0:T(2,128)}) custom-call(f32[8,12,16,128]{3,2,1,0:T(8,128)} %bitcast.51), custom_call_target="tpu_custom_call" | custom-call | tf_op jit(solution)/shard_map/pack_edges/pallas_call | solution.py:55
  3.1 4.3 %collective-permute-start = (f32[8,2,16,128]{3,2,1,0:T(8,128)}, f32[8,2,16,128]{3,2,1,0:T(8,128)S(1)}, u32[]{:S(2)}, u32[]{:S(2)}) collective-permute-start(f32[8,2,16,128]{3,2,1,0:T(8,128)} %get-tuple-element.10), channel_id=1, source_target_pairs={{0,1},{1,2},{2,3},{3,4},{4,5},{5,6},{6,7},{7,8},{8,9},{9,10},{10,1... | collective-permute-start | bytes 393224 | tf_op jit(solution)/shard_map/ppermute | solution.py:192
  7.4 4.5 %collective-permute-start.1 = (f32[8,2,16,128]{3,2,1,0:T(8,128)}, f32[8,2,16,128]{3,2,1,0:T(8,128)S(1)}, u32[]{:S(2)}, u32[]{:S(2)}) collective-permute-start(f32[8,2,16,128]{3,2,1,0:T(8,128)} %get-tuple-element.11), channel_id=1, source_target_pairs={{1,0},{2,1},{3,2},{4,3},{5,4},{6,5},{7,6},{8,7},{9,8},{10,9},{11,1... | collective-permute-start | bytes 393224 | tf_op jit(solution)/shard_map/ppermute | solution.py:193
  11.9 1.9 %collective-permute-start.2 = (f32[2,1536]{1,0:T(2,128)}, f32[2,1536]{1,0:T(2,128)S(1)}, u32[]{:S(2)}, u32[]{:S(2)}) collective-permute-start(f32[2,1536]{1,0:T(2,128)} %get-tuple-element.12), channel_id=1, source_target_pairs={{0,32},{32,64},{64,96},{96,128},{128,160},{160,192},{192,224},{224... | collective-permute-start | bytes 36872 | tf_op jit(solution)/shard_map/ppermute | solution.py:190
  13.9 5.8 %collective-permute-start.3 = (f32[2,1536]{1,0:T(2,128)}, f32[2,1536]{1,0:T(2,128)S(1)}, u32[]{:S(2)}, u32[]{:S(2)}) collective-permute-start(f32[2,1536]{1,0:T(2,128)} %get-tuple-element.13), channel_id=1, source_target_pairs={{32,0},{64,32},{96,64},{128,96},{160,128},{192,160},{224,192},{256... | collective-permute-start | bytes 36872 | tf_op jit(solution)/shard_map/ppermute | solution.py:191
  19.6 1.6 %collective-permute-done.3.xright_ref = f32[2,1536]{1,0:T(2,128)S(1)} collective-permute-done((f32[2,1536]{1,0:T(2,128)}, f32[2,1536]{1,0:T(2,128)S(1)}, u32[]{:S(2)}, u32[]{:S(2)}) %collective-permute-start.3) | collective-permute-done | bytes 12320 | tf_op jit(solution)/shard_map/ppermute | solution.py:191
  21.9 5.8 %stencil.1 = (f32[8,12,16,128]{3,2,1,0:T(8,128)}, f32[8,12,16,128]{3,2,1,0:T(8,128)}, f32[8,12,16,128]{3,2,1,0:T(8,128)}) custom-call(f32[8,12,16,128]{3,2,1,0:T(8,128)} %bitcast.52, f32[8,12,16,128]{3,2,1,0:T(8,128)} %bitcast.53, bf16[8,12,16,128]{3,2,1,0:T(8,128)(2,1)} %bitcast.54, f32[3,12,16,128]{3,2,1,0:T(8,128)} %bitcast.59, f32[12,16,128]{2,1,0:T(8,128)} %bitcast.60, ...), custom_call_target="tpu_custom_call" | custom-call | tf_op jit(solution)/shard_map/stencil/pallas_call | solution.py:122
  27.7 2.1 %collective-permute-start.11 = (f32[1536,128]{1,0:T(8,128)}, f32[1536,128]{1,0:T(8,128)S(1)}, u32[]{:S(2)}, u32[]{:S(2)}) collective-permute-start(f32[1536,128]{1,0:T(8,128)} %bitcast.40), channel_id=1, source_target_pairs={{64,0},{96,32},{0,64},{32,96},{192,128},{224,160},{128,192},{160,2... | collective-permute-start | bytes 2359304 | tf_op jit(solution)/shard_map/ppermute | solution.py:30
  29.8 1.9 %collective-permute-start.4 = (f32[1536,128]{1,0:T(8,128)}, f32[1536,128]{1,0:T(8,128)S(1)}, u32[]{:S(2)}, u32[]{:S(2)}) collective-permute-start(f32[1536,128]{1,0:T(8,128)} %bitcast.41), channel_id=1, source_target_pairs={{32,0},{0,32},{96,64},{64,96},{160,128},{128,160},{224,192},{192,2... | collective-permute-start | bytes 2359304 | tf_op jit(solution)/shard_map/ppermute | solution.py:30
  31.7 1.2 fusion.27
  32.9 2.3 %collective-permute-start.8 = (f32[768,128]{1,0:T(8,128)S(1)}, f32[768,128]{1,0:T(8,128)S(1)}, u32[]{:S(2)}, u32[]{:S(2)}) collective-permute-start(f32[768,128]{1,0:T(8,128)S(1)} %bitcast.57), channel_id=1, source_target_pairs={{384,0},{416,32},{448,64},{480,96},{0,128},{32,160},{64,192},{96,2... | collective-permute-start | bytes 1179656 | tf_op jit(solution)/shard_map/ppermute | solution.py:30
  35.2 6.0 %collective-permute-start.5 = (f32[768,128]{1,0:T(8,128)S(1)}, f32[768,128]{1,0:T(8,128)S(1)}, u32[]{:S(2)}, u32[]{:S(2)}) collective-permute-start(f32[768,128]{1,0:T(8,128)S(1)} %bitcast.55), channel_id=1, source_target_pairs={{128,0},{160,32},{192,64},{224,96},{256,128},{288,160},{320,192},{... | collective-permute-start | bytes 1179656 | tf_op jit(solution)/shard_map/ppermute | solution.py:30
  41.2 3.9 %collective-permute-start.6 = (f32[768,128]{1,0:T(8,128)S(1)}, f32[768,128]{1,0:T(8,128)S(1)}, u32[]{:S(2)}, u32[]{:S(2)}) collective-permute-start(f32[768,128]{1,0:T(8,128)S(1)} %bitcast.58), channel_id=1, source_target_pairs={{128,0},{160,32},{192,64},{224,96},{256,128},{288,160},{320,192},{... | collective-permute-start | bytes 1179656 | tf_op jit(solution)/shard_map/ppermute | solution.py:30
  45.2 3.4 %collective-permute-done.8 = f32[768,128]{1,0:T(8,128)S(1)} collective-permute-done((f32[768,128]{1,0:T(8,128)S(1)}, f32[768,128]{1,0:T(8,128)S(1)}, u32[]{:S(2)}, u32[]{:S(2)}) %collective-permute-start.8) | collective-permute-done | bytes 393248 | tf_op jit(solution)/shard_map/ppermute | solution.py:30
  48.6 1.9 %collective-permute-start.7 = (f32[768,128]{1,0:T(8,128)S(1)}, f32[768,128]{1,0:T(8,128)S(1)}, u32[]{:S(2)}, u32[]{:S(2)}) collective-permute-start(f32[768,128]{1,0:T(8,128)S(1)} %bitcast.56), channel_id=1, source_target_pairs={{384,0},{416,32},{448,64},{480,96},{0,128},{32,160},{64,192},{96,2... | collective-permute-start | bytes 1179656 | tf_op jit(solution)/shard_map/ppermute | solution.py:30
  50.7 3.8 %collective-permute-start.10 = (f32[768,128]{1,0:T(8,128)S(1)}, f32[768,128]{1,0:T(8,128)S(1)}, u32[]{:S(2)}, u32[]{:S(2)}) collective-permute-start(f32[768,128]{1,0:T(8,128)S(1)} %collective-permute-done.8), channel_id=1, source_target_pairs={{384,0},{416,32},{448,64},{480,96},{0,128},{32,160},{64,192},{96,2... | collective-permute-start | bytes 1179656 | tf_op jit(solution)/shard_map/ppermute | solution.py:30
  54.5 3.7 %collective-permute-start.9 = (f32[768,128]{1,0:T(8,128)S(1)}, f32[768,128]{1,0:T(8,128)S(1)}, u32[]{:S(2)}, u32[]{:S(2)}) collective-permute-start(f32[768,128]{1,0:T(8,128)S(1)} %collective-permute-done.5), channel_id=1, source_target_pairs={{128,0},{160,32},{192,64},{224,96},{256,128},{288,160},{320,192},{... | collective-permute-start | bytes 1179656 | tf_op jit(solution)/shard_map/ppermute | solution.py:30
  58.3 1.9 %collective-permute-start.12 = (f32[1536,128]{1,0:T(8,128)S(1)}, f32[1536,128]{1,0:T(8,128)S(1)}, u32[]{:S(2)}, u32[]{:S(2)}) collective-permute-start(f32[1536,128]{1,0:T(8,128)S(1)} %collective-permute-done.11), channel_id=1, source_target_pairs={{32,0},{0,32},{96,64},{64,96},{160,128},{128,160},{224,192},{192,2... | collective-permute-start | bytes 2359304 | tf_op jit(solution)/shard_map/ppermute | solution.py:30
  61.7 2.0 %collective-permute-done.7 = f32[768,128]{1,0:T(8,128)S(1)} collective-permute-done((f32[768,128]{1,0:T(8,128)S(1)}, f32[768,128]{1,0:T(8,128)S(1)}, u32[]{:S(2)}, u32[]{:S(2)}) %collective-permute-start.7) | collective-permute-done | bytes 393248 | tf_op jit(solution)/shard_map/ppermute | solution.py:30
  64.1 0.8 fusion.1
  65.0 1.9 %collective-permute-start.15 = (f32[3,128,256]{2,1,0:T(8,128)S(1)}, f32[3,128,256]{2,1,0:T(8,128)S(1)}, u32[]{:S(2)}, u32[]{:S(2)}) collective-permute-start(f32[3,128,256]{2,1,0:T(8,128)S(1)} %pad_maximum_fusion.4.near_ref), channel_id=1, source_target_pairs={{32,0},{0,32},{96,64},{64,96},{160,128},{128,160},{224,192},{192,2... | collective-permute-start | bytes 1179656 | tf_op jit(solution)/shard_map/ppermute | solution.py:30
  69.1 0.8 convolution_bitcast_fusion
  69.9 2.9 %collective-permute-start.13 = (f32[3,128,256]{2,1,0:T(8,128)S(1)}, f32[3,128,256]{2,1,0:T(8,128)S(1)}, u32[]{:S(2)}, u32[]{:S(2)}) collective-permute-start(f32[3,128,256]{2,1,0:T(8,128)S(1)} %pad_maximum_fusion.5), channel_id=1, source_target_pairs={{64,0},{96,32},{0,64},{32,96},{192,128},{224,160},{128,192},{160,2... | collective-permute-start | bytes 1179656 | tf_op jit(solution)/shard_map/ppermute | solution.py:30
  73.8 9.5 %collective-permute-done.13.near_y_ref = f32[3,128,256]{2,1,0:T(8,128)S(1)} collective-permute-done((f32[3,128,256]{2,1,0:T(8,128)S(1)}, f32[3,128,256]{2,1,0:T(8,128)S(1)}, u32[]{:S(2)}, u32[]{:S(2)}) %collective-permute-start.13) | collective-permute-done | bytes 393248 | tf_op jit(solution)/shard_map/ppermute | solution.py:30
  83.3 1.9 %collective-permute-start.17 = (f32[3,128,256]{2,1,0:T(8,128)S(1)}, f32[3,128,256]{2,1,0:T(8,128)S(1)}, u32[]{:S(2)}, u32[]{:S(2)}) collective-permute-start(f32[3,128,256]{2,1,0:T(8,128)S(1)} %collective-permute-done.13.near_y_ref), channel_id=1, source_target_pairs={{32,0},{0,32},{96,64},{64,96},{160,128},{128,160},{224,192},{192,2... | collective-permute-start | bytes 1179656 | tf_op jit(solution)/shard_map/ppermute | solution.py:30
  85.8 2.9 %collective-permute-start.14 = (f32[128,256]{1,0:T(8,128)S(1)}, f32[128,256]{1,0:T(8,128)S(1)}, u32[]{:S(2)}, u32[]{:S(2)}) collective-permute-start(f32[128,256]{1,0:T(8,128)S(1)} %convolution_add_fusion), channel_id=1, source_target_pairs={{64,0},{96,32},{0,64},{32,96},{192,128},{224,160},{128,192},{160,2... | collective-permute-start | bytes 393224 | tf_op jit(solution)/shard_map/ppermute | solution.py:30
  89.2 2.1 %collective-permute-start.16 = (f32[128,256]{1,0:T(8,128)S(1)}, f32[128,256]{1,0:T(8,128)S(1)}, u32[]{:S(2)}, u32[]{:S(2)}) collective-permute-start(f32[128,256]{1,0:T(8,128)S(1)} %convolution_add_fusion.3.far_ref), channel_id=1, source_target_pairs={{32,0},{0,32},{96,64},{64,96},{160,128},{128,160},{224,192},{192,2... | collective-permute-start | bytes 393224 | tf_op jit(solution)/shard_map/ppermute | solution.py:30
  91.3 2.3 %collective-permute-done.14.far_y_ref = f32[128,256]{1,0:T(8,128)S(1)} collective-permute-done((f32[128,256]{1,0:T(8,128)S(1)}, f32[128,256]{1,0:T(8,128)S(1)}, u32[]{:S(2)}, u32[]{:S(2)}) %collective-permute-start.14) | collective-permute-done | bytes 131104 | tf_op jit(solution)/shard_map/ppermute | solution.py:30
  93.6 1.9 %collective-permute-start.18 = (f32[128,256]{1,0:T(8,128)S(1)}, f32[128,256]{1,0:T(8,128)S(1)}, u32[]{:S(2)}, u32[]{:S(2)}) collective-permute-start(f32[128,256]{1,0:T(8,128)S(1)} %collective-permute-done.14.far_y_ref), channel_id=1, source_target_pairs={{32,0},{0,32},{96,64},{64,96},{160,128},{128,160},{224,192},{192,2... | collective-permute-start | bytes 393224 | tf_op jit(solution)/shard_map/ppermute | solution.py:30
  95.5 1.3 collective-permute-done.18.far_yc_ref
  98.2 2.6 %place.1 = f32[16,128,128]{2,1,0:T(8,128)} custom-call(f32[3,128,256]{2,1,0:T(8,128)} %copy-done.1, f32[128,256]{1,0:T(8,128)} %copy-done.2, f32[3,128,256]{2,1,0:T(8,128)} %copy-done.4, f32[128,256]{1,0:T(8,128)} %copy-done.6, f32[3,128,256]{2,1,0:T(8,128)} %copy-done.3, f32[128,256]{1,0:T(8,128)} %copy-done.9, f32[3,128,256]{2,1,0:T(8,128)} %copy-done.5, ...), custom_call_target="tpu_custom_call" | custom-call | tf_op jit(solution)/shard_map/place/pallas_call | solution.py:167
  100.8 44.5 %all_to_all.5 = f32[32,64,128]{2,1,0:T(8,128)S(1)} all-to-all(f32[32,64,128]{2,1,0:T(8,128)} %bitcast.50), channel_id=1, replica_groups=mesh['gx'=16,'gy'=32] {'gy'}, dimensions={0} | all-to-all | bytes 2097152 | tf_op jit(solution)/shard_map/all_to_all | solution.py:224
  (57 shorter events, 9.1 us)
Async XLA Ops:
  3.1 18.1 %collective-permute-start = (f32[8,2,16,128]{3,2,1,0:T(8,128)}, f32[8,2,16,128]{3,2,1,0:T(8,128)S(1)}, u32[]{:S(2)}, u32[]{:S(2)}) collective-permute-start(f32[8,2,16,128]{3,2,1,0:T(8,128)} %get-tuple-element.10), channel_id=1, source_target_pairs={{0,1},{1,2},{2,3},{3,4},{4,5},{5,6},{6,7},{7,8},{8,9},{9,10},{10,1... | collective-permute-start | bytes 393224 | tf_op jit(solution)/shard_map/ppermute | solution.py:192
  7.4 13.8 %collective-permute-start.1 = (f32[8,2,16,128]{3,2,1,0:T(8,128)}, f32[8,2,16,128]{3,2,1,0:T(8,128)S(1)}, u32[]{:S(2)}, u32[]{:S(2)}) collective-permute-start(f32[8,2,16,128]{3,2,1,0:T(8,128)} %get-tuple-element.11), channel_id=1, source_target_pairs={{1,0},{2,1},{3,2},{4,3},{5,4},{6,5},{7,6},{8,7},{9,8},{10,9},{11,1... | collective-permute-start | bytes 393224 | tf_op jit(solution)/shard_map/ppermute | solution.py:193
  11.9 7.7 %collective-permute-start.2 = (f32[2,1536]{1,0:T(2,128)}, f32[2,1536]{1,0:T(2,128)S(1)}, u32[]{:S(2)}, u32[]{:S(2)}) collective-permute-start(f32[2,1536]{1,0:T(2,128)} %get-tuple-element.12), channel_id=1, source_target_pairs={{0,32},{32,64},{64,96},{96,128},{128,160},{160,192},{192,224},{224... | collective-permute-start | bytes 36872 | tf_op jit(solution)/shard_map/ppermute | solution.py:190
  13.9 7.4 %collective-permute-start.3 = (f32[2,1536]{1,0:T(2,128)}, f32[2,1536]{1,0:T(2,128)S(1)}, u32[]{:S(2)}, u32[]{:S(2)}) collective-permute-start(f32[2,1536]{1,0:T(2,128)} %get-tuple-element.13), channel_id=1, source_target_pairs={{32,0},{64,32},{96,64},{128,96},{160,128},{192,160},{224,192},{256... | collective-permute-start | bytes 36872 | tf_op jit(solution)/shard_map/ppermute | solution.py:191
  19.6 1.6 %copy-start.11 = (f32[2,1536]{1,0:T(2,128)}, f32[2,1536]{1,0:T(2,128)S(1)}, u32[]{:S(2)}) copy-start(f32[2,1536]{1,0:T(2,128)S(1)} %collective-permute-done.2.xleft_ref) | copy-start | bytes 36868
  21.2 0.6 copy-start.12
  21.2 0.7 copy-start.7
  21.2 0.7 copy-start.8
  27.7 32.5 %copy-start = (f32[8,12,16,128]{3,2,1,0:T(8,128)S(1)}, f32[8,12,16,128]{3,2,1,0:T(8,128)}, u32[]{:S(2)}) copy-start(f32[8,12,16,128]{3,2,1,0:T(8,128)} %get-tuple-element.16) | copy-start | bytes 2359300
  27.7 26.8 %collective-permute-start.11 = (f32[1536,128]{1,0:T(8,128)}, f32[1536,128]{1,0:T(8,128)S(1)}, u32[]{:S(2)}, u32[]{:S(2)}) collective-permute-start(f32[1536,128]{1,0:T(8,128)} %bitcast.40), channel_id=1, source_target_pairs={{64,0},{96,32},{0,64},{32,96},{192,128},{224,160},{128,192},{160,2... | collective-permute-start | bytes 2359304 | tf_op jit(solution)/shard_map/ppermute | solution.py:30
  29.8 28.5 %collective-permute-start.4 = (f32[1536,128]{1,0:T(8,128)}, f32[1536,128]{1,0:T(8,128)S(1)}, u32[]{:S(2)}, u32[]{:S(2)}) collective-permute-start(f32[1536,128]{1,0:T(8,128)} %bitcast.41), channel_id=1, source_target_pairs={{32,0},{0,32},{96,64},{64,96},{160,128},{128,160},{224,192},{192,2... | collective-permute-start | bytes 2359304 | tf_op jit(solution)/shard_map/ppermute | solution.py:30
  32.9 15.7 %collective-permute-start.8 = (f32[768,128]{1,0:T(8,128)S(1)}, f32[768,128]{1,0:T(8,128)S(1)}, u32[]{:S(2)}, u32[]{:S(2)}) collective-permute-start(f32[768,128]{1,0:T(8,128)S(1)} %bitcast.57), channel_id=1, source_target_pairs={{384,0},{416,32},{448,64},{480,96},{0,128},{32,160},{64,192},{96,2... | collective-permute-start | bytes 1179656 | tf_op jit(solution)/shard_map/ppermute | solution.py:30
  35.2 15.5 %collective-permute-start.5 = (f32[768,128]{1,0:T(8,128)S(1)}, f32[768,128]{1,0:T(8,128)S(1)}, u32[]{:S(2)}, u32[]{:S(2)}) collective-permute-start(f32[768,128]{1,0:T(8,128)S(1)} %bitcast.55), channel_id=1, source_target_pairs={{128,0},{160,32},{192,64},{224,96},{256,128},{288,160},{320,192},{... | collective-permute-start | bytes 1179656 | tf_op jit(solution)/shard_map/ppermute | solution.py:30
  41.2 19.5 %collective-permute-start.6 = (f32[768,128]{1,0:T(8,128)S(1)}, f32[768,128]{1,0:T(8,128)S(1)}, u32[]{:S(2)}, u32[]{:S(2)}) collective-permute-start(f32[768,128]{1,0:T(8,128)S(1)} %bitcast.58), channel_id=1, source_target_pairs={{128,0},{160,32},{192,64},{224,96},{256,128},{288,160},{320,192},{... | collective-permute-start | bytes 1179656 | tf_op jit(solution)/shard_map/ppermute | solution.py:30
  48.6 15.1 %collective-permute-start.7 = (f32[768,128]{1,0:T(8,128)S(1)}, f32[768,128]{1,0:T(8,128)S(1)}, u32[]{:S(2)}, u32[]{:S(2)}) collective-permute-start(f32[768,128]{1,0:T(8,128)S(1)} %bitcast.56), channel_id=1, source_target_pairs={{384,0},{416,32},{448,64},{480,96},{0,128},{32,160},{64,192},{96,2... | collective-permute-start | bytes 1179656 | tf_op jit(solution)/shard_map/ppermute | solution.py:30
  50.7 22.1 %collective-permute-start.10 = (f32[768,128]{1,0:T(8,128)S(1)}, f32[768,128]{1,0:T(8,128)S(1)}, u32[]{:S(2)}, u32[]{:S(2)}) collective-permute-start(f32[768,128]{1,0:T(8,128)S(1)} %collective-permute-done.8), channel_id=1, source_target_pairs={{384,0},{416,32},{448,64},{480,96},{0,128},{32,160},{64,192},{96,2... | collective-permute-start | bytes 1179656 | tf_op jit(solution)/shard_map/ppermute | solution.py:30
  54.5 30.8 %collective-permute-start.9 = (f32[768,128]{1,0:T(8,128)S(1)}, f32[768,128]{1,0:T(8,128)S(1)}, u32[]{:S(2)}, u32[]{:S(2)}) collective-permute-start(f32[768,128]{1,0:T(8,128)S(1)} %collective-permute-done.5), channel_id=1, source_target_pairs={{128,0},{160,32},{192,64},{224,96},{256,128},{288,160},{320,192},{... | collective-permute-start | bytes 1179656 | tf_op jit(solution)/shard_map/ppermute | solution.py:30
  58.3 8.8 %collective-permute-start.12 = (f32[1536,128]{1,0:T(8,128)S(1)}, f32[1536,128]{1,0:T(8,128)S(1)}, u32[]{:S(2)}, u32[]{:S(2)}) collective-permute-start(f32[1536,128]{1,0:T(8,128)S(1)} %collective-permute-done.11), channel_id=1, source_target_pairs={{32,0},{0,32},{96,64},{64,96},{160,128},{128,160},{224,192},{192,2... | collective-permute-start | bytes 2359304 | tf_op jit(solution)/shard_map/ppermute | solution.py:30
  65.0 2.1 %copy-start.1 = (f32[3,128,256]{2,1,0:T(8,128)}, f32[3,128,256]{2,1,0:T(8,128)S(1)}, u32[]{:S(2)}) copy-start(f32[3,128,256]{2,1,0:T(8,128)S(1)} %pad_maximum_fusion.4.near_ref) | copy-start | bytes 1179652
  65.0 30.5 %collective-permute-start.15 = (f32[3,128,256]{2,1,0:T(8,128)S(1)}, f32[3,128,256]{2,1,0:T(8,128)S(1)}, u32[]{:S(2)}, u32[]{:S(2)}) collective-permute-start(f32[3,128,256]{2,1,0:T(8,128)S(1)} %pad_maximum_fusion.4.near_ref), channel_id=1, source_target_pairs={{32,0},{0,32},{96,64},{64,96},{160,128},{128,160},{224,192},{192,2... | collective-permute-start | bytes 1179656 | tf_op jit(solution)/shard_map/ppermute | solution.py:30
  69.9 13.4 %collective-permute-start.13 = (f32[3,128,256]{2,1,0:T(8,128)S(1)}, f32[3,128,256]{2,1,0:T(8,128)S(1)}, u32[]{:S(2)}, u32[]{:S(2)}) collective-permute-start(f32[3,128,256]{2,1,0:T(8,128)S(1)} %pad_maximum_fusion.5), channel_id=1, source_target_pairs={{64,0},{96,32},{0,64},{32,96},{192,128},{224,160},{128,192},{160,2... | collective-permute-start | bytes 1179656 | tf_op jit(solution)/shard_map/ppermute | solution.py:30
  83.3 5.8 %copy-start.4 = (f32[3,128,256]{2,1,0:T(8,128)}, f32[3,128,256]{2,1,0:T(8,128)S(1)}, u32[]{:S(2)}) copy-start(f32[3,128,256]{2,1,0:T(8,128)S(1)} %collective-permute-done.13.near_y_ref) | copy-start | bytes 1179652
  83.3 13.5 %collective-permute-start.17 = (f32[3,128,256]{2,1,0:T(8,128)S(1)}, f32[3,128,256]{2,1,0:T(8,128)S(1)}, u32[]{:S(2)}, u32[]{:S(2)}) collective-permute-start(f32[3,128,256]{2,1,0:T(8,128)S(1)} %collective-permute-done.13.near_y_ref), channel_id=1, source_target_pairs={{32,0},{0,32},{96,64},{64,96},{160,128},{128,160},{224,192},{192,2... | collective-permute-start | bytes 1179656 | tf_op jit(solution)/shard_map/ppermute | solution.py:30
  85.8 7.8 %collective-permute-start.14 = (f32[128,256]{1,0:T(8,128)S(1)}, f32[128,256]{1,0:T(8,128)S(1)}, u32[]{:S(2)}, u32[]{:S(2)}) collective-permute-start(f32[128,256]{1,0:T(8,128)S(1)} %convolution_add_fusion), channel_id=1, source_target_pairs={{64,0},{96,32},{0,64},{32,96},{192,128},{224,160},{128,192},{160,2... | collective-permute-start | bytes 393224 | tf_op jit(solution)/shard_map/ppermute | solution.py:30
  89.1 7.6 %copy-start.2 = (f32[128,256]{1,0:T(8,128)}, f32[128,256]{1,0:T(8,128)S(1)}, u32[]{:S(2)}) copy-start(f32[128,256]{1,0:T(8,128)S(1)} %convolution_add_fusion.3.far_ref) | copy-start | bytes 393220
  89.2 6.3 %collective-permute-start.16 = (f32[128,256]{1,0:T(8,128)S(1)}, f32[128,256]{1,0:T(8,128)S(1)}, u32[]{:S(2)}, u32[]{:S(2)}) collective-permute-start(f32[128,256]{1,0:T(8,128)S(1)} %convolution_add_fusion.3.far_ref), channel_id=1, source_target_pairs={{32,0},{0,32},{96,64},{64,96},{160,128},{128,160},{224,192},{192,2... | collective-permute-start | bytes 393224 | tf_op jit(solution)/shard_map/ppermute | solution.py:30
  93.6 3.2 %copy-start.6 = (f32[128,256]{1,0:T(8,128)}, f32[128,256]{1,0:T(8,128)S(1)}, u32[]{:S(2)}) copy-start(f32[128,256]{1,0:T(8,128)S(1)} %collective-permute-done.14.far_y_ref) | copy-start | bytes 393220
  93.6 3.2 %collective-permute-start.18 = (f32[128,256]{1,0:T(8,128)S(1)}, f32[128,256]{1,0:T(8,128)S(1)}, u32[]{:S(2)}, u32[]{:S(2)}) collective-permute-start(f32[128,256]{1,0:T(8,128)S(1)} %collective-permute-done.14.far_y_ref), channel_id=1, source_target_pairs={{32,0},{0,32},{96,64},{64,96},{160,128},{128,160},{224,192},{192,2... | collective-permute-start | bytes 393224 | tf_op jit(solution)/shard_map/ppermute | solution.py:30
  95.5 1.3 copy-start.9
  95.5 1.3 copy-start.3
  96.8 0.7 copy-start.10
  97.4 0.8 copy-start.5

commit v3 on v2

--- a/solution.py
+++ b/solution.py
@@ -4,6 +4,7 @@
 from jax.experimental import pallas as pl
 from jax.experimental.pallas import tpu as pltpu
 from jax.sharding import PartitionSpec as P
+
 
 step_size = 0.3
 carry_weight = -5.0 / 9.0
@@ -112,7 +113,7 @@
             chg_ref[v, y] = new_state - c_ref[v, y].astype(jnp.float32)
 
 
-def stencil(s, r, c, vel, dif, ybelow, yabove, xleft, xright, per_step=2):
+def stencil(s, r, c, vel, dif, ybelow, yabove, xleft, xright, per_step=4):
     nv, ny, nz, nx = s.shape
     whole = pl.BlockSpec((per_step, ny, nz, nx), lambda i: (i, 0, 0, 0))
     side = pl.BlockSpec((per_step, 2, nz, nx), lambda i: (i, 0, 0, 0))
@@ -135,30 +136,26 @@
     )(s, r, c, vel, dif, ybelow, yabove, xleft, xright)
 
 
-def place_kernel(near_ref, far_ref, near_y_ref, far_y_ref, near_c_ref, far_c_ref, near_yc_ref, far_yc_ref, out_ref):
+def place_kernel(*refs):
+    *parts, out_ref = refs
     gx = lax.axis_index("gx")
     core = lax.rem(gx, CORES)
     y = lax.rem(lax.div(gx, CORES), NY_LO)
     x = lax.div(gx, CORES * NY_LO)
-    nx = out_ref.shape[-1]
-    sources = (
-        (0, 0, near_ref, far_ref),
-        (1, 0, near_y_ref, far_y_ref),
-        (0, 1, near_c_ref, far_c_ref),
-        (1, 1, near_yc_ref, far_yc_ref),
-    )
-    for dy, dcore, near, far in sources:
-        lanes = slice(dcore * nx, dcore * nx + nx)
-        for dx in range(NX_CHIPS):
-            at = (
+    for n, (dx, dcore) in enumerate(ORDER):
+        part, at = next((p, n - first) for p, first in zip(parts[::2], PARTS) if first <= n < first + p.shape[0])
+        other = parts[1::2][[p is part for p in parts[::2]].index(True)]
+        for dy, value in ((0, part[at]), (1, other[at])):
+            place_at = (
                 lax.rem(x + dx, NX_CHIPS) * (NY_LO * CORES)
                 + lax.rem(y + dy, NY_LO) * CORES
                 + lax.rem(core + dcore, CORES)
             )
-            out_ref[at] = far[:, lanes] if dx == 2 else near[NEAR.index(dx), :, lanes]
-
-
-NEAR = (0, 1, 3)
+            out_ref[place_at] = value
+
+
+ORDER = ((0, 0), (0, 1), (1, 0), (3, 0), (1, 1), (3, 1), (2, 0), (2, 1))
+PARTS = (0, 4)
 
 
 def place(*parts):
@@ -179,7 +176,7 @@
     )
 
 
-def on_device(state, register, checkpoint, velocity, diffusivity):
+def section(state, register, checkpoint, velocity, diffusivity):
     nv, nz, ny, nx = state.shape
     to_yzx = lambda a: jnp.swapaxes(a, -3, -2)
     s, r, c = to_yzx(state), to_yzx(register), to_yzx(checkpoint)
@@ -197,30 +194,30 @@
     depth = nv * ny * nz
     half = depth // 2
     mine = change.reshape(depth, nx)
-    front, back = mine[:half], mine[half:]
-    right0 = fetch(front, 1, 0, 0)
-    left1 = fetch(back, -1, 0, 0)
+    right = fetch(mine, 1, 0, 0)
+    left = fetch(mine, -1, 0, 0)
     across = fetch(mine, 0, 1, 0)
     mine_c = fetch(mine, 0, 0, 1)
-    right1 = fetch(back, 1, 0, 0)
-    left0 = fetch(front, -1, 0, 0)
-    far0 = fetch(right0, 1, 0, 0)
-    far1 = fetch(left1, -1, 0, 0)
-    across_c = fetch(across, 0, 0, 1)
-
-    def by_halves(a, b, rows):
+    far0 = fetch(right[:half], 1, 0, 0)
+    far1 = fetch(left[half:], -1, 0, 0)
+    right_c = fetch(right, 0, 0, 1)
+    left_c = fetch(left, 0, 0, 1)
+    far0_c = fetch(far0, 0, 0, 1)
+    far1_c = fetch(far1, 0, 0, 1)
+
+    def split(a, b, rows):
         return against(a, rows[:half]) + against(b, rows[half:])
 
-    def products(rows):
-        near = jnp.stack([against(mine, rows), by_halves(right0, right1, rows), by_halves(left0, left1, rows)])
-        return near, by_halves(far0, far1, rows)
-
-    near, far = products(jnp.concatenate([mine, mine_c], axis=1))
-    near_y, far_y = products(jnp.concatenate([across, across_c], axis=1))
-    near_c, far_c = fetch(near, 0, 0, 1), fetch(far, 0, 0, 1)
-    near_y, far_y = fetch(near_y, 0, 1, 0), fetch(far_y, 0, 1, 0)
-    near_yc, far_yc = fetch(near_y, 0, 0, 1), fetch(far_y, 0, 0, 1)
-    partial = place(near, far, near_y, far_y, near_c, far_c, near_yc, far_yc).reshape(n_gy, -1, nx)
+    def first(rows):
+        return jnp.stack([against(a, rows) for a in (mine, mine_c, right, left)])
+
+    def second(rows):
+        wide = [against(a, rows) for a in (right_c, left_c)]
+        return jnp.stack(wide + [split(far0, far1, rows), split(far0_c, far1_c, rows)])
+
+    first_y = fetch(first(across), 0, 1, 0)
+    second_y = fetch(second(across), 0, 1, 0)
+    partial = place(first(mine), first_y, second(mine), second_y).reshape(n_gy, -1, nx)
     pieces = lax.all_to_all(partial, "gy", 0, 0, tiled=True)
     columns = nv * nz * ny * n_gy
     gram = jnp.sum(pieces, axis=0) / jnp.float32(columns)
@@ -236,6 +233,4 @@
         P(None, "gy", "gx"),
     )
     out_specs = (P(None, None, "gy", "gx"), P(None, None, "gy", "gx"), P("gx", "gy"))
-    return jax.shard_map(
-        on_device, mesh=mesh, in_specs=in_specs, out_specs=out_specs, check_vma=False
-    )
+    return jax.shard_map(section, mesh=mesh, in_specs=in_specs, out_specs=out_specs, check_vma=False)

time: 147 us -> 137 us (0.932)
  the two profiles are of different devices: /device:TPU:64 before, /device:TPU:14 now
where the time goes in v3:
time: 137 us
  starting transfers between devices  54.8 us (40%)
  blocking collectives  38.8 us (28%)
  matrix products  14.8 us (11%)
  waiting for transfers between devices  14 us (10%)
  Pallas kernels  9.7 us (7%)
  other arithmetic  2.16 us (2%)
  local copies, waits for them, and re-layouts  1.48 us (1%)
    all_to_all x1, blocking collectives, section(): pieces = lax.all_to_all(partial, 'gy', 0, 0, tiled=True)  38.8 us
    ppermute x12, starting transfers between devices, fetch(): return lax.ppermute(value, 'gx', from_offset(dx, dy, dcore))  33.6 us
    dot_general x20, matrix products, against(): lax.dot_general(columns, rows, (((0,), (0,)), ((), ())), preferred_elemen...  14.8 us
    ppermute x12, waiting for transfers between devices, fetch(): return lax.ppermute(value, 'gx', from_offset(dx, dy, dcore))  12.4 us
    ppermute x1, starting transfers between devices, section(): yabove = lax.ppermute(ylo, 'gy', down(n_gy))  11.4 us
    pallas_call x1, Pallas kernels, stencil(): pl.pallas_call(stencil_kernel, grid=(nv // per_step,), in_specs=[whole, w...  4.96 us
    ppermute x1, starting transfers between devices, section(): ybelow = lax.ppermute(yhi, 'gy', up(n_gy))  4.27 us
    ppermute x1, starting transfers between devices, section(): xright = lax.ppermute(xlo, 'gx', down(n_gx))  3.64 us
  transfers between devices with their start and end apart: 16, of which 5 were waited for; matrix products, arithmetic and copies ran while one was open for 12% of the time, Pallas kernels for 0%

profile of v3, /device:TPU:14, one launch (start us, length us, event | category | flops | bytes accessed | tf_op | source)
XLA Modules:
  0.0 136.6 jit_solution(1394396338212289607)
XLA Ops:
  0.6 2.5 %pack_edges.1 = (f32[8,2,16,128]{3,2,1,0:T(8,128)}, f32[8,2,16,128]{3,2,1,0:T(8,128)}, f32[2,1536]{1,0:T(2,128)}, f32[2,1536]{1,0:T(2,128)}) custom-call(f32[8,12,16,128]{3,2,1,0:T(8,128)} %bitcast.100), custom_call_target="tpu_custom_call" | custom-call | tf_op jit(solution)/shard_map/pack_edges/pallas_call | solution.py:56
  3.1 4.3 %collective-permute-start = (f32[8,2,16,128]{3,2,1,0:T(8,128)}, f32[8,2,16,128]{3,2,1,0:T(8,128)S(1)}, u32[]{:S(2)}, u32[]{:S(2)}) collective-permute-start(f32[8,2,16,128]{3,2,1,0:T(8,128)} %get-tuple-element.10), channel_id=1, source_target_pairs={{0,1},{1,2},{2,3},{3,4},{4,5},{5,6},{6,7},{7,8},{8,9},{9,10},{10,1... | collective-permute-start | bytes 393224 | tf_op jit(solution)/shard_map/ppermute | solution.py:189
  7.4 11.4 %collective-permute-start.1 = (f32[8,2,16,128]{3,2,1,0:T(8,128)}, f32[8,2,16,128]{3,2,1,0:T(8,128)S(1)}, u32[]{:S(2)}, u32[]{:S(2)}) collective-permute-start(f32[8,2,16,128]{3,2,1,0:T(8,128)} %get-tuple-element.11), channel_id=1, source_target_pairs={{1,0},{2,1},{3,2},{4,3},{5,4},{6,5},{7,6},{8,7},{9,8},{10,9},{11,1... | collective-permute-start | bytes 393224 | tf_op jit(solution)/shard_map/ppermute | solution.py:190
  18.8 1.9 %collective-permute-start.2 = (f32[2,1536]{1,0:T(2,128)}, f32[2,1536]{1,0:T(2,128)S(1)}, u32[]{:S(2)}, u32[]{:S(2)}) collective-permute-start(f32[2,1536]{1,0:T(2,128)} %get-tuple-element.12), channel_id=1, source_target_pairs={{0,32},{32,64},{64,96},{96,128},{128,160},{160,192},{192,224},{224... | collective-permute-start | bytes 36872 | tf_op jit(solution)/shard_map/ppermute | solution.py:187
  20.7 3.6 %collective-permute-start.3 = (f32[2,1536]{1,0:T(2,128)}, f32[2,1536]{1,0:T(2,128)S(1)}, u32[]{:S(2)}, u32[]{:S(2)}) collective-permute-start(f32[2,1536]{1,0:T(2,128)} %get-tuple-element.13), channel_id=1, source_target_pairs={{32,0},{64,32},{96,64},{128,96},{160,128},{192,160},{224,192},{256... | collective-permute-start | bytes 36872 | tf_op jit(solution)/shard_map/ppermute | solution.py:188
  24.4 1.6 %collective-permute-done.3.xright_ref = f32[2,1536]{1,0:T(2,128)S(1)} collective-permute-done((f32[2,1536]{1,0:T(2,128)}, f32[2,1536]{1,0:T(2,128)S(1)}, u32[]{:S(2)}, u32[]{:S(2)}) %collective-permute-start.3) | collective-permute-done | bytes 12320 | tf_op jit(solution)/shard_map/ppermute | solution.py:188
  26.6 5.0 %stencil.1 = (f32[8,12,16,128]{3,2,1,0:T(8,128)}, f32[8,12,16,128]{3,2,1,0:T(8,128)}, f32[8,12,16,128]{3,2,1,0:T(8,128)}) custom-call(f32[8,12,16,128]{3,2,1,0:T(8,128)} %bitcast.101, f32[8,12,16,128]{3,2,1,0:T(8,128)} %bitcast.102, bf16[8,12,16,128]{3,2,1,0:T(8,128)(2,1)} %bitcast.103, f32[3,12,16,128]{3,2,1,0:T(8,128)} %bitcast.104, ...), custom_call_target="tpu_custom_call" | custom-call | tf_op jit(solution)/shard_map/stencil/pallas_call | solution.py:123
  31.6 2.5 %collective-permute-start.6 = (f32[1536,128]{1,0:T(8,128)}, f32[1536,128]{1,0:T(8,128)S(1)}, u32[]{:S(2)}, u32[]{:S(2)}) collective-permute-start(f32[1536,128]{1,0:T(8,128)} %bitcast.85), channel_id=1, source_target_pairs={{384,0},{416,32},{448,64},{480,96},{0,128},{32,160},{64,192},{96,2... | collective-permute-start | bytes 2359304 | tf_op jit(solution)/shard_map/ppermute | solution.py:31
  34.1 3.5 %collective-permute-start.5 = (f32[1536,128]{1,0:T(8,128)}, f32[1536,128]{1,0:T(8,128)S(1)}, u32[]{:S(2)}, u32[]{:S(2)}) collective-permute-start(f32[1536,128]{1,0:T(8,128)} %bitcast.86), channel_id=1, source_target_pairs={{128,0},{160,32},{192,64},{224,96},{256,128},{288,160},{320,192},{... | collective-permute-start | bytes 2359304 | tf_op jit(solution)/shard_map/ppermute | solution.py:31
  37.6 4.2 %collective-permute-start.7 = (f32[1536,128]{1,0:T(8,128)}, f32[1536,128]{1,0:T(8,128)S(1)}, u32[]{:S(2)}, u32[]{:S(2)}) collective-permute-start(f32[1536,128]{1,0:T(8,128)} %bitcast.87), channel_id=1, source_target_pairs={{64,0},{96,32},{0,64},{32,96},{192,128},{224,160},{128,192},{160,2... | collective-permute-start | bytes 2359304 | tf_op jit(solution)/shard_map/ppermute | solution.py:31
  41.7 2.6 %collective-permute-start.4 = (f32[1536,128]{1,0:T(8,128)}, f32[1536,128]{1,0:T(8,128)S(1)}, u32[]{:S(2)}, u32[]{:S(2)}) collective-permute-start(f32[1536,128]{1,0:T(8,128)} %bitcast.88), channel_id=1, source_target_pairs={{32,0},{0,32},{96,64},{64,96},{160,128},{128,160},{224,192},{192,2... | collective-permute-start | bytes 2359304 | tf_op jit(solution)/shard_map/ppermute | solution.py:31
  44.3 2.2 %convolution_bitcast_fusion.11 = f32[1,128,128]{2,1,0:T(8,128)S(1)} fusion(f32[8,12,16,128]{3,2,1,0:T(8,128)} %get-tuple-element.16), kind=kOutput, calls=%fused_computation.11 | convolution fusion | flops 150994944 | bytes 851968 | tf_op jit(solution)/shard_map/dot_general | solution.py:174
  46.6 5.2 %collective-permute-done.6 = f32[1536,128]{1,0:T(8,128)S(1)} collective-permute-done((f32[1536,128]{1,0:T(8,128)}, f32[1536,128]{1,0:T(8,128)S(1)}, u32[]{:S(2)}, u32[]{:S(2)}) %collective-permute-start.6) | collective-permute-done | bytes 786464 | tf_op jit(solution)/shard_map/ppermute | solution.py:31
  51.8 3.8 %collective-permute-start.12 = (f32[768,128]{1,0:T(8,128)S(1)}, f32[768,128]{1,0:T(8,128)S(1)}, u32[]{:S(2)}, u32[]{:S(2)}) collective-permute-start(f32[768,128]{1,0:T(8,128)S(1)} %slice.37), channel_id=1, source_target_pairs={{384,0},{416,32},{448,64},{480,96},{0,128},{32,160},{64,192},{96,2... | collective-permute-start | bytes 1179656 | tf_op jit(solution)/shard_map/ppermute | solution.py:31
  55.9 2.1 %collective-permute-start.11 = (f32[768,128]{1,0:T(8,128)S(1)}, f32[768,128]{1,0:T(8,128)S(1)}, u32[]{:S(2)}, u32[]{:S(2)}) collective-permute-start(f32[768,128]{1,0:T(8,128)S(1)} %slice.36), channel_id=1, source_target_pairs={{128,0},{160,32},{192,64},{224,96},{256,128},{288,160},{320,192},{... | collective-permute-start | bytes 1179656 | tf_op jit(solution)/shard_map/ppermute | solution.py:31
  57.9 2.0 %collective-permute-done.7 = f32[1536,128]{1,0:T(8,128)S(1)} collective-permute-done((f32[1536,128]{1,0:T(8,128)}, f32[1536,128]{1,0:T(8,128)S(1)}, u32[]{:S(2)}, u32[]{:S(2)}) %collective-permute-start.7) | collective-permute-done | bytes 786464 | tf_op jit(solution)/shard_map/ppermute | solution.py:31
  60.7 0.8 convolution_bitcast_fusion.4
  63.2 4.3 %collective-permute-start.8 = (f32[4,128,128]{2,1,0:T(8,128)S(1)}, f32[4,128,128]{2,1,0:T(8,128)S(1)}, u32[]{:S(2)}, u32[]{:S(2)}) collective-permute-start(f32[4,128,128]{2,1,0:T(8,128)S(1)} %pad_maximum_fusion.1), channel_id=1, source_target_pairs={{64,0},{96,32},{0,64},{32,96},{192,128},{224,160},{128,192},{160,2... | collective-permute-start | bytes 786440 | tf_op jit(solution)/shard_map/ppermute | solution.py:31
  67.5 0.8 convolution_bitcast_fusion.8
  68.3 1.9 %collective-permute-start.10 = (f32[1536,128]{1,0:T(8,128)S(1)}, f32[1536,128]{1,0:T(8,128)S(1)}, u32[]{:S(2)}, u32[]{:S(2)}) collective-permute-start(f32[1536,128]{1,0:T(8,128)S(1)} %collective-permute-done.6), channel_id=1, source_target_pairs={{32,0},{0,32},{96,64},{64,96},{160,128},{128,160},{224,192},{192,2... | collective-permute-start | bytes 2359304 | tf_op jit(solution)/shard_map/ppermute | solution.py:31
  70.2 0.8 convolution_bitcast_fusion.9
  71.0 0.8 convolution_bitcast_fusion.10
  72.5 2.4 %collective-permute-start.9 = (f32[1536,128]{1,0:T(8,128)S(1)}, f32[1536,128]{1,0:T(8,128)S(1)}, u32[]{:S(2)}, u32[]{:S(2)}) collective-permute-start(f32[1536,128]{1,0:T(8,128)S(1)} %collective-permute-done.5), channel_id=1, source_target_pairs={{32,0},{0,32},{96,64},{64,96},{160,128},{128,160},{224,192},{192,2... | collective-permute-start | bytes 2359304 | tf_op jit(solution)/shard_map/ppermute | solution.py:31
  75.4 1.9 %collective-permute-start.14 = (f32[768,128]{1,0:T(8,128)S(1)}, f32[768,128]{1,0:T(8,128)S(1)}, u32[]{:S(2)}, u32[]{:S(2)}) collective-permute-start(f32[768,128]{1,0:T(8,128)S(1)} %collective-permute-done.12), channel_id=1, source_target_pairs={{32,0},{0,32},{96,64},{64,96},{160,128},{128,160},{224,192},{192,2... | collective-permute-start | bytes 1179656 | tf_op jit(solution)/shard_map/ppermute | solution.py:31
  77.3 2.6 %collective-permute-start.13 = (f32[768,128]{1,0:T(8,128)S(1)}, f32[768,128]{1,0:T(8,128)S(1)}, u32[]{:S(2)}, u32[]{:S(2)}) collective-permute-start(f32[768,128]{1,0:T(8,128)S(1)} %collective-permute-done.11), channel_id=1, source_target_pairs={{32,0},{0,32},{96,64},{64,96},{160,128},{128,160},{224,192},{192,2... | collective-permute-start | bytes 1179656 | tf_op jit(solution)/shard_map/ppermute | solution.py:31
  82.2 0.8 convolution_bitcast_fusion.1
  84.1 1.9 %collective-permute-start.15 = (f32[4,128,128]{2,1,0:T(8,128)S(1)}, f32[4,128,128]{2,1,0:T(8,128)S(1)}, u32[]{:S(2)}, u32[]{:S(2)}) collective-permute-start(f32[4,128,128]{2,1,0:T(8,128)S(1)} %pad_maximum_fusion.3), channel_id=1, source_target_pairs={{64,0},{96,32},{0,64},{32,96},{192,128},{224,160},{128,192},{160,2... | collective-permute-start | bytes 786440 | tf_op jit(solution)/shard_map/ppermute | solution.py:31
  86.5 0.8 convolution_bitcast_fusion.2
  87.3 0.8 convolution_bitcast_fusion.3
  89.3 4.9 %collective-permute-done.15.refs_3_ = f32[4,128,128]{2,1,0:T(8,128)S(1)} collective-permute-done((f32[4,128,128]{2,1,0:T(8,128)S(1)}, f32[4,128,128]{2,1,0:T(8,128)S(1)}, u32[]{:S(2)}, u32[]{:S(2)}) %collective-permute-start.15) | collective-permute-done | bytes 262176 | tf_op jit(solution)/shard_map/ppermute | solution.py:31
  94.9 2.3 %place.1 = f32[16,128,128]{2,1,0:T(8,128)} custom-call(f32[4,128,128]{2,1,0:T(8,128)} %pad_maximum_fusion.refs_0_, f32[4,128,128]{2,1,0:T(8,128)} %copy-done.1, f32[4,128,128]{2,1,0:T(8,128)} %pad_maximum_fusion.2.refs_2_, f32[4,128,128]{2,1,0:T(8,128)} %copy-done.2), custom_call_target="tpu_custom_call" | custom-call | tf_op jit(solution)/shard_map/place/pallas_call | solution.py:164
  97.1 38.8 %all_to_all.5 = f32[32,64,128]{2,1,0:T(8,128)S(1)} all-to-all(f32[32,64,128]{2,1,0:T(8,128)} %bitcast.95), channel_id=1, replica_groups=mesh['gx'=16,'gy'=32] {'gy'}, dimensions={0} | all-to-all | bytes 2097152 | tf_op jit(solution)/shard_map/all_to_all | solution.py:221
  (47 shorter events, 11.0 us)
Async XLA Ops:
  3.1 22.8 %collective-permute-start = (f32[8,2,16,128]{3,2,1,0:T(8,128)}, f32[8,2,16,128]{3,2,1,0:T(8,128)S(1)}, u32[]{:S(2)}, u32[]{:S(2)}) collective-permute-start(f32[8,2,16,128]{3,2,1,0:T(8,128)} %get-tuple-element.10), channel_id=1, source_target_pairs={{0,1},{1,2},{2,3},{3,4},{4,5},{5,6},{6,7},{7,8},{8,9},{9,10},{10,1... | collective-permute-start | bytes 393224 | tf_op jit(solution)/shard_map/ppermute | solution.py:189
  7.4 18.6 %collective-permute-start.1 = (f32[8,2,16,128]{3,2,1,0:T(8,128)}, f32[8,2,16,128]{3,2,1,0:T(8,128)S(1)}, u32[]{:S(2)}, u32[]{:S(2)}) collective-permute-start(f32[8,2,16,128]{3,2,1,0:T(8,128)} %get-tuple-element.11), channel_id=1, source_target_pairs={{1,0},{2,1},{3,2},{4,3},{5,4},{6,5},{7,6},{8,7},{9,8},{10,9},{11,1... | collective-permute-start | bytes 393224 | tf_op jit(solution)/shard_map/ppermute | solution.py:190
  18.8 5.6 %collective-permute-start.2 = (f32[2,1536]{1,0:T(2,128)}, f32[2,1536]{1,0:T(2,128)S(1)}, u32[]{:S(2)}, u32[]{:S(2)}) collective-permute-start(f32[2,1536]{1,0:T(2,128)} %get-tuple-element.12), channel_id=1, source_target_pairs={{0,32},{32,64},{64,96},{96,128},{128,160},{160,192},{192,224},{224... | collective-permute-start | bytes 36872 | tf_op jit(solution)/shard_map/ppermute | solution.py:187
  20.7 5.2 %collective-permute-start.3 = (f32[2,1536]{1,0:T(2,128)}, f32[2,1536]{1,0:T(2,128)S(1)}, u32[]{:S(2)}, u32[]{:S(2)}) collective-permute-start(f32[2,1536]{1,0:T(2,128)} %get-tuple-element.13), channel_id=1, source_target_pairs={{32,0},{64,32},{96,64},{128,96},{160,128},{192,160},{224,192},{256... | collective-permute-start | bytes 36872 | tf_op jit(solution)/shard_map/ppermute | solution.py:188
  24.4 1.6 %copy-start.5 = (f32[2,1536]{1,0:T(2,128)}, f32[2,1536]{1,0:T(2,128)S(1)}, u32[]{:S(2)}) copy-start(f32[2,1536]{1,0:T(2,128)S(1)} %collective-permute-done.2.xleft_ref) | copy-start | bytes 36868
  25.9 0.6 copy-start.6
  25.9 0.7 copy-start.3
  26.0 0.7 copy-start.4
  31.6 14.9 %copy-start = (f32[8,12,16,128]{3,2,1,0:T(8,128)S(1)}, f32[8,12,16,128]{3,2,1,0:T(8,128)}, u32[]{:S(2)}) copy-start(f32[8,12,16,128]{3,2,1,0:T(8,128)} %get-tuple-element.16) | copy-start | bytes 2359300
  31.6 20.2 %collective-permute-start.6 = (f32[1536,128]{1,0:T(8,128)}, f32[1536,128]{1,0:T(8,128)S(1)}, u32[]{:S(2)}, u32[]{:S(2)}) collective-permute-start(f32[1536,128]{1,0:T(8,128)} %bitcast.85), channel_id=1, source_target_pairs={{384,0},{416,32},{448,64},{480,96},{0,128},{32,160},{64,192},{96,2... | collective-permute-start | bytes 2359304 | tf_op jit(solution)/shard_map/ppermute | solution.py:31
  34.1 21.7 %collective-permute-start.5 = (f32[1536,128]{1,0:T(8,128)}, f32[1536,128]{1,0:T(8,128)S(1)}, u32[]{:S(2)}, u32[]{:S(2)}) collective-permute-start(f32[1536,128]{1,0:T(8,128)} %bitcast.86), channel_id=1, source_target_pairs={{128,0},{160,32},{192,64},{224,96},{256,128},{288,160},{320,192},{... | collective-permute-start | bytes 2359304 | tf_op jit(solution)/shard_map/ppermute | solution.py:31
  37.6 22.4 %collective-permute-start.7 = (f32[1536,128]{1,0:T(8,128)}, f32[1536,128]{1,0:T(8,128)S(1)}, u32[]{:S(2)}, u32[]{:S(2)}) collective-permute-start(f32[1536,128]{1,0:T(8,128)} %bitcast.87), channel_id=1, source_target_pairs={{64,0},{96,32},{0,64},{32,96},{192,128},{224,160},{128,192},{160,2... | collective-permute-start | bytes 2359304 | tf_op jit(solution)/shard_map/ppermute | solution.py:31
  41.7 20.6 %collective-permute-start.4 = (f32[1536,128]{1,0:T(8,128)}, f32[1536,128]{1,0:T(8,128)S(1)}, u32[]{:S(2)}, u32[]{:S(2)}) collective-permute-start(f32[1536,128]{1,0:T(8,128)} %bitcast.88), channel_id=1, source_target_pairs={{32,0},{0,32},{96,64},{64,96},{160,128},{128,160},{224,192},{192,2... | collective-permute-start | bytes 2359304 | tf_op jit(solution)/shard_map/ppermute | solution.py:31
  51.8 23.1 %collective-permute-start.12 = (f32[768,128]{1,0:T(8,128)S(1)}, f32[768,128]{1,0:T(8,128)S(1)}, u32[]{:S(2)}, u32[]{:S(2)}) collective-permute-start(f32[768,128]{1,0:T(8,128)S(1)} %slice.37), channel_id=1, source_target_pairs={{384,0},{416,32},{448,64},{480,96},{0,128},{32,160},{64,192},{96,2... | collective-permute-start | bytes 1179656 | tf_op jit(solution)/shard_map/ppermute | solution.py:31
  55.9 21.5 %collective-permute-start.11 = (f32[768,128]{1,0:T(8,128)S(1)}, f32[768,128]{1,0:T(8,128)S(1)}, u32[]{:S(2)}, u32[]{:S(2)}) collective-permute-start(f32[768,128]{1,0:T(8,128)S(1)} %slice.36), channel_id=1, source_target_pairs={{128,0},{160,32},{192,64},{224,96},{256,128},{288,160},{320,192},{... | collective-permute-start | bytes 1179656 | tf_op jit(solution)/shard_map/ppermute | solution.py:31
  63.2 26.1 %collective-permute-start.8 = (f32[4,128,128]{2,1,0:T(8,128)S(1)}, f32[4,128,128]{2,1,0:T(8,128)S(1)}, u32[]{:S(2)}, u32[]{:S(2)}) collective-permute-start(f32[4,128,128]{2,1,0:T(8,128)S(1)} %pad_maximum_fusion.1), channel_id=1, source_target_pairs={{64,0},{96,32},{0,64},{32,96},{192,128},{224,160},{128,192},{160,2... | collective-permute-start | bytes 786440 | tf_op jit(solution)/shard_map/ppermute | solution.py:31
  68.3 13.2 %collective-permute-start.10 = (f32[1536,128]{1,0:T(8,128)S(1)}, f32[1536,128]{1,0:T(8,128)S(1)}, u32[]{:S(2)}, u32[]{:S(2)}) collective-permute-start(f32[1536,128]{1,0:T(8,128)S(1)} %collective-permute-done.6), channel_id=1, source_target_pairs={{32,0},{0,32},{96,64},{64,96},{160,128},{128,160},{224,192},{192,2... | collective-permute-start | bytes 2359304 | tf_op jit(solution)/shard_map/ppermute | solution.py:31
  72.5 9.7 %collective-permute-start.9 = (f32[1536,128]{1,0:T(8,128)S(1)}, f32[1536,128]{1,0:T(8,128)S(1)}, u32[]{:S(2)}, u32[]{:S(2)}) collective-permute-start(f32[1536,128]{1,0:T(8,128)S(1)} %collective-permute-done.5), channel_id=1, source_target_pairs={{32,0},{0,32},{96,64},{64,96},{160,128},{128,160},{224,192},{192,2... | collective-permute-start | bytes 2359304 | tf_op jit(solution)/shard_map/ppermute | solution.py:31
  75.4 7.6 %collective-permute-start.14 = (f32[768,128]{1,0:T(8,128)S(1)}, f32[768,128]{1,0:T(8,128)S(1)}, u32[]{:S(2)}, u32[]{:S(2)}) collective-permute-start(f32[768,128]{1,0:T(8,128)S(1)} %collective-permute-done.12), channel_id=1, source_target_pairs={{32,0},{0,32},{96,64},{64,96},{160,128},{128,160},{224,192},{192,2... | collective-permute-start | bytes 1179656 | tf_op jit(solution)/shard_map/ppermute | solution.py:31
  77.3 6.2 %collective-permute-start.13 = (f32[768,128]{1,0:T(8,128)S(1)}, f32[768,128]{1,0:T(8,128)S(1)}, u32[]{:S(2)}, u32[]{:S(2)}) collective-permute-start(f32[768,128]{1,0:T(8,128)S(1)} %collective-permute-done.11), channel_id=1, source_target_pairs={{32,0},{0,32},{96,64},{64,96},{160,128},{128,160},{224,192},{192,2... | collective-permute-start | bytes 1179656 | tf_op jit(solution)/shard_map/ppermute | solution.py:31
  84.1 10.1 %collective-permute-start.15 = (f32[4,128,128]{2,1,0:T(8,128)S(1)}, f32[4,128,128]{2,1,0:T(8,128)S(1)}, u32[]{:S(2)}, u32[]{:S(2)}) collective-permute-start(f32[4,128,128]{2,1,0:T(8,128)S(1)} %pad_maximum_fusion.3), channel_id=1, source_target_pairs={{64,0},{96,32},{0,64},{32,96},{192,128},{224,160},{128,192},{160,2... | collective-permute-start | bytes 786440 | tf_op jit(solution)/shard_map/ppermute | solution.py:31
  89.3 4.9 %copy-start.1 = (f32[4,128,128]{2,1,0:T(8,128)}, f32[4,128,128]{2,1,0:T(8,128)S(1)}, u32[]{:S(2)}) copy-start(f32[4,128,128]{2,1,0:T(8,128)S(1)} %collective-permute-done.8.refs_1_) | copy-start | bytes 786436
  94.2 0.7 copy-start.2

commit v4 on v3

--- a/solution.py
+++ b/solution.py
@@ -43,11 +43,10 @@
     ylo_ref[...] = s_ref[:, 0:2]
     yhi_ref[...] = s_ref[:, ny - 2 : ny]
     flat = s_ref[...].reshape(-1, 128)
-    edges = lax.dot_general(
-        edge_lanes(), flat, (((1,), (1,)), ((), ())), preferred_element_type=jnp.float32, precision=HIGHEST
-    )
-    xlo_ref[...] = edges[0:2]
-    xhi_ref[...] = edges[2:4]
+    for start in range(0, flat.shape[0], 128):
+        turned = flat[start : start + 128].T
+        xlo_ref[:, start : start + 128] = turned[0:2]
+        xhi_ref[:, start : start + 128] = turned[126:128]
 
 
 def pack(s):
@@ -142,10 +141,11 @@
     core = lax.rem(gx, CORES)
     y = lax.rem(lax.div(gx, CORES), NY_LO)
     x = lax.div(gx, CORES * NY_LO)
+    nx = out_ref.shape[-1]
     for n, (dx, dcore) in enumerate(ORDER):
         part, at = next((p, n - first) for p, first in zip(parts[::2], PARTS) if first <= n < first + p.shape[0])
         other = parts[1::2][[p is part for p in parts[::2]].index(True)]
-        for dy, value in ((0, part[at]), (1, other[at])):
+        for dy, value in ((0, part[at, :, :nx]), (1, other[at])):
             place_at = (
                 lax.rem(x + dx, NX_CHIPS) * (NY_LO * CORES)
                 + lax.rem(y + dy, NY_LO) * CORES
@@ -155,7 +155,7 @@
 
 
 ORDER = ((0, 0), (0, 1), (1, 0), (3, 0), (1, 1), (3, 1), (2, 0), (2, 1))
-PARTS = (0, 4)
+PARTS = (0, 6)
 
 
 def place(*parts):
@@ -202,22 +202,18 @@
     far1 = fetch(left[half:], -1, 0, 0)
     right_c = fetch(right, 0, 0, 1)
     left_c = fetch(left, 0, 0, 1)
-    far0_c = fetch(far0, 0, 0, 1)
-    far1_c = fetch(far1, 0, 0, 1)
-
-    def split(a, b, rows):
-        return against(a, rows[:half]) + against(b, rows[half:])
-
-    def first(rows):
-        return jnp.stack([against(a, rows) for a in (mine, mine_c, right, left)])
-
-    def second(rows):
-        wide = [against(a, rows) for a in (right_c, left_c)]
-        return jnp.stack(wide + [split(far0, far1, rows), split(far0_c, far1_c, rows)])
-
-    first_y = fetch(first(across), 0, 1, 0)
-    second_y = fetch(second(across), 0, 1, 0)
-    partial = place(first(mine), first_y, second(mine), second_y).reshape(n_gy, -1, nx)
+    far = jnp.concatenate([far0, far1], axis=0)
+    far_c = fetch(far, 0, 0, 1)
+    rows = jnp.concatenate([mine, across], axis=1)
+
+    def products(*columns):
+        return jnp.stack([against(a, rows) for a in columns])
+
+    first = products(mine, mine_c, right, left, right_c, left_c)
+    second = products(far, far_c)
+    first_y = fetch(first[:, :, nx:], 0, 1, 0)
+    second_y = fetch(second[:, :, nx:], 0, 1, 0)
+    partial = place(first, first_y, second, second_y).reshape(n_gy, -1, nx)
     pieces = lax.all_to_all(partial, "gy", 0, 0, tiled=True)
     columns = nv * nz * ny * n_gy
     gram = jnp.sum(pieces, axis=0) / jnp.float32(columns)
@@ -233,4 +229,6 @@
         P(None, "gy", "gx"),
     )
     out_specs = (P(None, None, "gy", "gx"), P(None, None, "gy", "gx"), P("gx", "gy"))
-    return jax.shard_map(section, mesh=mesh, in_specs=in_specs, out_specs=out_specs, check_vma=False)
+    return jax.shard_map(
+        section, mesh=mesh, in_specs=in_specs, out_specs=out_specs, check_vma=False
+    )

time: 137 us -> 140 us (1.022)
  the two profiles are of different devices: /device:TPU:14 before, /device:TPU:8 now
where the time goes in v4:
time: 140 us; the launch traced here: 139 us
  starting transfers between devices  56.8 us (41%)
  blocking collectives  41.9 us (30%)
  waiting for transfers between devices  20.7 us (15%)
  Pallas kernels  9.41 us (7%)
  matrix products  6.44 us (5%)
  local copies, waits for them, and re-layouts  1.47 us (1%)
  other arithmetic  1.43 us (1%)
    all_to_all x1, blocking collectives, section(): pieces = lax.all_to_all(partial, 'gy', 0, 0, tiled=True)  41.9 us
    ppermute x11, starting transfers between devices, fetch(): return lax.ppermute(value, 'gx', from_offset(dx, dy, dcore))  35.6 us
    ppermute x11, waiting for transfers between devices, fetch(): return lax.ppermute(value, 'gx', from_offset(dx, dy, dcore))  19.1 us
    ppermute x1, starting transfers between devices, section(): yabove = lax.ppermute(ylo, 'gy', down(n_gy))  11.4 us
    dot_general x8, matrix products, against(): lax.dot_general(columns, rows, (((0,), (0,)), ((), ())), preferred_elemen...  6.44 us
    pallas_call x1, Pallas kernels, stencil(): pl.pallas_call(stencil_kernel, grid=(nv // per_step,), in_specs=[whole, w...  4.96 us
    ppermute x1, starting transfers between devices, section(): ybelow = lax.ppermute(yhi, 'gy', up(n_gy))  4.27 us
    ppermute x1, starting transfers between devices, section(): xright = lax.ppermute(xlo, 'gx', down(n_gx))  3.64 us
  transfers between devices with their start and end apart: 15, of which 6 were waited for; matrix products, arithmetic and copies ran while one was open for 5% of the time, Pallas kernels for 0%

profile of v4, /device:TPU:8, one launch (start us, length us, event | category | flops | bytes accessed | tf_op | source)
XLA Modules:
  0.0 139.2 jit_solution(7702877037671890796)
XLA Ops:
  0.6 2.0 %pack_edges.1 = (f32[8,2,16,128]{3,2,1,0:T(8,128)}, f32[8,2,16,128]{3,2,1,0:T(8,128)}, f32[2,1536]{1,0:T(2,128)}, f32[2,1536]{1,0:T(2,128)}) custom-call(f32[8,12,16,128]{3,2,1,0:T(8,128)} %bitcast.60), custom_call_target="tpu_custom_call" | custom-call | tf_op jit(solution)/shard_map/pack_edges/pallas_call | solution.py:55
  2.6 4.3 %collective-permute-start = (f32[8,2,16,128]{3,2,1,0:T(8,128)}, f32[8,2,16,128]{3,2,1,0:T(8,128)S(1)}, u32[]{:S(2)}, u32[]{:S(2)}) collective-permute-start(f32[8,2,16,128]{3,2,1,0:T(8,128)} %get-tuple-element.10), channel_id=1, source_target_pairs={{0,1},{1,2},{2,3},{3,4},{4,5},{5,6},{6,7},{7,8},{8,9},{9,10},{10,1... | collective-permute-start | bytes 393224 | tf_op jit(solution)/shard_map/ppermute | solution.py:189
  6.9 11.4 %collective-permute-start.1 = (f32[8,2,16,128]{3,2,1,0:T(8,128)}, f32[8,2,16,128]{3,2,1,0:T(8,128)S(1)}, u32[]{:S(2)}, u32[]{:S(2)}) collective-permute-start(f32[8,2,16,128]{3,2,1,0:T(8,128)} %get-tuple-element.11), channel_id=1, source_target_pairs={{1,0},{2,1},{3,2},{4,3},{5,4},{6,5},{7,6},{8,7},{9,8},{10,9},{11,1... | collective-permute-start | bytes 393224 | tf_op jit(solution)/shard_map/ppermute | solution.py:190
  18.3 1.9 %collective-permute-start.2 = (f32[2,1536]{1,0:T(2,128)}, f32[2,1536]{1,0:T(2,128)S(1)}, u32[]{:S(2)}, u32[]{:S(2)}) collective-permute-start(f32[2,1536]{1,0:T(2,128)} %get-tuple-element.12), channel_id=1, source_target_pairs={{0,32},{32,64},{64,96},{96,128},{128,160},{160,192},{192,224},{224... | collective-permute-start | bytes 36872 | tf_op jit(solution)/shard_map/ppermute | solution.py:187
  20.2 3.6 %collective-permute-start.3 = (f32[2,1536]{1,0:T(2,128)}, f32[2,1536]{1,0:T(2,128)S(1)}, u32[]{:S(2)}, u32[]{:S(2)}) collective-permute-start(f32[2,1536]{1,0:T(2,128)} %get-tuple-element.13), channel_id=1, source_target_pairs={{32,0},{64,32},{96,64},{128,96},{160,128},{192,160},{224,192},{256... | collective-permute-start | bytes 36872 | tf_op jit(solution)/shard_map/ppermute | solution.py:188
  23.9 1.6 %collective-permute-done.3.xright_ref = f32[2,1536]{1,0:T(2,128)S(1)} collective-permute-done((f32[2,1536]{1,0:T(2,128)}, f32[2,1536]{1,0:T(2,128)S(1)}, u32[]{:S(2)}, u32[]{:S(2)}) %collective-permute-start.3) | collective-permute-done | bytes 12320 | tf_op jit(solution)/shard_map/ppermute | solution.py:188
  26.2 5.0 %stencil.1 = (f32[8,12,16,128]{3,2,1,0:T(8,128)}, f32[8,12,16,128]{3,2,1,0:T(8,128)}, f32[8,12,16,128]{3,2,1,0:T(8,128)}) custom-call(f32[8,12,16,128]{3,2,1,0:T(8,128)} %bitcast.61, f32[8,12,16,128]{3,2,1,0:T(8,128)} %bitcast.62, bf16[8,12,16,128]{3,2,1,0:T(8,128)(2,1)} %bitcast.63, f32[3,12,16,128]{3,2,1,0:T(8,128)} %bitcast.64, f32[12,16,128]{2,1,0:T(8,128)} %bitcast.65, ...), custom_call_target="tpu_custom_call" | custom-call | tf_op jit(solution)/shard_map/stencil/pallas_call | solution.py:122
  31.2 4.8 %collective-permute-start.6 = (f32[1536,128]{1,0:T(8,128)}, f32[1536,128]{1,0:T(8,128)S(1)}, u32[]{:S(2)}, u32[]{:S(2)}) collective-permute-start(f32[1536,128]{1,0:T(8,128)} %bitcast.47), channel_id=1, source_target_pairs={{128,0},{160,32},{192,64},{224,96},{256,128},{288,160},{320,192},{... | collective-permute-start | bytes 2359304 | tf_op jit(solution)/shard_map/ppermute | solution.py:31
  36.0 1.9 %collective-permute-start.7 = (f32[1536,128]{1,0:T(8,128)}, f32[1536,128]{1,0:T(8,128)S(1)}, u32[]{:S(2)}, u32[]{:S(2)}) collective-permute-start(f32[1536,128]{1,0:T(8,128)} %bitcast.48), channel_id=1, source_target_pairs={{384,0},{416,32},{448,64},{480,96},{0,128},{32,160},{64,192},{96,2... | collective-permute-start | bytes 2359304 | tf_op jit(solution)/shard_map/ppermute | solution.py:31
  37.9 4.6 %collective-permute-start.4 = (f32[1536,128]{1,0:T(8,128)}, f32[1536,128]{1,0:T(8,128)S(1)}, u32[]{:S(2)}, u32[]{:S(2)}) collective-permute-start(f32[1536,128]{1,0:T(8,128)} %bitcast.49), channel_id=1, source_target_pairs={{64,0},{96,32},{0,64},{32,96},{192,128},{224,160},{128,192},{160,2... | collective-permute-start | bytes 2359304 | tf_op jit(solution)/shard_map/ppermute | solution.py:31
  42.5 2.4 %collective-permute-start.5 = (f32[1536,128]{1,0:T(8,128)}, f32[1536,128]{1,0:T(8,128)S(1)}, u32[]{:S(2)}, u32[]{:S(2)}) collective-permute-start(f32[1536,128]{1,0:T(8,128)} %bitcast.50), channel_id=1, source_target_pairs={{32,0},{0,32},{96,64},{64,96},{160,128},{128,160},{224,192},{192,2... | collective-permute-start | bytes 2359304 | tf_op jit(solution)/shard_map/ppermute | solution.py:31
  44.9 6.8 %collective-permute-done.6 = f32[1536,128]{1,0:T(8,128)S(1)} collective-permute-done((f32[1536,128]{1,0:T(8,128)}, f32[1536,128]{1,0:T(8,128)S(1)}, u32[]{:S(2)}, u32[]{:S(2)}) %collective-permute-start.6) | collective-permute-done | bytes 786464 | tf_op jit(solution)/shard_map/ppermute | solution.py:31
  51.7 5.5 %collective-permute-start.11 = (f32[768,128]{1,0:T(8,128)S(1)}, f32[768,128]{1,0:T(8,128)S(1)}, u32[]{:S(2)}, u32[]{:S(2)}) collective-permute-start(f32[768,128]{1,0:T(8,128)S(1)} %slice.17), channel_id=1, source_target_pairs={{128,0},{160,32},{192,64},{224,96},{256,128},{288,160},{320,192},{... | collective-permute-start | bytes 1179656 | tf_op jit(solution)/shard_map/ppermute | solution.py:31
  57.5 1.9 %collective-permute-start.12 = (f32[768,128]{1,0:T(8,128)S(1)}, f32[768,128]{1,0:T(8,128)S(1)}, u32[]{:S(2)}, u32[]{:S(2)}) collective-permute-start(f32[768,128]{1,0:T(8,128)S(1)} %slice.18), channel_id=1, source_target_pairs={{384,0},{416,32},{448,64},{480,96},{0,128},{32,160},{64,192},{96,2... | collective-permute-start | bytes 1179656 | tf_op jit(solution)/shard_map/ppermute | solution.py:31
  59.4 3.9 %collective-permute-start.8 = (f32[1536,128]{1,0:T(8,128)S(1)}, f32[1536,128]{1,0:T(8,128)S(1)}, u32[]{:S(2)}, u32[]{:S(2)}) collective-permute-start(f32[1536,128]{1,0:T(8,128)S(1)} %collective-permute-done.6), channel_id=1, source_target_pairs={{32,0},{0,32},{96,64},{64,96},{160,128},{128,160},{224,192},{192,2... | collective-permute-start | bytes 2359304 | tf_op jit(solution)/shard_map/ppermute | solution.py:31
  63.4 1.9 %collective-permute-start.9 = (f32[1536,128]{1,0:T(8,128)S(1)}, f32[1536,128]{1,0:T(8,128)S(1)}, u32[]{:S(2)}, u32[]{:S(2)}) collective-permute-start(f32[1536,128]{1,0:T(8,128)S(1)} %collective-permute-done.7), channel_id=1, source_target_pairs={{32,0},{0,32},{96,64},{64,96},{160,128},{128,160},{224,192},{192,2... | collective-permute-start | bytes 2359304 | tf_op jit(solution)/shard_map/ppermute | solution.py:31
  65.3 0.8 fusion.5
  66.2 0.8 fusion.4
  67.0 0.8 fusion.3
  67.8 3.7 %collective-permute-done.12 = f32[768,128]{1,0:T(8,128)S(1)} collective-permute-done((f32[768,128]{1,0:T(8,128)S(1)}, f32[768,128]{1,0:T(8,128)S(1)}, u32[]{:S(2)}, u32[]{:S(2)}) %collective-permute-start.12) | collective-permute-done | bytes 393248 | tf_op jit(solution)/shard_map/ppermute | solution.py:31
  71.6 2.8 %collective-permute-start.13 = (f32[1536,128]{1,0:T(8,128)S(1)}, f32[1536,128]{1,0:T(8,128)S(1)}, u32[]{:S(2)}, u32[]{:S(2)}) collective-permute-start(f32[1536,128]{1,0:T(8,128)S(1)} %constant_dynamic-update-slice_fusion), channel_id=1, source_target_pairs={{32,0},{0,32},{96,64},{64,96},{160,128},{128,160},{224,192},{192,2... | collective-permute-start | bytes 2359304 | tf_op jit(solution)/shard_map/ppermute | solution.py:31
  74.4 0.8 fusion.2
  75.2 0.8 convolution_bitcast_fusion.1
  76.0 0.8 fusion.1
  76.8 0.8 fusion.refs_0_
  77.7 3.3 %collective-permute-start.10 = (f32[6,128,128]{2,1,0:T(8,128)S(1)}, f32[6,128,128]{2,1,0:T(8,128)S(1)}, u32[]{:S(2)}, u32[]{:S(2)}) collective-permute-start(f32[6,128,128]{2,1,0:T(8,128)S(1)} %slice.16), channel_id=1, source_target_pairs={{64,0},{96,32},{0,64},{32,96},{192,128},{224,160},{128,192},{160,2... | collective-permute-start | bytes 1179656 | tf_op jit(solution)/shard_map/ppermute | solution.py:31
  81.0 0.8 convolution_bitcast_fusion
  81.8 2.6 %collective-permute-start.14 = (f32[2,128,128]{2,1,0:T(8,128)S(1)}, f32[2,128,128]{2,1,0:T(8,128)S(1)}, u32[]{:S(2)}, u32[]{:S(2)}) collective-permute-start(f32[2,128,128]{2,1,0:T(8,128)S(1)} %fusion.6), channel_id=1, source_target_pairs={{64,0},{96,32},{0,64},{32,96},{192,128},{224,160},{128,192},{160,2... | collective-permute-start | bytes 393224 | tf_op jit(solution)/shard_map/ppermute | solution.py:31
  85.1 6.4 %collective-permute-done.10.refs_1_ = f32[6,128,128]{2,1,0:T(8,128)S(1)} collective-permute-done((f32[6,128,128]{2,1,0:T(8,128)S(1)}, f32[6,128,128]{2,1,0:T(8,128)S(1)}, u32[]{:S(2)}, u32[]{:S(2)}) %collective-permute-start.10) | collective-permute-done | bytes 393248 | tf_op jit(solution)/shard_map/ppermute | solution.py:31
  91.6 2.0 %collective-permute-done.14.refs_3_ = f32[2,128,128]{2,1,0:T(8,128)S(1)} collective-permute-done((f32[2,128,128]{2,1,0:T(8,128)S(1)}, f32[2,128,128]{2,1,0:T(8,128)S(1)}, u32[]{:S(2)}, u32[]{:S(2)}) %collective-permute-start.14) | collective-permute-done | bytes 131104 | tf_op jit(solution)/shard_map/ppermute | solution.py:31
  94.2 2.4 %place.1 = f32[16,128,128]{2,1,0:T(8,128)} custom-call(f32[6,128,256]{2,1,0:T(8,128)} %copy-done.1, f32[6,128,128]{2,1,0:T(8,128)} %copy-done.2, f32[2,128,256]{2,1,0:T(8,128)} %pad_maximum_fusion.1.refs_2_, f32[2,128,128]{2,1,0:T(8,128)} %copy-done.5), custom_call_target="tpu_custom_call" | custom-call | tf_op jit(solution)/shard_map/place/pallas_call | solution.py:164
  96.6 41.9 %all_to_all.5 = f32[32,64,128]{2,1,0:T(8,128)S(1)} all-to-all(f32[32,64,128]{2,1,0:T(8,128)} %bitcast.59), channel_id=1, replica_groups=mesh['gx'=16,'gy'=32] {'gy'}, dimensions={0} | all-to-all | bytes 2097152 | tf_op jit(solution)/shard_map/all_to_all | solution.py:217
  (35 shorter events, 3.2 us)
Async XLA Ops:
  2.6 22.8 %collective-permute-start = (f32[8,2,16,128]{3,2,1,0:T(8,128)}, f32[8,2,16,128]{3,2,1,0:T(8,128)S(1)}, u32[]{:S(2)}, u32[]{:S(2)}) collective-permute-start(f32[8,2,16,128]{3,2,1,0:T(8,128)} %get-tuple-element.10), channel_id=1, source_target_pairs={{0,1},{1,2},{2,3},{3,4},{4,5},{5,6},{6,7},{7,8},{8,9},{9,10},{10,1... | collective-permute-start | bytes 393224 | tf_op jit(solution)/shard_map/ppermute | solution.py:189
  6.9 18.6 %collective-permute-start.1 = (f32[8,2,16,128]{3,2,1,0:T(8,128)}, f32[8,2,16,128]{3,2,1,0:T(8,128)S(1)}, u32[]{:S(2)}, u32[]{:S(2)}) collective-permute-start(f32[8,2,16,128]{3,2,1,0:T(8,128)} %get-tuple-element.11), channel_id=1, source_target_pairs={{1,0},{2,1},{3,2},{4,3},{5,4},{6,5},{7,6},{8,7},{9,8},{10,9},{11,1... | collective-permute-start | bytes 393224 | tf_op jit(solution)/shard_map/ppermute | solution.py:190
  18.3 5.6 %collective-permute-start.2 = (f32[2,1536]{1,0:T(2,128)}, f32[2,1536]{1,0:T(2,128)S(1)}, u32[]{:S(2)}, u32[]{:S(2)}) collective-permute-start(f32[2,1536]{1,0:T(2,128)} %get-tuple-element.12), channel_id=1, source_target_pairs={{0,32},{32,64},{64,96},{96,128},{128,160},{160,192},{192,224},{224... | collective-permute-start | bytes 36872 | tf_op jit(solution)/shard_map/ppermute | solution.py:187
  20.2 5.2 %collective-permute-start.3 = (f32[2,1536]{1,0:T(2,128)}, f32[2,1536]{1,0:T(2,128)S(1)}, u32[]{:S(2)}, u32[]{:S(2)}) collective-permute-start(f32[2,1536]{1,0:T(2,128)} %get-tuple-element.13), channel_id=1, source_target_pairs={{32,0},{64,32},{96,64},{128,96},{160,128},{192,160},{224,192},{256... | collective-permute-start | bytes 36872 | tf_op jit(solution)/shard_map/ppermute | solution.py:188
  23.9 1.6 %copy-start.6 = (f32[2,1536]{1,0:T(2,128)}, f32[2,1536]{1,0:T(2,128)S(1)}, u32[]{:S(2)}) copy-start(f32[2,1536]{1,0:T(2,128)S(1)} %collective-permute-done.2.xleft_ref) | copy-start | bytes 36868
  25.5 0.6 copy-start.7
  25.5 0.7 copy-start.3
  25.5 0.7 copy-start.4
  31.1 34.2 %copy-start = (f32[8,12,16,128]{3,2,1,0:T(8,128)S(1)}, f32[8,12,16,128]{3,2,1,0:T(8,128)}, u32[]{:S(2)}) copy-start(f32[8,12,16,128]{3,2,1,0:T(8,128)} %get-tuple-element.16) | copy-start | bytes 2359300
  31.2 20.5 %collective-permute-start.6 = (f32[1536,128]{1,0:T(8,128)}, f32[1536,128]{1,0:T(8,128)S(1)}, u32[]{:S(2)}, u32[]{:S(2)}) collective-permute-start(f32[1536,128]{1,0:T(8,128)} %bitcast.47), channel_id=1, source_target_pairs={{128,0},{160,32},{192,64},{224,96},{256,128},{288,160},{320,192},{... | collective-permute-start | bytes 2359304 | tf_op jit(solution)/shard_map/ppermute | solution.py:31
  36.0 21.5 %collective-permute-start.7 = (f32[1536,128]{1,0:T(8,128)}, f32[1536,128]{1,0:T(8,128)S(1)}, u32[]{:S(2)}, u32[]{:S(2)}) collective-permute-start(f32[1536,128]{1,0:T(8,128)} %bitcast.48), channel_id=1, source_target_pairs={{384,0},{416,32},{448,64},{480,96},{0,128},{32,160},{64,192},{96,2... | collective-permute-start | bytes 2359304 | tf_op jit(solution)/shard_map/ppermute | solution.py:31
  37.9 25.5 %collective-permute-start.4 = (f32[1536,128]{1,0:T(8,128)}, f32[1536,128]{1,0:T(8,128)S(1)}, u32[]{:S(2)}, u32[]{:S(2)}) collective-permute-start(f32[1536,128]{1,0:T(8,128)} %bitcast.49), channel_id=1, source_target_pairs={{64,0},{96,32},{0,64},{32,96},{192,128},{224,160},{128,192},{160,2... | collective-permute-start | bytes 2359304 | tf_op jit(solution)/shard_map/ppermute | solution.py:31
  42.5 23.6 %collective-permute-start.5 = (f32[1536,128]{1,0:T(8,128)}, f32[1536,128]{1,0:T(8,128)S(1)}, u32[]{:S(2)}, u32[]{:S(2)}) collective-permute-start(f32[1536,128]{1,0:T(8,128)} %bitcast.50), channel_id=1, source_target_pairs={{32,0},{0,32},{96,64},{64,96},{160,128},{128,160},{224,192},{192,2... | collective-permute-start | bytes 2359304 | tf_op jit(solution)/shard_map/ppermute | solution.py:31
  51.7 16.1 %collective-permute-start.11 = (f32[768,128]{1,0:T(8,128)S(1)}, f32[768,128]{1,0:T(8,128)S(1)}, u32[]{:S(2)}, u32[]{:S(2)}) collective-permute-start(f32[768,128]{1,0:T(8,128)S(1)} %slice.17), channel_id=1, source_target_pairs={{128,0},{160,32},{192,64},{224,96},{256,128},{288,160},{320,192},{... | collective-permute-start | bytes 1179656 | tf_op jit(solution)/shard_map/ppermute | solution.py:31
  57.5 14.0 %collective-permute-start.12 = (f32[768,128]{1,0:T(8,128)S(1)}, f32[768,128]{1,0:T(8,128)S(1)}, u32[]{:S(2)}, u32[]{:S(2)}) collective-permute-start(f32[768,128]{1,0:T(8,128)S(1)} %slice.18), channel_id=1, source_target_pairs={{384,0},{416,32},{448,64},{480,96},{0,128},{32,160},{64,192},{96,2... | collective-permute-start | bytes 1179656 | tf_op jit(solution)/shard_map/ppermute | solution.py:31
  59.4 16.6 %collective-permute-start.8 = (f32[1536,128]{1,0:T(8,128)S(1)}, f32[1536,128]{1,0:T(8,128)S(1)}, u32[]{:S(2)}, u32[]{:S(2)}) collective-permute-start(f32[1536,128]{1,0:T(8,128)S(1)} %collective-permute-done.6), channel_id=1, source_target_pairs={{32,0},{0,32},{96,64},{64,96},{160,128},{128,160},{224,192},{192,2... | collective-permute-start | bytes 2359304 | tf_op jit(solution)/shard_map/ppermute | solution.py:31
  63.4 13.4 %collective-permute-start.9 = (f32[1536,128]{1,0:T(8,128)S(1)}, f32[1536,128]{1,0:T(8,128)S(1)}, u32[]{:S(2)}, u32[]{:S(2)}) collective-permute-start(f32[1536,128]{1,0:T(8,128)S(1)} %collective-permute-done.7), channel_id=1, source_target_pairs={{32,0},{0,32},{96,64},{64,96},{160,128},{128,160},{224,192},{192,2... | collective-permute-start | bytes 2359304 | tf_op jit(solution)/shard_map/ppermute | solution.py:31
  71.6 9.4 %collective-permute-start.13 = (f32[1536,128]{1,0:T(8,128)S(1)}, f32[1536,128]{1,0:T(8,128)S(1)}, u32[]{:S(2)}, u32[]{:S(2)}) collective-permute-start(f32[1536,128]{1,0:T(8,128)S(1)} %constant_dynamic-update-slice_fusion), channel_id=1, source_target_pairs={{32,0},{0,32},{96,64},{64,96},{160,128},{128,160},{224,192},{192,2... | collective-permute-start | bytes 2359304 | tf_op jit(solution)/shard_map/ppermute | solution.py:31
  77.6 4.1 %copy-start.1 = (f32[6,128,256]{2,1,0:T(8,128)}, f32[6,128,256]{2,1,0:T(8,128)S(1)}, u32[]{:S(2)}) copy-start(f32[6,128,256]{2,1,0:T(8,128)S(1)} %fusion.refs_0_) | copy-start | bytes 2359300
  77.7 13.9 %collective-permute-start.10 = (f32[6,128,128]{2,1,0:T(8,128)S(1)}, f32[6,128,128]{2,1,0:T(8,128)S(1)}, u32[]{:S(2)}, u32[]{:S(2)}) collective-permute-start(f32[6,128,128]{2,1,0:T(8,128)S(1)} %slice.16), channel_id=1, source_target_pairs={{64,0},{96,32},{0,64},{32,96},{192,128},{224,160},{128,192},{160,2... | collective-permute-start | bytes 1179656 | tf_op jit(solution)/shard_map/ppermute | solution.py:31
  81.8 11.7 %collective-permute-start.14 = (f32[2,128,128]{2,1,0:T(8,128)S(1)}, f32[2,128,128]{2,1,0:T(8,128)S(1)}, u32[]{:S(2)}, u32[]{:S(2)}) collective-permute-start(f32[2,128,128]{2,1,0:T(8,128)S(1)} %fusion.6), channel_id=1, source_target_pairs={{64,0},{96,32},{0,64},{32,96},{192,128},{224,160},{128,192},{160,2... | collective-permute-start | bytes 393224 | tf_op jit(solution)/shard_map/ppermute | solution.py:31
  91.6 2.0 %copy-start.2 = (f32[6,128,128]{2,1,0:T(8,128)}, f32[6,128,128]{2,1,0:T(8,128)S(1)}, u32[]{:S(2)}) copy-start(f32[6,128,128]{2,1,0:T(8,128)S(1)} %collective-permute-done.10.refs_1_) | copy-start | bytes 1179652
  93.5 0.6 copy-start.5

commit v5 on v4

--- a/solution.py
+++ b/solution.py
@@ -12,6 +12,8 @@
 
 NX_CHIPS, NY_LO, CORES = 4, 2, 2
 HIGHEST = lax.Precision.HIGHEST
+FIRST = ((0, 0), (0, 1), (1, 0), (3, 0), (1, 1), (3, 1))
+SECOND = ((2, 0), (2, 1))
 
 
 def gx_of(x, y, core):
@@ -135,39 +137,23 @@
     )(s, r, c, vel, dif, ybelow, yabove, xleft, xright)
 
 
-def place_kernel(*refs):
-    *parts, out_ref = refs
-    gx = lax.axis_index("gx")
-    core = lax.rem(gx, CORES)
-    y = lax.rem(lax.div(gx, CORES), NY_LO)
-    x = lax.div(gx, CORES * NY_LO)
-    nx = out_ref.shape[-1]
-    for n, (dx, dcore) in enumerate(ORDER):
-        part, at = next((p, n - first) for p, first in zip(parts[::2], PARTS) if first <= n < first + p.shape[0])
-        other = parts[1::2][[p is part for p in parts[::2]].index(True)]
-        for dy, value in ((0, part[at, :, :nx]), (1, other[at])):
-            place_at = (
-                lax.rem(x + dx, NX_CHIPS) * (NY_LO * CORES)
-                + lax.rem(y + dy, NY_LO) * CORES
-                + lax.rem(core + dcore, CORES)
-            )
-            out_ref[place_at] = value
-
-
-ORDER = ((0, 0), (0, 1), (1, 0), (3, 0), (1, 1), (3, 1), (2, 0), (2, 1))
-PARTS = (0, 6)
-
-
-def place(*parts):
-    nx = parts[0].shape[-2]
-    vmem = pl.BlockSpec(memory_space=pltpu.VMEM)
-    return pl.pallas_call(
-        place_kernel,
-        in_specs=[vmem] * len(parts),
-        out_specs=vmem,
-        out_shape=jax.ShapeDtypeStruct((NX_CHIPS * NY_LO * CORES, nx, nx), jnp.float32),
-        name="place",
-    )(*parts)
+ORDER = tuple(
+    (dx, dy, dcore)
+    for dy, columns in ((0, FIRST), (0, SECOND), (1, FIRST), (1, SECOND))
+    for dx, dcore in columns
+)
+
+
+def owners(n_gy):
+    groups = []
+    for x in range(NX_CHIPS):
+        for y in range(NY_LO):
+            for core in range(CORES):
+                blocks = [gx_of(x + dx, y + dy, core + dcore) for dx, dy, dcore in ORDER]
+                mine = gx_of(x, y, core)
+                each = n_gy // len(blocks)
+                groups.append([mine * n_gy + block * each + part for block in blocks for part in range(each)])
+    return groups
 
 
 def against(columns, rows):
@@ -202,7 +188,7 @@
     far1 = fetch(left[half:], -1, 0, 0)
     right_c = fetch(right, 0, 0, 1)
     left_c = fetch(left, 0, 0, 1)
-    far = jnp.concatenate([far0, far1], axis=0)
+    far = jnp.pad(far0, ((0, half), (0, 0))) + jnp.pad(far1, ((half, 0), (0, 0)))
     far_c = fetch(far, 0, 0, 1)
     rows = jnp.concatenate([mine, across], axis=1)
 
@@ -213,8 +199,9 @@
     second = products(far, far_c)
     first_y = fetch(first[:, :, nx:], 0, 1, 0)
     second_y = fetch(second[:, :, nx:], 0, 1, 0)
-    partial = place(first, first_y, second, second_y).reshape(n_gy, -1, nx)
-    pieces = lax.all_to_all(partial, "gy", 0, 0, tiled=True)
+    partial = jnp.concatenate([first[:, :, :nx], second[:, :, :nx], first_y, second_y], axis=0)
+    partial = partial.reshape(n_gy, -1, nx)
+    pieces = lax.all_to_all(partial, ("gx", "gy"), 0, 0, tiled=True, axis_index_groups=owners(n_gy))
     columns = nv * nz * ny * n_gy
     gram = jnp.sum(pieces, axis=0) / jnp.float32(columns)
     return to_yzx(new_state), to_yzx(new_register), gram.T
@@ -229,6 +216,4 @@
         P(None, "gy", "gx"),
     )
     out_specs = (P(None, None, "gy", "gx"), P(None, None, "gy", "gx"), P("gx", "gy"))
-    return jax.shard_map(
-        section, mesh=mesh, in_specs=in_specs, out_specs=out_specs, check_vma=False
-    )
+    return jax.shard_map(section, mesh=mesh, in_specs=in_specs, out_specs=out_specs, check_vma=False)

time: 140 us -> 134 us (0.957)
  the two profiles are of different devices: /device:TPU:8 before, /device:TPU:1 now
where the time goes in v5:
time: 134 us; the launch traced here: 133 us
  starting transfers between devices  58.1 us (43%)
  blocking collectives  37.7 us (28%)
  waiting for transfers between devices  21.3 us (16%)
  Pallas kernels  6.97 us (5%)
  matrix products  6.44 us (5%)
    all_to_all x1, blocking collectives, section(): lax.all_to_all(partial, ('gx', 'gy'), 0, 0, tiled=True, axis_index_groups...  37.7 us
    ppermute x11, starting transfers between devices, fetch(): return lax.ppermute(value, 'gx', from_offset(dx, dy, dcore))  35.9 us
    ppermute x11, waiting for transfers between devices, fetch(): return lax.ppermute(value, 'gx', from_offset(dx, dy, dcore))  18.1 us
    ppermute x1, starting transfers between devices, section(): yabove = lax.ppermute(ylo, 'gy', down(n_gy))  12.3 us
    dot_general x8, matrix products, against(): lax.dot_general(columns, rows, (((0,), (0,)), ((), ())), preferred_elemen...  6.44 us
    pallas_call x1, Pallas kernels, stencil(): pl.pallas_call(stencil_kernel, grid=(nv // per_step,), in_specs=[whole, w...  4.96 us
    ppermute x1, starting transfers between devices, section(): ybelow = lax.ppermute(yhi, 'gy', up(n_gy))  4.81 us
    ppermute x1, waiting for transfers between devices, section(): xright = lax.ppermute(xlo, 'gx', down(n_gx))  3.28 us
  transfers between devices with their start and end apart: 15, of which 5 were waited for; matrix products, arithmetic and copies ran while one was open for 5% of the time, Pallas kernels for 0%

profile of v5, /device:TPU:1, one launch (start us, length us, event | category | flops | bytes accessed | tf_op | source)
XLA Modules:
  0.0 133.2 jit_solution(9669888365125766)
XLA Ops:
  0.6 2.0 %pack_edges.1 = (f32[8,2,16,128]{3,2,1,0:T(8,128)}, f32[8,2,16,128]{3,2,1,0:T(8,128)}, f32[2,1536]{1,0:T(2,128)}, f32[2,1536]{1,0:T(2,128)}) custom-call(f32[8,12,16,128]{3,2,1,0:T(8,128)} %bitcast.59), custom_call_target="tpu_custom_call" | custom-call | tf_op jit(solution)/shard_map/pack_edges/pallas_call | solution.py:57
  2.6 4.8 %collective-permute-start = (f32[8,2,16,128]{3,2,1,0:T(8,128)}, f32[8,2,16,128]{3,2,1,0:T(8,128)S(1)}, u32[]{:S(2)}, u32[]{:S(2)}) collective-permute-start(f32[8,2,16,128]{3,2,1,0:T(8,128)} %get-tuple-element.10), channel_id=1, source_target_pairs={{0,1},{1,2},{2,3},{3,4},{4,5},{5,6},{6,7},{7,8},{8,9},{9,10},{10,1... | collective-permute-start | bytes 393224 | tf_op jit(solution)/shard_map/ppermute | solution.py:175
  7.5 12.3 %collective-permute-start.1 = (f32[8,2,16,128]{3,2,1,0:T(8,128)}, f32[8,2,16,128]{3,2,1,0:T(8,128)S(1)}, u32[]{:S(2)}, u32[]{:S(2)}) collective-permute-start(f32[8,2,16,128]{3,2,1,0:T(8,128)} %get-tuple-element.11), channel_id=1, source_target_pairs={{1,0},{2,1},{3,2},{4,3},{5,4},{6,5},{7,6},{8,7},{9,8},{10,9},{11,1... | collective-permute-start | bytes 393224 | tf_op jit(solution)/shard_map/ppermute | solution.py:176
  19.7 3.1 %collective-permute-start.2 = (f32[2,1536]{1,0:T(2,128)}, f32[2,1536]{1,0:T(2,128)S(1)}, u32[]{:S(2)}, u32[]{:S(2)}) collective-permute-start(f32[2,1536]{1,0:T(2,128)} %get-tuple-element.12), channel_id=1, source_target_pairs={{0,32},{32,64},{64,96},{96,128},{128,160},{160,192},{192,224},{224... | collective-permute-start | bytes 36872 | tf_op jit(solution)/shard_map/ppermute | solution.py:173
  22.9 1.9 %collective-permute-start.3 = (f32[2,1536]{1,0:T(2,128)}, f32[2,1536]{1,0:T(2,128)S(1)}, u32[]{:S(2)}, u32[]{:S(2)}) collective-permute-start(f32[2,1536]{1,0:T(2,128)} %get-tuple-element.13), channel_id=1, source_target_pairs={{32,0},{64,32},{96,64},{128,96},{160,128},{192,160},{224,192},{256... | collective-permute-start | bytes 36872 | tf_op jit(solution)/shard_map/ppermute | solution.py:174
  24.8 3.3 %collective-permute-done.3.xright_ref = f32[2,1536]{1,0:T(2,128)S(1)} collective-permute-done((f32[2,1536]{1,0:T(2,128)}, f32[2,1536]{1,0:T(2,128)S(1)}, u32[]{:S(2)}, u32[]{:S(2)}) %collective-permute-start.3) | collective-permute-done | bytes 12320 | tf_op jit(solution)/shard_map/ppermute | solution.py:174
  28.8 5.0 %stencil.1 = (f32[8,12,16,128]{3,2,1,0:T(8,128)}, f32[8,12,16,128]{3,2,1,0:T(8,128)}, f32[8,12,16,128]{3,2,1,0:T(8,128)}) custom-call(f32[8,12,16,128]{3,2,1,0:T(8,128)} %bitcast.60, f32[8,12,16,128]{3,2,1,0:T(8,128)} %bitcast.61, bf16[8,12,16,128]{3,2,1,0:T(8,128)(2,1)} %bitcast.62, f32[3,12,16,128]{3,2,1,0:T(8,128)} %bitcast.63, f32[12,16,128]{2,1,0:T(8,128)} %bitcast.64, ...), custom_call_target="tpu_custom_call" | custom-call | tf_op jit(solution)/shard_map/stencil/pallas_call | solution.py:124
  33.8 4.5 %collective-permute-start.6 = (f32[1536,128]{1,0:T(8,128)}, f32[1536,128]{1,0:T(8,128)S(1)}, u32[]{:S(2)}, u32[]{:S(2)}) collective-permute-start(f32[1536,128]{1,0:T(8,128)} %bitcast.46), channel_id=1, source_target_pairs={{128,0},{160,32},{192,64},{224,96},{256,128},{288,160},{320,192},{... | collective-permute-start | bytes 2359304 | tf_op jit(solution)/shard_map/ppermute | solution.py:33
  38.3 1.9 %collective-permute-start.7 = (f32[1536,128]{1,0:T(8,128)}, f32[1536,128]{1,0:T(8,128)S(1)}, u32[]{:S(2)}, u32[]{:S(2)}) collective-permute-start(f32[1536,128]{1,0:T(8,128)} %bitcast.47), channel_id=1, source_target_pairs={{384,0},{416,32},{448,64},{480,96},{0,128},{32,160},{64,192},{96,2... | collective-permute-start | bytes 2359304 | tf_op jit(solution)/shard_map/ppermute | solution.py:33
  40.2 5.0 %collective-permute-start.4 = (f32[1536,128]{1,0:T(8,128)}, f32[1536,128]{1,0:T(8,128)S(1)}, u32[]{:S(2)}, u32[]{:S(2)}) collective-permute-start(f32[1536,128]{1,0:T(8,128)} %bitcast.48), channel_id=1, source_target_pairs={{64,0},{96,32},{0,64},{32,96},{192,128},{224,160},{128,192},{160,2... | collective-permute-start | bytes 2359304 | tf_op jit(solution)/shard_map/ppermute | solution.py:33
  45.2 1.9 %collective-permute-start.5 = (f32[1536,128]{1,0:T(8,128)}, f32[1536,128]{1,0:T(8,128)S(1)}, u32[]{:S(2)}, u32[]{:S(2)}) collective-permute-start(f32[1536,128]{1,0:T(8,128)} %bitcast.49), channel_id=1, source_target_pairs={{32,0},{0,32},{96,64},{64,96},{160,128},{128,160},{224,192},{192,2... | collective-permute-start | bytes 2359304 | tf_op jit(solution)/shard_map/ppermute | solution.py:33
  47.2 7.7 %collective-permute-done.6 = f32[1536,128]{1,0:T(8,128)S(1)} collective-permute-done((f32[1536,128]{1,0:T(8,128)}, f32[1536,128]{1,0:T(8,128)S(1)}, u32[]{:S(2)}, u32[]{:S(2)}) %collective-permute-start.6) | collective-permute-done | bytes 786464 | tf_op jit(solution)/shard_map/ppermute | solution.py:33
  54.9 5.2 %collective-permute-start.10 = (f32[768,128]{1,0:T(8,128)S(1)}, f32[768,128]{1,0:T(8,128)S(1)}, u32[]{:S(2)}, u32[]{:S(2)}) collective-permute-start(f32[768,128]{1,0:T(8,128)S(1)} %slice.25), channel_id=1, source_target_pairs={{128,0},{160,32},{192,64},{224,96},{256,128},{288,160},{320,192},{... | collective-permute-start | bytes 1179656 | tf_op jit(solution)/shard_map/ppermute | solution.py:33
  60.2 1.9 %collective-permute-start.11 = (f32[768,128]{1,0:T(8,128)S(1)}, f32[768,128]{1,0:T(8,128)S(1)}, u32[]{:S(2)}, u32[]{:S(2)}) collective-permute-start(f32[768,128]{1,0:T(8,128)S(1)} %slice.26), channel_id=1, source_target_pairs={{384,0},{416,32},{448,64},{480,96},{0,128},{32,160},{64,192},{96,2... | collective-permute-start | bytes 1179656 | tf_op jit(solution)/shard_map/ppermute | solution.py:33
  62.1 3.7 %collective-permute-start.8 = (f32[1536,128]{1,0:T(8,128)S(1)}, f32[1536,128]{1,0:T(8,128)S(1)}, u32[]{:S(2)}, u32[]{:S(2)}) collective-permute-start(f32[1536,128]{1,0:T(8,128)S(1)} %collective-permute-done.6), channel_id=1, source_target_pairs={{32,0},{0,32},{96,64},{64,96},{160,128},{128,160},{224,192},{192,2... | collective-permute-start | bytes 2359304 | tf_op jit(solution)/shard_map/ppermute | solution.py:33
  65.8 1.9 %collective-permute-start.9 = (f32[1536,128]{1,0:T(8,128)S(1)}, f32[1536,128]{1,0:T(8,128)S(1)}, u32[]{:S(2)}, u32[]{:S(2)}) collective-permute-start(f32[1536,128]{1,0:T(8,128)S(1)} %collective-permute-done.7), channel_id=1, source_target_pairs={{32,0},{0,32},{96,64},{64,96},{160,128},{128,160},{224,192},{192,2... | collective-permute-start | bytes 2359304 | tf_op jit(solution)/shard_map/ppermute | solution.py:33
  67.7 0.8 fusion.5
  68.6 0.8 fusion.4
  69.4 0.8 fusion.3
  70.2 0.8 fusion.2
  71.0 1.1 collective-permute-done.11
  72.2 4.5 %collective-permute-start.12 = (f32[1536,128]{1,0:T(8,128)S(1)}, f32[1536,128]{1,0:T(8,128)S(1)}, u32[]{:S(2)}, u32[]{:S(2)}) collective-permute-start(f32[1536,128]{1,0:T(8,128)S(1)} %pad_add_fusion), channel_id=1, source_target_pairs={{32,0},{0,32},{96,64},{64,96},{160,128},{128,160},{224,192},{192,2... | collective-permute-start | bytes 2359304 | tf_op jit(solution)/shard_map/ppermute | solution.py:33
  76.8 0.8 convolution_bitcast_fusion.1
  77.6 0.8 fusion.1
  78.4 0.8 fusion
  79.3 1.9 %collective-permute-start.13 = (f32[6,128,128]{2,1,0:T(8,128)S(1)}, f32[6,128,128]{2,1,0:T(8,128)S(1)}, u32[]{:S(2)}, u32[]{:S(2)}) collective-permute-start(f32[6,128,128]{2,1,0:T(8,128)S(1)} %get-tuple-element.18), channel_id=1, source_target_pairs={{64,0},{96,32},{0,64},{32,96},{192,128},{224,160},{128,192},{160,2... | collective-permute-start | bytes 1179656 | tf_op jit(solution)/shard_map/ppermute | solution.py:33
  81.2 0.8 convolution_bitcast_fusion
  82.1 3.4 %collective-permute-start.14 = (f32[2,128,128]{2,1,0:T(8,128)S(1)}, f32[2,128,128]{2,1,0:T(8,128)S(1)}, u32[]{:S(2)}, u32[]{:S(2)}) collective-permute-start(f32[2,128,128]{2,1,0:T(8,128)S(1)} %get-tuple-element.20), channel_id=1, source_target_pairs={{64,0},{96,32},{0,64},{32,96},{192,128},{224,160},{128,192},{160,2... | collective-permute-start | bytes 393224 | tf_op jit(solution)/shard_map/ppermute | solution.py:33
  85.4 6.4 %collective-permute-done.13 = f32[6,128,128]{2,1,0:T(8,128)S(1)} collective-permute-done((f32[6,128,128]{2,1,0:T(8,128)S(1)}, f32[6,128,128]{2,1,0:T(8,128)S(1)}, u32[]{:S(2)}, u32[]{:S(2)}) %collective-permute-start.13) | collective-permute-done | bytes 393248 | tf_op jit(solution)/shard_map/ppermute | solution.py:33
  91.8 2.8 %collective-permute-done.14 = f32[2,128,128]{2,1,0:T(8,128)S(1)} collective-permute-done((f32[2,128,128]{2,1,0:T(8,128)S(1)}, f32[2,128,128]{2,1,0:T(8,128)S(1)}, u32[]{:S(2)}, u32[]{:S(2)}) %collective-permute-start.14) | collective-permute-done | bytes 131104 | tf_op jit(solution)/shard_map/ppermute | solution.py:33
  94.7 37.7 %all_to_all.5 = f32[32,64,128]{2,1,0:T(8,128)S(1)} all-to-all(f32[32,64,128]{2,1,0:T(8,128)S(1)} %bitcast.58), channel_id=1, replica_groups={{0,1,2,3,8,9,24,25,10,11,26,27,16,17,18,19,4,5,6,7,12,13,28,29,14,15,30..., dimensions={0} | all-to-all | bytes 2097152 | tf_op jit(solution)/shard_map/all_to_all | solution.py:204
  132.5 0.6 multiply_bitcast_fusion
  (27 shorter events, 1.0 us)
Async XLA Ops:
  2.6 25.5 %collective-permute-start = (f32[8,2,16,128]{3,2,1,0:T(8,128)}, f32[8,2,16,128]{3,2,1,0:T(8,128)S(1)}, u32[]{:S(2)}, u32[]{:S(2)}) collective-permute-start(f32[8,2,16,128]{3,2,1,0:T(8,128)} %get-tuple-element.10), channel_id=1, source_target_pairs={{0,1},{1,2},{2,3},{3,4},{4,5},{5,6},{6,7},{7,8},{8,9},{9,10},{10,1... | collective-permute-start | bytes 393224 | tf_op jit(solution)/shard_map/ppermute | solution.py:175
  7.5 20.7 %collective-permute-start.1 = (f32[8,2,16,128]{3,2,1,0:T(8,128)}, f32[8,2,16,128]{3,2,1,0:T(8,128)S(1)}, u32[]{:S(2)}, u32[]{:S(2)}) collective-permute-start(f32[8,2,16,128]{3,2,1,0:T(8,128)} %get-tuple-element.11), channel_id=1, source_target_pairs={{1,0},{2,1},{3,2},{4,3},{5,4},{6,5},{7,6},{8,7},{9,8},{10,9},{11,1... | collective-permute-start | bytes 393224 | tf_op jit(solution)/shard_map/ppermute | solution.py:176
  19.7 5.1 %collective-permute-start.2 = (f32[2,1536]{1,0:T(2,128)}, f32[2,1536]{1,0:T(2,128)S(1)}, u32[]{:S(2)}, u32[]{:S(2)}) collective-permute-start(f32[2,1536]{1,0:T(2,128)} %get-tuple-element.12), channel_id=1, source_target_pairs={{0,32},{32,64},{64,96},{96,128},{128,160},{160,192},{192,224},{224... | collective-permute-start | bytes 36872 | tf_op jit(solution)/shard_map/ppermute | solution.py:173
  22.9 5.2 %collective-permute-start.3 = (f32[2,1536]{1,0:T(2,128)}, f32[2,1536]{1,0:T(2,128)S(1)}, u32[]{:S(2)}, u32[]{:S(2)}) collective-permute-start(f32[2,1536]{1,0:T(2,128)} %get-tuple-element.13), channel_id=1, source_target_pairs={{32,0},{64,32},{96,64},{128,96},{160,128},{192,160},{224,192},{256... | collective-permute-start | bytes 36872 | tf_op jit(solution)/shard_map/ppermute | solution.py:174
  24.8 3.3 %copy-start.3 = (f32[2,1536]{1,0:T(2,128)}, f32[2,1536]{1,0:T(2,128)S(1)}, u32[]{:S(2)}) copy-start(f32[2,1536]{1,0:T(2,128)S(1)} %collective-permute-done.2.xleft_ref) | copy-start | bytes 36868
  28.1 0.6 copy-start.4
  28.1 0.6 copy-start.1
  28.1 0.7 copy-start.2
  33.8 33.9 %copy-start = (f32[8,12,16,128]{3,2,1,0:T(8,128)S(1)}, f32[8,12,16,128]{3,2,1,0:T(8,128)}, u32[]{:S(2)}) copy-start(f32[8,12,16,128]{3,2,1,0:T(8,128)} %get-tuple-element.16) | copy-start | bytes 2359300
  33.8 21.1 %collective-permute-start.6 = (f32[1536,128]{1,0:T(8,128)}, f32[1536,128]{1,0:T(8,128)S(1)}, u32[]{:S(2)}, u32[]{:S(2)}) collective-permute-start(f32[1536,128]{1,0:T(8,128)} %bitcast.46), channel_id=1, source_target_pairs={{128,0},{160,32},{192,64},{224,96},{256,128},{288,160},{320,192},{... | collective-permute-start | bytes 2359304 | tf_op jit(solution)/shard_map/ppermute | solution.py:33
  38.3 21.8 %collective-permute-start.7 = (f32[1536,128]{1,0:T(8,128)}, f32[1536,128]{1,0:T(8,128)S(1)}, u32[]{:S(2)}, u32[]{:S(2)}) collective-permute-start(f32[1536,128]{1,0:T(8,128)} %bitcast.47), channel_id=1, source_target_pairs={{384,0},{416,32},{448,64},{480,96},{0,128},{32,160},{64,192},{96,2... | collective-permute-start | bytes 2359304 | tf_op jit(solution)/shard_map/ppermute | solution.py:33
  40.2 25.5 %collective-permute-start.4 = (f32[1536,128]{1,0:T(8,128)}, f32[1536,128]{1,0:T(8,128)S(1)}, u32[]{:S(2)}, u32[]{:S(2)}) collective-permute-start(f32[1536,128]{1,0:T(8,128)} %bitcast.48), channel_id=1, source_target_pairs={{64,0},{96,32},{0,64},{32,96},{192,128},{224,160},{128,192},{160,2... | collective-permute-start | bytes 2359304 | tf_op jit(solution)/shard_map/ppermute | solution.py:33
  45.2 23.3 %collective-permute-start.5 = (f32[1536,128]{1,0:T(8,128)}, f32[1536,128]{1,0:T(8,128)S(1)}, u32[]{:S(2)}, u32[]{:S(2)}) collective-permute-start(f32[1536,128]{1,0:T(8,128)} %bitcast.49), channel_id=1, source_target_pairs={{32,0},{0,32},{96,64},{64,96},{160,128},{128,160},{224,192},{192,2... | collective-permute-start | bytes 2359304 | tf_op jit(solution)/shard_map/ppermute | solution.py:33
  54.9 16.1 %collective-permute-start.10 = (f32[768,128]{1,0:T(8,128)S(1)}, f32[768,128]{1,0:T(8,128)S(1)}, u32[]{:S(2)}, u32[]{:S(2)}) collective-permute-start(f32[768,128]{1,0:T(8,128)S(1)} %slice.25), channel_id=1, source_target_pairs={{128,0},{160,32},{192,64},{224,96},{256,128},{288,160},{320,192},{... | collective-permute-start | bytes 1179656 | tf_op jit(solution)/shard_map/ppermute | solution.py:33
  60.2 12.0 %collective-permute-start.11 = (f32[768,128]{1,0:T(8,128)S(1)}, f32[768,128]{1,0:T(8,128)S(1)}, u32[]{:S(2)}, u32[]{:S(2)}) collective-permute-start(f32[768,128]{1,0:T(8,128)S(1)} %slice.26), channel_id=1, source_target_pairs={{384,0},{416,32},{448,64},{480,96},{0,128},{32,160},{64,192},{96,2... | collective-permute-start | bytes 1179656 | tf_op jit(solution)/shard_map/ppermute | solution.py:33
  62.1 15.5 %collective-permute-start.8 = (f32[1536,128]{1,0:T(8,128)S(1)}, f32[1536,128]{1,0:T(8,128)S(1)}, u32[]{:S(2)}, u32[]{:S(2)}) collective-permute-start(f32[1536,128]{1,0:T(8,128)S(1)} %collective-permute-done.6), channel_id=1, source_target_pairs={{32,0},{0,32},{96,64},{64,96},{160,128},{128,160},{224,192},{192,2... | collective-permute-start | bytes 2359304 | tf_op jit(solution)/shard_map/ppermute | solution.py:33
  65.8 12.6 %collective-permute-start.9 = (f32[1536,128]{1,0:T(8,128)S(1)}, f32[1536,128]{1,0:T(8,128)S(1)}, u32[]{:S(2)}, u32[]{:S(2)}) collective-permute-start(f32[1536,128]{1,0:T(8,128)S(1)} %collective-permute-done.7), channel_id=1, source_target_pairs={{32,0},{0,32},{96,64},{64,96},{160,128},{128,160},{224,192},{192,2... | collective-permute-start | bytes 2359304 | tf_op jit(solution)/shard_map/ppermute | solution.py:33
  72.2 9.0 %collective-permute-start.12 = (f32[1536,128]{1,0:T(8,128)S(1)}, f32[1536,128]{1,0:T(8,128)S(1)}, u32[]{:S(2)}, u32[]{:S(2)}) collective-permute-start(f32[1536,128]{1,0:T(8,128)S(1)} %pad_add_fusion), channel_id=1, source_target_pairs={{32,0},{0,32},{96,64},{64,96},{160,128},{128,160},{224,192},{192,2... | collective-permute-start | bytes 2359304 | tf_op jit(solution)/shard_map/ppermute | solution.py:33
  79.3 12.6 %collective-permute-start.13 = (f32[6,128,128]{2,1,0:T(8,128)S(1)}, f32[6,128,128]{2,1,0:T(8,128)S(1)}, u32[]{:S(2)}, u32[]{:S(2)}) collective-permute-start(f32[6,128,128]{2,1,0:T(8,128)S(1)} %get-tuple-element.18), channel_id=1, source_target_pairs={{64,0},{96,32},{0,64},{32,96},{192,128},{224,160},{128,192},{160,2... | collective-permute-start | bytes 1179656 | tf_op jit(solution)/shard_map/ppermute | solution.py:33
  82.1 12.6 %collective-permute-start.14 = (f32[2,128,128]{2,1,0:T(8,128)S(1)}, f32[2,128,128]{2,1,0:T(8,128)S(1)}, u32[]{:S(2)}, u32[]{:S(2)}) collective-permute-start(f32[2,128,128]{2,1,0:T(8,128)S(1)} %get-tuple-element.20), channel_id=1, source_target_pairs={{64,0},{96,32},{0,64},{32,96},{192,128},{224,160},{128,192},{160,2... | collective-permute-start | bytes 393224 | tf_op jit(solution)/shard_map/ppermute | solution.py:33

commit v6 on v5

--- a/solution.py
+++ b/solution.py
@@ -12,8 +12,9 @@
 
 NX_CHIPS, NY_LO, CORES = 4, 2, 2
 HIGHEST = lax.Precision.HIGHEST
-FIRST = ((0, 0), (0, 1), (1, 0), (3, 0), (1, 1), (3, 1))
-SECOND = ((2, 0), (2, 1))
+COLUMNS = (0, 1, 3, 2)
+ROWS = ((0, 0), (0, 1), (1, 0), (1, 1))
+FLIPS = (0, 2, 5, 6)
 
 
 def gx_of(x, y, core):
@@ -137,23 +138,39 @@
     )(s, r, c, vel, dif, ybelow, yabove, xleft, xright)
 
 
-ORDER = tuple(
-    (dx, dy, dcore)
-    for dy, columns in ((0, FIRST), (0, SECOND), (1, FIRST), (1, SECOND))
-    for dx, dcore in columns
-)
-
-
-def owners(n_gy):
-    groups = []
-    for x in range(NX_CHIPS):
-        for y in range(NY_LO):
-            for core in range(CORES):
-                blocks = [gx_of(x + dx, y + dy, core + dcore) for dx, dy, dcore in ORDER]
-                mine = gx_of(x, y, core)
-                each = n_gy // len(blocks)
-                groups.append([mine * n_gy + block * each + part for block in blocks for part in range(each)])
-    return groups
+def chips():
+    return [(x, y, core) for x in range(NX_CHIPS) for y in range(NY_LO) for core in range(CORES)]
+
+
+def slot(y, core):
+    return y * 2 * CORES + core * 2
+
+
+def reducers(n_gy):
+    nz = n_gy // NX_CHIPS
+    return [
+        [
+            gx_of(x, y, core) * n_gy + ((x + dx) % NX_CHIPS) * nz + ((slot(y, core) + part) ^ flip)
+            for flip in FLIPS
+            for dx in COLUMNS
+            for part in range(2)
+        ]
+        for x, y, core in chips()
+    ]
+
+
+def to_owners(n_gy):
+    nz = n_gy // NX_CHIPS
+    return [
+        (
+            gx_of(x, y, core) * n_gy + block * nz + ((slot(y, core) + part) ^ flip),
+            gx_of(x, y + dy, core + dcore) * n_gy + block * nz + slot(y, core) + part,
+        )
+        for x, y, core in chips()
+        for (dy, dcore), flip in zip(ROWS[1:], FLIPS[1:])
+        for block in range(NX_CHIPS)
+        for part in range(2)
+    ]
 
 
 def against(columns, rows):
@@ -186,24 +203,24 @@
     mine_c = fetch(mine, 0, 0, 1)
     far0 = fetch(right[:half], 1, 0, 0)
     far1 = fetch(left[half:], -1, 0, 0)
-    right_c = fetch(right, 0, 0, 1)
-    left_c = fetch(left, 0, 0, 1)
-    far = jnp.pad(far0, ((0, half), (0, 0))) + jnp.pad(far1, ((half, 0), (0, 0)))
-    far_c = fetch(far, 0, 0, 1)
-    rows = jnp.concatenate([mine, across], axis=1)
-
-    def products(*columns):
-        return jnp.stack([against(a, rows) for a in columns])
-
-    first = products(mine, mine_c, right, left, right_c, left_c)
-    second = products(far, far_c)
-    first_y = fetch(first[:, :, nx:], 0, 1, 0)
-    second_y = fetch(second[:, :, nx:], 0, 1, 0)
-    partial = jnp.concatenate([first[:, :, :nx], second[:, :, :nx], first_y, second_y], axis=0)
+    across_c = fetch(across, 0, 0, 1)
+    row_pairs = [jnp.concatenate(pair, axis=1) for pair in ((mine, mine_c), (across, across_c))]
+
+    def products(rows):
+        near = [against(a, rows) for a in (mine, right, left)]
+        return jnp.stack(near + [against(far0, rows[:half]) + against(far1, rows[half:])])
+
+    parts = [products(rows) for rows in row_pairs]
+    partial = jnp.concatenate([p[:, :, lanes] for p in parts for lanes in (slice(0, nx), slice(nx, 2 * nx))], axis=0)
     partial = partial.reshape(n_gy, -1, nx)
-    pieces = lax.all_to_all(partial, ("gx", "gy"), 0, 0, tiled=True, axis_index_groups=owners(n_gy))
+    both = ("gx", "gy")
+    pieces = lax.all_to_all(partial, both, 0, 0, tiled=True, axis_index_groups=reducers(n_gy))
+    summed = jnp.sum(pieces, axis=0)
+    moved = lax.ppermute(summed, both, to_owners(n_gy))
+    gx, z = lax.axis_index("gx"), lax.rem(lax.axis_index("gy"), n_gy // NX_CHIPS)
+    stays = lax.div(z, 2) == lax.rem(gx, NY_LO * CORES)
     columns = nv * nz * ny * n_gy
-    gram = jnp.sum(pieces, axis=0) / jnp.float32(columns)
+    gram = jnp.where(stays, summed, moved) / jnp.float32(columns)
     return to_yzx(new_state), to_yzx(new_register), gram.T
 
 
@@ -216,4 +233,6 @@
         P(None, "gy", "gx"),
     )
     out_specs = (P(None, None, "gy", "gx"), P(None, None, "gy", "gx"), P("gx", "gy"))
-    return jax.shard_map(section, mesh=mesh, in_specs=in_specs, out_specs=out_specs, check_vma=False)
+    return jax.shard_map(
+        section, mesh=mesh, in_specs=in_specs, out_specs=out_specs, check_vma=False
+    )

time: 134 us -> 123 us (0.918)
  the two profiles are of different devices: /device:TPU:1 before, /device:TPU:14 now
where the time goes in v6:
time: 123 us; the launch traced here: 122 us
  starting transfers between devices  45.1 us (37%)
  blocking collectives  37.7 us (31%)
  waiting for transfers between devices  22.8 us (19%)
  Pallas kernels  6.98 us (6%)
  matrix products  6.78 us (6%)
    all_to_all x1, blocking collectives, section(): lax.all_to_all(partial, both, 0, 0, tiled=True, axis_index_groups=reducer...  37.7 us
    ppermute x7, starting transfers between devices, fetch(): return lax.ppermute(value, 'gx', from_offset(dx, dy, dcore))  20.9 us
    ppermute x7, waiting for transfers between devices, fetch(): return lax.ppermute(value, 'gx', from_offset(dx, dy, dcore))  14.4 us
    ppermute x1, starting transfers between devices, section(): yabove = lax.ppermute(ylo, 'gy', down(n_gy))  11.4 us
    dot_general x10, matrix products, against(): lax.dot_general(columns, rows, (((0,), (0,)), ((), ())), preferred_elemen...  6.78 us
    ppermute x1, waiting for transfers between devices, section(): moved = lax.ppermute(summed, both, to_owners(n_gy))  6.78 us
    pallas_call x1, Pallas kernels, stencil(): pl.pallas_call(stencil_kernel, grid=(nv // per_step,), in_specs=[whole, w...  4.96 us
    ppermute x1, starting transfers between devices, section(): ybelow = lax.ppermute(yhi, 'gy', up(n_gy))  4.27 us
  transfers between devices with their start and end apart: 12, of which 6 were waited for; matrix products, arithmetic and copies ran while one was open for 3% of the time, Pallas kernels for 0%

profile of v6, /device:TPU:14, one launch (start us, length us, event | category | flops | bytes accessed | tf_op | source)
XLA Modules:
  0.0 122.0 jit_solution(827493124112307518)
XLA Ops:
  0.6 2.0 %pack_edges.1 = (f32[8,2,16,128]{3,2,1,0:T(8,128)}, f32[8,2,16,128]{3,2,1,0:T(8,128)}, f32[2,1536]{1,0:T(2,128)}, f32[2,1536]{1,0:T(2,128)}) custom-call(f32[8,12,16,128]{3,2,1,0:T(8,128)} %bitcast.51), custom_call_target="tpu_custom_call" | custom-call | tf_op jit(solution)/shard_map/pack_edges/pallas_call | solution.py:58
  2.6 4.3 %collective-permute-start = (f32[8,2,16,128]{3,2,1,0:T(8,128)}, f32[8,2,16,128]{3,2,1,0:T(8,128)S(1)}, u32[]{:S(2)}, u32[]{:S(2)}) collective-permute-start(f32[8,2,16,128]{3,2,1,0:T(8,128)} %get-tuple-element.10), channel_id=1, source_target_pairs={{0,1},{1,2},{2,3},{3,4},{4,5},{5,6},{6,7},{7,8},{8,9},{9,10},{10,1... | collective-permute-start | bytes 393224 | tf_op jit(solution)/shard_map/ppermute | solution.py:192
  6.9 11.4 %collective-permute-start.1 = (f32[8,2,16,128]{3,2,1,0:T(8,128)}, f32[8,2,16,128]{3,2,1,0:T(8,128)S(1)}, u32[]{:S(2)}, u32[]{:S(2)}) collective-permute-start(f32[8,2,16,128]{3,2,1,0:T(8,128)} %get-tuple-element.11), channel_id=1, source_target_pairs={{1,0},{2,1},{3,2},{4,3},{5,4},{6,5},{7,6},{8,7},{9,8},{10,9},{11,1... | collective-permute-start | bytes 393224 | tf_op jit(solution)/shard_map/ppermute | solution.py:193
  18.3 1.9 %collective-permute-start.2 = (f32[2,1536]{1,0:T(2,128)}, f32[2,1536]{1,0:T(2,128)S(1)}, u32[]{:S(2)}, u32[]{:S(2)}) collective-permute-start(f32[2,1536]{1,0:T(2,128)} %get-tuple-element.12), channel_id=1, source_target_pairs={{0,32},{32,64},{64,96},{96,128},{128,160},{160,192},{192,224},{224... | collective-permute-start | bytes 36872 | tf_op jit(solution)/shard_map/ppermute | solution.py:190
  20.2 3.6 %collective-permute-start.3 = (f32[2,1536]{1,0:T(2,128)}, f32[2,1536]{1,0:T(2,128)S(1)}, u32[]{:S(2)}, u32[]{:S(2)}) collective-permute-start(f32[2,1536]{1,0:T(2,128)} %get-tuple-element.13), channel_id=1, source_target_pairs={{32,0},{64,32},{96,64},{128,96},{160,128},{192,160},{224,192},{256... | collective-permute-start | bytes 36872 | tf_op jit(solution)/shard_map/ppermute | solution.py:191
  23.9 1.6 %collective-permute-done.3.xright_ref = f32[2,1536]{1,0:T(2,128)S(1)} collective-permute-done((f32[2,1536]{1,0:T(2,128)}, f32[2,1536]{1,0:T(2,128)S(1)}, u32[]{:S(2)}, u32[]{:S(2)}) %collective-permute-start.3) | collective-permute-done | bytes 12320 | tf_op jit(solution)/shard_map/ppermute | solution.py:191
  25.5 0.6 copy-done.4
  26.2 5.0 %stencil.1 = (f32[8,12,16,128]{3,2,1,0:T(8,128)}, f32[8,12,16,128]{3,2,1,0:T(8,128)}, f32[8,12,16,128]{3,2,1,0:T(8,128)}) custom-call(f32[8,12,16,128]{3,2,1,0:T(8,128)} %bitcast.52, f32[8,12,16,128]{3,2,1,0:T(8,128)} %bitcast.53, bf16[8,12,16,128]{3,2,1,0:T(8,128)(2,1)} %bitcast.54, f32[3,12,16,128]{3,2,1,0:T(8,128)} %bitcast.55, f32[12,16,128]{2,1,0:T(8,128)} %bitcast.56, ...), custom_call_target="tpu_custom_call" | custom-call | tf_op jit(solution)/shard_map/stencil/pallas_call | solution.py:125
  31.2 2.5 %collective-permute-start.6 = (f32[1536,128]{1,0:T(8,128)}, f32[1536,128]{1,0:T(8,128)S(1)}, u32[]{:S(2)}, u32[]{:S(2)}) collective-permute-start(f32[1536,128]{1,0:T(8,128)} %bitcast.40), channel_id=1, source_target_pairs={{384,0},{416,32},{448,64},{480,96},{0,128},{32,160},{64,192},{96,2... | collective-permute-start | bytes 2359304 | tf_op jit(solution)/shard_map/ppermute | solution.py:34
  33.7 3.5 %collective-permute-start.5 = (f32[1536,128]{1,0:T(8,128)}, f32[1536,128]{1,0:T(8,128)S(1)}, u32[]{:S(2)}, u32[]{:S(2)}) collective-permute-start(f32[1536,128]{1,0:T(8,128)} %bitcast.41), channel_id=1, source_target_pairs={{128,0},{160,32},{192,64},{224,96},{256,128},{288,160},{320,192},{... | collective-permute-start | bytes 2359304 | tf_op jit(solution)/shard_map/ppermute | solution.py:34
  37.1 4.2 %collective-permute-start.9 = (f32[1536,128]{1,0:T(8,128)}, f32[1536,128]{1,0:T(8,128)S(1)}, u32[]{:S(2)}, u32[]{:S(2)}) collective-permute-start(f32[1536,128]{1,0:T(8,128)} %bitcast.42), channel_id=1, source_target_pairs={{64,0},{96,32},{0,64},{32,96},{192,128},{224,160},{128,192},{160,2... | collective-permute-start | bytes 2359304 | tf_op jit(solution)/shard_map/ppermute | solution.py:34
  41.3 2.6 %collective-permute-start.4 = (f32[1536,128]{1,0:T(8,128)}, f32[1536,128]{1,0:T(8,128)S(1)}, u32[]{:S(2)}, u32[]{:S(2)}) collective-permute-start(f32[1536,128]{1,0:T(8,128)} %bitcast.43), channel_id=1, source_target_pairs={{32,0},{0,32},{96,64},{64,96},{160,128},{128,160},{224,192},{192,2... | collective-permute-start | bytes 2359304 | tf_op jit(solution)/shard_map/ppermute | solution.py:34
  43.9 7.4 %collective-permute-done.6 = f32[1536,128]{1,0:T(8,128)S(1)} collective-permute-done((f32[1536,128]{1,0:T(8,128)}, f32[1536,128]{1,0:T(8,128)S(1)}, u32[]{:S(2)}, u32[]{:S(2)}) %collective-permute-start.6) | collective-permute-done | bytes 786464 | tf_op jit(solution)/shard_map/ppermute | solution.py:34
  51.3 3.8 %collective-permute-start.8 = (f32[768,128]{1,0:T(8,128)S(1)}, f32[768,128]{1,0:T(8,128)S(1)}, u32[]{:S(2)}, u32[]{:S(2)}) collective-permute-start(f32[768,128]{1,0:T(8,128)S(1)} %slice.43), channel_id=1, source_target_pairs={{384,0},{416,32},{448,64},{480,96},{0,128},{32,160},{64,192},{96,2... | collective-permute-start | bytes 1179656 | tf_op jit(solution)/shard_map/ppermute | solution.py:34
  55.4 2.1 %collective-permute-start.7 = (f32[768,128]{1,0:T(8,128)S(1)}, f32[768,128]{1,0:T(8,128)S(1)}, u32[]{:S(2)}, u32[]{:S(2)}) collective-permute-start(f32[768,128]{1,0:T(8,128)S(1)} %slice.40), channel_id=1, source_target_pairs={{128,0},{160,32},{192,64},{224,96},{256,128},{288,160},{320,192},{... | collective-permute-start | bytes 1179656 | tf_op jit(solution)/shard_map/ppermute | solution.py:34
  57.5 2.0 %collective-permute-done.9 = f32[1536,128]{1,0:T(8,128)S(1)} collective-permute-done((f32[1536,128]{1,0:T(8,128)}, f32[1536,128]{1,0:T(8,128)S(1)}, u32[]{:S(2)}, u32[]{:S(2)}) %collective-permute-start.9) | collective-permute-done | bytes 786464 | tf_op jit(solution)/shard_map/ppermute | solution.py:34
  59.5 2.4 %collective-permute-start.10 = (f32[1536,128]{1,0:T(8,128)S(1)}, f32[1536,128]{1,0:T(8,128)S(1)}, u32[]{:S(2)}, u32[]{:S(2)}) collective-permute-start(f32[1536,128]{1,0:T(8,128)S(1)} %collective-permute-done.9), channel_id=1, source_target_pairs={{32,0},{0,32},{96,64},{64,96},{160,128},{128,160},{224,192},{192,2... | collective-permute-start | bytes 2359304 | tf_op jit(solution)/shard_map/ppermute | solution.py:34
  62.0 0.8 fusion.4
  62.8 0.8 fusion.5
  63.6 0.8 fusion.3
  64.5 0.5 fusion.11
  65.0 4.7 %collective-permute-done.7 = f32[768,128]{1,0:T(8,128)S(1)} collective-permute-done((f32[768,128]{1,0:T(8,128)S(1)}, f32[768,128]{1,0:T(8,128)S(1)}, u32[]{:S(2)}, u32[]{:S(2)}) %collective-permute-start.7) | collective-permute-done | bytes 393248 | tf_op jit(solution)/shard_map/ppermute | solution.py:34
  69.6 0.5 fusion.7
  70.3 0.8 convolution_bitcast_fusion.2
  71.1 0.5 fusion.13
  71.6 0.8 convolution_bitcast_fusion.1
  72.4 0.8 convolution_bitcast_fusion
  73.2 0.5 fusion.6
  73.9 37.7 %all_to_all.5 = f32[32,64,128]{2,1,0:T(8,128)S(1)} all-to-all(f32[32,64,128]{2,1,0:T(8,128)S(1)} %bitcast.50), channel_id=1, replica_groups={{0,1,8,9,24,25,16,17,2,3,10,11,26,27,18,19,5,4,13,12,29,28,21,20,6,7,14..., dimensions={0} | all-to-all | bytes 2097152 | tf_op jit(solution)/shard_map/all_to_all | solution.py:217
  111.7 2.9 %collective-permute-start.11 = (f32[64,128]{1,0:T(8,128)S(1)}, f32[64,128]{1,0:T(8,128)S(1)}, u32[]{:S(2)}, u32[]{:S(2)}) collective-permute-start(f32[64,128]{1,0:T(8,128)S(1)} %reduce_sum.9), channel_id=1, source_target_pairs={{2,32},{3,33},{10,40},{11,41},{18,48},{19,49},{26,56},{27,57},{5,6... | collective-permute-start | bytes 98312 | tf_op jit(solution)/shard_map/ppermute | solution.py:219
  114.6 6.8 %collective-permute-done.11 = f32[64,128]{1,0:T(8,128)S(1)} collective-permute-done((f32[64,128]{1,0:T(8,128)S(1)}, f32[64,128]{1,0:T(8,128)S(1)}, u32[]{:S(2)}, u32[]{:S(2)}) %collective-permute-start.11) | collective-permute-done | bytes 32800 | tf_op jit(solution)/shard_map/ppermute | solution.py:219
  121.4 0.6 multiply_bitcast_fusion
  (25 shorter events, 0.9 us)
Async XLA Ops:
  2.6 22.8 %collective-permute-start = (f32[8,2,16,128]{3,2,1,0:T(8,128)}, f32[8,2,16,128]{3,2,1,0:T(8,128)S(1)}, u32[]{:S(2)}, u32[]{:S(2)}) collective-permute-start(f32[8,2,16,128]{3,2,1,0:T(8,128)} %get-tuple-element.10), channel_id=1, source_target_pairs={{0,1},{1,2},{2,3},{3,4},{4,5},{5,6},{6,7},{7,8},{8,9},{9,10},{10,1... | collective-permute-start | bytes 393224 | tf_op jit(solution)/shard_map/ppermute | solution.py:192
  6.9 18.6 %collective-permute-start.1 = (f32[8,2,16,128]{3,2,1,0:T(8,128)}, f32[8,2,16,128]{3,2,1,0:T(8,128)S(1)}, u32[]{:S(2)}, u32[]{:S(2)}) collective-permute-start(f32[8,2,16,128]{3,2,1,0:T(8,128)} %get-tuple-element.11), channel_id=1, source_target_pairs={{1,0},{2,1},{3,2},{4,3},{5,4},{6,5},{7,6},{8,7},{9,8},{10,9},{11,1... | collective-permute-start | bytes 393224 | tf_op jit(solution)/shard_map/ppermute | solution.py:193
  18.3 5.6 %collective-permute-start.2 = (f32[2,1536]{1,0:T(2,128)}, f32[2,1536]{1,0:T(2,128)S(1)}, u32[]{:S(2)}, u32[]{:S(2)}) collective-permute-start(f32[2,1536]{1,0:T(2,128)} %get-tuple-element.12), channel_id=1, source_target_pairs={{0,32},{32,64},{64,96},{96,128},{128,160},{160,192},{192,224},{224... | collective-permute-start | bytes 36872 | tf_op jit(solution)/shard_map/ppermute | solution.py:190
  20.2 5.2 %collective-permute-start.3 = (f32[2,1536]{1,0:T(2,128)}, f32[2,1536]{1,0:T(2,128)S(1)}, u32[]{:S(2)}, u32[]{:S(2)}) collective-permute-start(f32[2,1536]{1,0:T(2,128)} %get-tuple-element.13), channel_id=1, source_target_pairs={{32,0},{64,32},{96,64},{128,96},{160,128},{192,160},{224,192},{256... | collective-permute-start | bytes 36872 | tf_op jit(solution)/shard_map/ppermute | solution.py:191
  23.9 1.6 %copy-start.3 = (f32[2,1536]{1,0:T(2,128)}, f32[2,1536]{1,0:T(2,128)S(1)}, u32[]{:S(2)}) copy-start(f32[2,1536]{1,0:T(2,128)S(1)} %collective-permute-done.2.xleft_ref) | copy-start | bytes 36868
  25.5 0.6 copy-start.4
  25.5 0.6 copy-start.1
  25.5 0.7 copy-start.2
  31.2 30.8 %copy-start = (f32[8,12,16,128]{3,2,1,0:T(8,128)S(1)}, f32[8,12,16,128]{3,2,1,0:T(8,128)}, u32[]{:S(2)}) copy-start(f32[8,12,16,128]{3,2,1,0:T(8,128)} %get-tuple-element.16) | copy-start | bytes 2359300
  31.2 20.2 %collective-permute-start.6 = (f32[1536,128]{1,0:T(8,128)}, f32[1536,128]{1,0:T(8,128)S(1)}, u32[]{:S(2)}, u32[]{:S(2)}) collective-permute-start(f32[1536,128]{1,0:T(8,128)} %bitcast.40), channel_id=1, source_target_pairs={{384,0},{416,32},{448,64},{480,96},{0,128},{32,160},{64,192},{96,2... | collective-permute-start | bytes 2359304 | tf_op jit(solution)/shard_map/ppermute | solution.py:34
  33.7 21.7 %collective-permute-start.5 = (f32[1536,128]{1,0:T(8,128)}, f32[1536,128]{1,0:T(8,128)S(1)}, u32[]{:S(2)}, u32[]{:S(2)}) collective-permute-start(f32[1536,128]{1,0:T(8,128)} %bitcast.41), channel_id=1, source_target_pairs={{128,0},{160,32},{192,64},{224,96},{256,128},{288,160},{320,192},{... | collective-permute-start | bytes 2359304 | tf_op jit(solution)/shard_map/ppermute | solution.py:34
  37.1 22.4 %collective-permute-start.9 = (f32[1536,128]{1,0:T(8,128)}, f32[1536,128]{1,0:T(8,128)S(1)}, u32[]{:S(2)}, u32[]{:S(2)}) collective-permute-start(f32[1536,128]{1,0:T(8,128)} %bitcast.42), channel_id=1, source_target_pairs={{64,0},{96,32},{0,64},{32,96},{192,128},{224,160},{128,192},{160,2... | collective-permute-start | bytes 2359304 | tf_op jit(solution)/shard_map/ppermute | solution.py:34
  41.3 20.7 %collective-permute-start.4 = (f32[1536,128]{1,0:T(8,128)}, f32[1536,128]{1,0:T(8,128)S(1)}, u32[]{:S(2)}, u32[]{:S(2)}) collective-permute-start(f32[1536,128]{1,0:T(8,128)} %bitcast.43), channel_id=1, source_target_pairs={{32,0},{0,32},{96,64},{64,96},{160,128},{128,160},{224,192},{192,2... | collective-permute-start | bytes 2359304 | tf_op jit(solution)/shard_map/ppermute | solution.py:34
  51.3 13.1 %collective-permute-start.8 = (f32[768,128]{1,0:T(8,128)S(1)}, f32[768,128]{1,0:T(8,128)S(1)}, u32[]{:S(2)}, u32[]{:S(2)}) collective-permute-start(f32[768,128]{1,0:T(8,128)S(1)} %slice.43), channel_id=1, source_target_pairs={{384,0},{416,32},{448,64},{480,96},{0,128},{32,160},{64,192},{96,2... | collective-permute-start | bytes 1179656 | tf_op jit(solution)/shard_map/ppermute | solution.py:34
  55.4 14.2 %collective-permute-start.7 = (f32[768,128]{1,0:T(8,128)S(1)}, f32[768,128]{1,0:T(8,128)S(1)}, u32[]{:S(2)}, u32[]{:S(2)}) collective-permute-start(f32[768,128]{1,0:T(8,128)S(1)} %slice.40), channel_id=1, source_target_pairs={{128,0},{160,32},{192,64},{224,96},{256,128},{288,160},{320,192},{... | collective-permute-start | bytes 1179656 | tf_op jit(solution)/shard_map/ppermute | solution.py:34
  59.5 10.7 %collective-permute-start.10 = (f32[1536,128]{1,0:T(8,128)S(1)}, f32[1536,128]{1,0:T(8,128)S(1)}, u32[]{:S(2)}, u32[]{:S(2)}) collective-permute-start(f32[1536,128]{1,0:T(8,128)S(1)} %collective-permute-done.9), channel_id=1, source_target_pairs={{32,0},{0,32},{96,64},{64,96},{160,128},{128,160},{224,192},{192,2... | collective-permute-start | bytes 2359304 | tf_op jit(solution)/shard_map/ppermute | solution.py:34
  111.7 9.7 %collective-permute-start.11 = (f32[64,128]{1,0:T(8,128)S(1)}, f32[64,128]{1,0:T(8,128)S(1)}, u32[]{:S(2)}, u32[]{:S(2)}) collective-permute-start(f32[64,128]{1,0:T(8,128)S(1)} %reduce_sum.9), channel_id=1, source_target_pairs={{2,32},{3,33},{10,40},{11,41},{18,48},{19,49},{26,56},{27,57},{5,6... | collective-permute-start | bytes 98312 | tf_op jit(solution)/shard_map/ppermute | solution.py:219
